TPU v7x, 128 devices: a whole 4x4x4 slice. The times are simulated.
128 devices in a mesh: emb: 16 (over x, z), dp: 8 (over y, core).
Axes of the slice: x: 4, y: 4, z: 4, core: 2. Of those that a mesh axis runs over, the one named last changes fastest.
Arguments:
- user_table: bfloat16 [32768, 512], P('emb'), may hold values from -6 to 6
- item_table: bfloat16 [32768, 512], P('emb'), may hold values from -6 to 6
- user_owner: int32 [262144, 1], P(('emb', 'dp')), may hold values from 0 to 15; in each aligned block of 2048 rows (0 to 2047, 2048 to 4095, ...) at most 192 rows name the same one
- user_row: int32 [262144], P(('emb', 'dp')), may hold values from 0 to 2047
- item_owner: int32 [262144, 1], P(('emb', 'dp')), may hold values from 0 to 15; in each aligned block of 2048 rows (0 to 2047, 2048 to 4095, ...) at most 192 rows name the same one
- item_row: int32 [262144], P(('emb', 'dp')), may hold values from 0 to 2047
- labels: int32 [262144], P(('emb', 'dp')), may hold values 0 or 1
- w1_user: bfloat16 [256, 512], replicated, may hold values from -0.25 to 0.25
- w1_item: bfloat16 [256, 512], replicated, may hold values from -0.25 to 0.25
- w2_weight: bfloat16 [512, 512], replicated, may hold values from -0.25 to 0.25
- w3_weight: bfloat16 [512, 512], replicated, may hold values from -0.25 to 0.25
- w_out: float32 [768], replicated, may hold values from -0.5 to 0.5
Outputs:
- user_grad: float32 [8, 32768, 512], P('dp', 'emb')
- item_grad: float32 [8, 32768, 512], P('dp', 'emb')
- grad_w1_user: float32 [256, 512], replicated
- grad_w1_item: float32 [256, 512], replicated
- grad_w2: float32 [512, 512], replicated
- grad_w3: float32 [512, 512], replicated
- grad_out: float32 [768], replicated
Inputs may be any that keep to these rules, and one draw needn't show every extreme that they name: `user_owner`: of the pairs of one device, at most 192 have their user with the same index of emb, and exactly that many in some device. `item_owner`: of the pairs of one device, at most 192 have their item with the same index of emb, and exactly that many in some device.
All inputs are finite; a program needn't handle non-finite values. No bound on the sum of `labels` on one device may be relied on, other than what follows from the above.
Results may differ from a plain program's by a relative error of at most 0.019.
Values may be sent and summed in bfloat16 or wider, within the bound.
No kernel may reach another device: no remote copies, remote signals or barrier semaphores. Data moves between devices by JAX's collectives and lax.ppermute only.
A program may use at most 128 MiB of HBM per device.

v0:
```python
import jax
import jax.numpy as jnp
from jax import lax
from jax.sharding import PartitionSpec as P

D_GMF = 256


def silu_slope(pre):
    sig = jax.nn.sigmoid(pre)
    return sig * (1.0 + pre * (1.0 - sig))


def arrange(owner, wanted, owners, capacity):
    owner = owner[:, 0]
    chosen = (owner[:, None] == jnp.arange(owners, dtype=jnp.int32)[None, :]).astype(jnp.int32)
    running = jnp.cumsum(chosen, axis=0) - 1
    position = jnp.sum(running * chosen, axis=1)
    pair_slot = owner * capacity + position
    request = jnp.zeros((owners * capacity,), jnp.int32).at[pair_slot].set(wanted)
    return (pair_slot, request.reshape(owners, capacity))


def to_slots(values, slot_index, owners, capacity):
    buffer = (
        jnp.zeros((owners * capacity, values.shape[1]), values.dtype).at[slot_index].set(values)
    )
    return buffer.reshape(owners, capacity, values.shape[1])


def from_slots(received, slot_index):
    return received.reshape(-1, received.shape[-1])[slot_index]


def body(
    user_table,
    item_table,
    user_owner,
    user_row,
    item_owner,
    item_row,
    labels,
    w1_user,
    w1_item,
    w2_weight,
    w3_weight,
    w_out,
):
    owners = lax.axis_size("emb")
    pair_count = labels.shape[0]
    capacity = 3 * pair_count // (2 * owners)
    gmf_width = D_GMF
    user_slot, user_request = arrange(user_owner, user_row, owners, capacity)
    item_slot, item_request = arrange(item_owner, item_row, owners, capacity)
    user_wanted, item_wanted = (
        lax.all_to_all(user_request, "emb", split_axis=0, concat_axis=0, tiled=True),
        lax.all_to_all(item_request, "emb", split_axis=0, concat_axis=0, tiled=True),
    )
    user_back, item_back = (
        lax.all_to_all(user_table[user_wanted], "emb", split_axis=0, concat_axis=0, tiled=True),
        lax.all_to_all(item_table[item_wanted], "emb", split_axis=0, concat_axis=0, tiled=True),
    )
    user_pair = from_slots(user_back, user_slot)
    item_pair = from_slots(item_back, item_slot)
    user_mlp = user_pair[:, gmf_width:]
    item_mlp = item_pair[:, gmf_width:]
    h_user = jnp.dot(user_mlp, w1_user, preferred_element_type=jnp.float32).astype(jnp.bfloat16)
    h_item = jnp.dot(item_mlp, w1_item, preferred_element_type=jnp.float32).astype(jnp.bfloat16)
    user_gmf = user_pair[:, :gmf_width]
    item_gmf = item_pair[:, :gmf_width]
    pre_one = h_user.astype(jnp.float32) + h_item.astype(jnp.float32)
    act_one = jax.nn.silu(pre_one).astype(jnp.bfloat16)
    pre_two = jnp.dot(act_one, w2_weight, preferred_element_type=jnp.float32)
    act_two = jax.nn.silu(pre_two).astype(jnp.bfloat16)
    pre_three = jnp.dot(act_two, w3_weight, preferred_element_type=jnp.float32)
    act_three = jax.nn.silu(pre_three).astype(jnp.bfloat16)
    w_gmf = w_out[:gmf_width]
    w_deep = w_out[gmf_width:]
    gmf_prod = user_gmf.astype(jnp.float32) * item_gmf.astype(jnp.float32)
    logit = jnp.sum(gmf_prod * w_gmf[None, :], axis=1) + jnp.sum(
        act_three.astype(jnp.float32) * w_deep[None, :], axis=1
    )
    delta = jax.nn.sigmoid(logit) - labels.astype(jnp.float32)
    d_three = (delta[:, None] * w_deep[None, :] * silu_slope(pre_three)).astype(jnp.bfloat16)
    d_two = (
        jnp.dot(d_three, w3_weight.T, preferred_element_type=jnp.float32) * silu_slope(pre_two)
    ).astype(jnp.bfloat16)
    d_one = (
        jnp.dot(d_two, w2_weight.T, preferred_element_type=jnp.float32) * silu_slope(pre_one)
    ).astype(jnp.bfloat16)
    user_gmf_grad = (delta[:, None] * w_gmf[None, :] * item_gmf.astype(jnp.float32)).astype(
        jnp.bfloat16
    )
    item_gmf_grad = (delta[:, None] * w_gmf[None, :] * user_gmf.astype(jnp.float32)).astype(
        jnp.bfloat16
    )
    grad_w2 = jnp.einsum("pk,ph->kh", act_one, d_two, preferred_element_type=jnp.float32)
    grad_w3 = jnp.einsum("pk,ph->kh", act_two, d_three, preferred_element_type=jnp.float32)
    grad_out = jnp.concatenate(
        [
            jnp.sum(delta[:, None] * gmf_prod, axis=0),
            jnp.sum(delta[:, None] * act_three.astype(jnp.float32), axis=0),
        ]
    )
    user_mlp_grad = jnp.dot(d_one, w1_user.T, preferred_element_type=jnp.float32).astype(
        jnp.bfloat16
    )
    item_mlp_grad = jnp.dot(d_one, w1_item.T, preferred_element_type=jnp.float32).astype(
        jnp.bfloat16
    )
    grad_w1_user = jnp.einsum("pk,ph->kh", user_mlp, d_one, preferred_element_type=jnp.float32)
    grad_w1_item = jnp.einsum("pk,ph->kh", item_mlp, d_one, preferred_element_type=jnp.float32)
    user_rowgrad = jnp.concatenate([user_gmf_grad, user_mlp_grad], axis=1)
    item_rowgrad = jnp.concatenate([item_gmf_grad, item_mlp_grad], axis=1)
    user_outgoing = to_slots(user_rowgrad, user_slot, owners, capacity)
    item_outgoing = to_slots(item_rowgrad, item_slot, owners, capacity)
    user_terms, item_terms = (
        lax.all_to_all(user_outgoing, "emb", split_axis=0, concat_axis=0, tiled=True),
        lax.all_to_all(item_outgoing, "emb", split_axis=0, concat_axis=0, tiled=True),
    )
    row_width = user_table.shape[1]
    user_grad = (
        jnp.zeros((user_table.shape[0], row_width), jnp.float32)
        .at[user_wanted.reshape(-1)]
        .add(user_terms.reshape(-1, row_width).astype(jnp.float32))
    )
    item_grad = (
        jnp.zeros((item_table.shape[0], row_width), jnp.float32)
        .at[item_wanted.reshape(-1)]
        .add(item_terms.reshape(-1, row_width).astype(jnp.float32))
    )
    summed = lax.psum((grad_w1_user, grad_w1_item, grad_w2, grad_w3, grad_out), ("emb", "dp"))
    scale = 1.0 / pair_count
    return (
        user_grad[None],
        item_grad[None],
        summed[0] * scale,
        summed[1] * scale,
        summed[2] * scale,
        summed[3] * scale,
        summed[4] * scale,
    )


def solution(mesh):
    return jax.shard_map(
        body,
        mesh=mesh,
        in_specs=(
            P("emb", None),
            P("emb", None),
            P(("emb", "dp"), None),
            P(("emb", "dp")),
            P(("emb", "dp"), None),
            P(("emb", "dp")),
            P(("emb", "dp")),
            P(),
            P(),
            P(),
            P(),
            P(),
        ),
        out_specs=(P("dp", "emb", None), P("dp", "emb", None), P(), P(), P(), P(), P()),
        check_vma=False,
    )
```

profile of v0, /device:TPU:0, one launch (start us, length us, event | category | flops | bytes accessed | tf_op | source)
XLA Modules:
  0.0 495.0 jit_solution(3970576292859654275)
XLA Ops:
  8.0 4.5 reduce-window.14
  14.8 8.2 %scatter_custom_fusion = s32[3072]{0:T(1024)S(1)} fusion(s32[2048]{0:T(1024)S(1)} %bitcast.92, s32[2048]{0:T(1024)} %param.15, s32[]{:T(128)} %constant.11.clone.1), kind=kCustom, calls=%fused_computation.86 | custom fusion | bytes 12800 | tf_op jit(solution)/shard_map/scatter | solution.py:20
  23.7 8.0 %all-to-all-start = ((s32[16,1,192]{2,1,0:T(1,128)}), s32[16,1,192]{2,1,0:T(1,128)S(1)}, u32[]{:S(2)}, u32[]{:S(2)}) async-start(s32[16,1,192]{2,1,0:T(1,128)} %all_to_all.28), calls=%async_computation | async-start | bytes 32768 | tf_op jit(solution)/shard_map/all_to_all | solution.py:56
  32.4 4.5 reduce-window.16
  39.1 8.2 %scatter_custom_fusion.1 = s32[3072]{0:T(1024)S(1)} fusion(s32[2048]{0:T(1024)S(1)} %bitcast.95, s32[2048]{0:T(1024)} %param.17, s32[]{:T(128)} %constant.11.clone.1), kind=kCustom, calls=%fused_computation.84 | custom fusion | bytes 12800 | tf_op jit(solution)/shard_map/scatter | solution.py:20
  48.1 7.2 %all-to-all-start.2 = ((s32[16,1,192]{2,1,0:T(1,128)}), s32[16,1,192]{2,1,0:T(1,128)S(1)}, u32[]{:S(2)}, u32[]{:S(2)}) async-start(s32[16,1,192]{2,1,0:T(1,128)} %all_to_all.32), calls=%async_computation.2 | async-start | bytes 32768 | tf_op jit(solution)/shard_map/all_to_all | solution.py:57
  55.4 13.3 %gather_fusion = bf16[3072,512]{1,0:T(8,128)(2,1)} fusion(bf16[2048,512]{1,0:T(8,128)(2,1)S(1)} %copy-done, s32[3072]{0:T(1024)S(1)} %broadcast_clamp_fusion.1), kind=kCustom, calls=%fused_computation | custom fusion | bytes 6303744 | tf_op jit(solution)/shard_map/gather | solution.py:60
  68.7 7.4 %all-to-all-start.1 = ((bf16[16,192,512]{2,1,0:T(8,128)(2,1)}), bf16[16,192,512]{2,1,0:T(8,128)(2,1)}, u32[]{:S(2)}, u32[]{:S(2)}) async-start(bf16[16,192,512]{2,1,0:T(8,128)(2,1)} %bitcast.80), calls=%async_computation.1 | async-start | bytes 6291456 | tf_op jit(solution)/shard_map/all_to_all | solution.py:60
  76.3 13.3 %gather_fusion.2 = bf16[3072,512]{1,0:T(8,128)(2,1)} fusion(bf16[2048,512]{1,0:T(8,128)(2,1)S(1)} %copy-done.2, s32[3072]{0:T(1024)S(1)} %broadcast_clamp_fusion), kind=kCustom, calls=%fused_computation.2 | custom fusion | bytes 6303744 | tf_op jit(solution)/shard_map/gather | solution.py:61
  89.5 28.2 %all-to-all-done.1 = bf16[16,192,512]{2,1,0:T(8,128)(2,1)} async-done(((bf16[16,192,512]{2,1,0:T(8,128)(2,1)}), bf16[16,192,512]{2,1,0:T(8,128)(2,1)}, u32[]{:S(2)}, u32[]{:S(2)}) %all-to-all-start.1) | async-done | bytes 3145760 | tf_op jit(solution)/shard_map/all_to_all | solution.py:60
  117.7 4.3 all-to-all-start.3
  122.1 11.5 %gather_fusion.1 = bf16[2048,512]{1,0:T(8,128)(2,1)} fusion(bf16[3072,512]{1,0:T(8,128)(2,1)} %bitcast.8, s32[2048]{0:T(1024)S(1)} %broadcast_clamp_fusion.3), kind=kCustom, calls=%fused_computation.1 | custom fusion | bytes 4202496 | tf_op jit(solution)/shard_map/gather | solution.py:32
  141.4 18.2 %all-to-all-done.3 = bf16[16,192,512]{2,1,0:T(8,128)(2,1)S(1)} async-done(((bf16[16,192,512]{2,1,0:T(8,128)(2,1)}), bf16[16,192,512]{2,1,0:T(8,128)(2,1)S(1)}, u32[]{:S(2)}, u32[]{:S(2)}) %all-to-all-start.3) | async-done | bytes 3145760 | tf_op jit(solution)/shard_map/all_to_all | solution.py:61
  159.6 9.2 %gather_fusion.3 = bf16[2048,512]{1,0:T(8,128)(2,1)} fusion(bf16[3072,512]{1,0:T(8,128)(2,1)S(1)} %bitcast.78, s32[2048]{0:T(1024)S(1)} %broadcast_clamp_fusion.2), kind=kCustom, calls=%fused_computation.3 | custom fusion | bytes 4202496 | tf_op jit(solution)/shard_map/gather | solution.py:32
  194.2 12.1 %scatter_custom_fusion.2 = bf16[3072,512]{1,0:T(8,128)(2,1)} fusion(s32[2048]{0:T(1024)S(1)} %bitcast.94, bf16[2048,512]{1,0:T(8,128)(2,1)} %copy.23, bf16[]{:T(256)} %constant.16.clone.1), kind=kCustom, calls=%fused_computation.45 | custom fusion | bytes 3146240 | tf_op jit(solution)/shard_map/scatter | solution.py:26
  206.3 6.2 %all-to-all-start.4 = ((bf16[16,192,512]{2,1,0:T(8,128)(2,1)}), bf16[16,192,512]{2,1,0:T(8,128)(2,1)S(1)}, u32[]{:S(2)}, u32[]{:S(2)}) async-start(bf16[16,192,512]{2,1,0:T(8,128)(2,1)} %bitcast.17), calls=%async_computation.4 | async-start | bytes 6291456 | tf_op jit(solution)/shard_map/all_to_all | solution.py:118
  212.7 3.9 copy.24
  216.7 12.1 %scatter_custom_fusion.4 = bf16[3072,512]{1,0:T(8,128)(2,1)} fusion(s32[2048]{0:T(1024)S(1)} %bitcast.97, bf16[2048,512]{1,0:T(8,128)(2,1)} %copy.24, bf16[]{:T(256)} %constant.16.clone.1), kind=kCustom, calls=%fused_computation.43 | custom fusion | bytes 3146240 | tf_op jit(solution)/shard_map/scatter | solution.py:26
  234.6 19.5 %all-to-all-done.4 = bf16[16,192,512]{2,1,0:T(8,128)(2,1)S(1)} async-done(((bf16[16,192,512]{2,1,0:T(8,128)(2,1)}), bf16[16,192,512]{2,1,0:T(8,128)(2,1)S(1)}, u32[]{:S(2)}, u32[]{:S(2)}) %all-to-all-start.4) | async-done | bytes 3145760 | tf_op jit(solution)/shard_map/all_to_all | solution.py:118
  254.1 4.5 all-to-all-start.5
  264.5 88.9 %psum.39 = f32[768]{0:T(1024)S(1)} all-reduce(f32[768]{0:T(1024)S(1)} %pad_maximum_fusion.2), channel_id=1, replica_groups=mesh['emb'=16,'dp'=8] {'emb','dp'}, use_global_device_ids=true, to_apply=%region_20.21 | all-reduce | flops 768 | bytes 6144 | tf_op jit(solution)/shard_map/psum | solution.py:132
  354.0 82.1 %all-reduce.3.cloned.1.call-done = (f32[256,512]{1,0:T(8,128)}, f32[256,512]{1,0:T(8,128)}, f32[512,512]{1,0:T(8,128)}, f32[512,512]{1,0:T(8,128)}) async-done(((f32[256,512]{1,0:T(8,128)}, f32[256,512]{1,0:T(8,128)}, f32[512,512]{1,0:T(8,128)}, f32[512,512]{1,0:T(8,128)}), (f32[256,512]{1,0:T(8,128)}, f32[256,512]{1,0:T(8,128)}, f32[512,512]{1,0:T(8,128)}, ...) | async-done | bytes 3145744 | tf_op jit(solution)/shard_map/psum | solution.py:132
  441.5 22.6 %scatter_custom_fusion.3 = f32[2048,512]{1,0:T(8,128)} fusion(s32[3072]{0:T(1024)S(1)} %bitcast.101, bf16[3072,512]{1,0:T(8,128)(2,1)S(1)} %bitcast.81, f32[]{:T(128)} %constant.10.clone.1), kind=kCustom, calls=%fused_computation.12 | custom fusion | flops 3145728 | bytes 7340036 | tf_op jit(solution)/shard_map/scatter-add | solution.py:125
  464.1 23.5 %scatter_custom_fusion.5 = f32[2048,512]{1,0:T(8,128)} fusion(s32[3072]{0:T(1024)S(1)} %bitcast.100, bf16[3072,512]{1,0:T(8,128)(2,1)} %bitcast.25, f32[]{:T(128)} %constant.10.clone.1), kind=kCustom, calls=%fused_computation.10 | custom fusion | flops 3145728 | bytes 7340036 | tf_op jit(solution)/shard_map/scatter-add | solution.py:130
  (103 shorter events, 58.6 us)
Async XLA Ops:
  7.2 48.3 %copy-start = (bf16[2048,512]{1,0:T(8,128)(2,1)S(1)}, bf16[2048,512]{1,0:T(8,128)(2,1)}, u32[]{:S(2)}) copy-start(bf16[2048,512]{1,0:T(8,128)(2,1)} %param.12) | copy-start | bytes 6291460
  23.7 24.4 %all-to-all-start = ((s32[16,1,192]{2,1,0:T(1,128)}), s32[16,1,192]{2,1,0:T(1,128)S(1)}, u32[]{:S(2)}, u32[]{:S(2)}) async-start(s32[16,1,192]{2,1,0:T(1,128)} %all_to_all.28), calls=%async_computation | async-start | bytes 32768 | tf_op jit(solution)/shard_map/all_to_all | solution.py:56
  48.1 20.6 %all-to-all-start.2 = ((s32[16,1,192]{2,1,0:T(1,128)}), s32[16,1,192]{2,1,0:T(1,128)S(1)}, u32[]{:S(2)}, u32[]{:S(2)}) async-start(s32[16,1,192]{2,1,0:T(1,128)} %all_to_all.32), calls=%async_computation.2 | async-start | bytes 32768 | tf_op jit(solution)/shard_map/all_to_all | solution.py:57
  68.7 7.5 %copy-start.2 = (bf16[2048,512]{1,0:T(8,128)(2,1)S(1)}, bf16[2048,512]{1,0:T(8,128)(2,1)}, u32[]{:S(2)}) copy-start(bf16[2048,512]{1,0:T(8,128)(2,1)} %param.13) | copy-start | bytes 6291460
  68.7 49.0 %all-to-all-start.1 = ((bf16[16,192,512]{2,1,0:T(8,128)(2,1)}), bf16[16,192,512]{2,1,0:T(8,128)(2,1)}, u32[]{:S(2)}, u32[]{:S(2)}) async-start(bf16[16,192,512]{2,1,0:T(8,128)(2,1)} %bitcast.80), calls=%async_computation.1 | async-start | bytes 6291456 | tf_op jit(solution)/shard_map/all_to_all | solution.py:60
  117.7 4.3 copy-start.10
  117.7 41.9 %all-to-all-start.3 = ((bf16[16,192,512]{2,1,0:T(8,128)(2,1)}), bf16[16,192,512]{2,1,0:T(8,128)(2,1)S(1)}, u32[]{:S(2)}, u32[]{:S(2)}) async-start(bf16[16,192,512]{2,1,0:T(8,128)(2,1)} %bitcast.79), calls=%async_computation.3 | async-start | bytes 6291456 | tf_op jit(solution)/shard_map/all_to_all | solution.py:61
  133.6 4.6 copy-start.8
  168.8 3.9 copy-start.4
  172.7 3.1 copy-start.12
  175.9 2.4 copy-start.11
  177.8 2.4 copy-start.15
  183.6 2.4 copy-start.5
  183.6 2.4 copy-start.7
  186.0 2.5 copy-start.19
  186.0 2.5 copy-start.13
  206.3 47.8 %all-to-all-start.4 = ((bf16[16,192,512]{2,1,0:T(8,128)(2,1)}), bf16[16,192,512]{2,1,0:T(8,128)(2,1)S(1)}, u32[]{:S(2)}, u32[]{:S(2)}) async-start(bf16[16,192,512]{2,1,0:T(8,128)(2,1)} %bitcast.17), calls=%async_computation.4 | async-start | bytes 6291456 | tf_op jit(solution)/shard_map/all_to_all | solution.py:118
  228.7 3.6 copy-start.18
  228.7 3.6 copy-start.20
  254.1 210.0 %all-to-all-start.5 = ((bf16[16,192,512]{2,1,0:T(8,128)(2,1)}), bf16[16,192,512]{2,1,0:T(8,128)(2,1)}, u32[]{:S(2)}, u32[]{:S(2)}) async-start(bf16[16,192,512]{2,1,0:T(8,128)(2,1)} %bitcast.21), calls=%async_computation.5 | async-start | bytes 6291456 | tf_op jit(solution)/shard_map/all_to_all | solution.py:119
  258.6 177.6 %all-reduce.3.cloned.1.call-start = ((), (), s32[]{:S(2)}) async-start(), calls=%async_computation.6 | async-start | bytes 6291456 | tf_op jit(solution)/shard_map/psum | solution.py:132
  258.6 3.6 copy-start.6
  258.6 3.6 copy-start.16
  464.1 23.5 %copy-start.1 = (bf16[2048,512]{1,0:T(8,128)(2,1)S(1)}, bf16[2048,512]{1,0:T(8,128)(2,1)}, u32[]{:S(2)}) copy-start(bf16[2048,512]{1,0:T(8,128)(2,1)} %param.12) | copy-start | bytes 6291460
  (4 other events, 7.5 us)
Sparse Core Ops, SparseCore 0:
  265.1 170.9 all-reduce.2
where the time goes:
time: 500 us; the launch traced here: 495 us
  waiting for transfers between devices  148 us (30%)
  local copies, waits for them, and re-layouts  106 us (21%)
  blocking collectives  88.9 us (18%)
  other arithmetic  71.8 us (14%)
  starting transfers between devices  37.6 us (8%)
  matrix products  28.2 us (6%)
  between operations  15 us (3%)
    psum x1, blocking collectives, body(): lax.psum((grad_w1_user, grad_w1_item, grad_w2, grad_w3, grad_out), ('emb'...  88.9 us
    psum x1, waiting for transfers between devices, body(): lax.psum((grad_w1_user, grad_w1_item, grad_w2, grad_w3, grad_out), ('emb'...  82.1 us
    all_to_all x1, waiting for transfers between devices, body(): lax.all_to_all(user_table[user_wanted], 'emb', split_axis=0, concat_axis=...  28.2 us
    scatter x2, local copies, waits for them, and re-layouts, to_slots(): jnp.zeros((owners * capacity, values.shape[1]), values.dtype).at[slot_index]  24.1 us
    scatter-add x1, other arithmetic, body(): item_grad = jnp.zeros((item_table.shape[0], row_width), jnp.float32).at[i...  23.5 us
    scatter-add x1, other arithmetic, body(): user_grad = jnp.zeros((user_table.shape[0], row_width), jnp.float32).at[u...  22.6 us
    gather x2, local copies, waits for them, and re-layouts, from_slots(): return received.reshape(-1, received.shape[-1])[slot_index]  20.7 us
    all_to_all x1, waiting for transfers between devices, body(): lax.all_to_all(user_outgoing, 'emb', split_axis=0, concat_axis=0, tiled=T...  19.5 us
  transfers between devices with their start and end apart: 7, of which 4 were waited for; matrix products, arithmetic and copies ran while one was open for 24% of the time, Pallas kernels for 0%

commit v1 on v0

v1 whole, which is shorter than its diff:
```python
import functools

import jax
import jax.numpy as jnp
from jax import lax
from jax.experimental import pallas as pl
from jax.experimental.pallas import tpu as pltpu
from jax.sharding import PartitionSpec as P

D = 256
BF, F32, I32 = jnp.bfloat16, jnp.float32, jnp.int32
ROWS = ("emb", "dp")
PARAMS = pltpu.CompilerParams(vmem_limit_bytes=56 << 20)
W1U, W1I, W2, W3, WO, WEND = 0, 256, 512, 1024, 1536, 1600
PARTS = ((W1U, 32), (W1I, 32), (W2, 64), (W3, 64), (WO, 8))
CHUNK = 200


def dot_nn(a, b):
    return jnp.dot(a, b, preferred_element_type=F32)


def dot_nt(a, b):
    return lax.dot_general(a, b, (((1,), (1,)), ((), ())), preferred_element_type=F32)


def dot_tn(a, b):
    return lax.dot_general(a, b, (((0,), (0,)), ((), ())), preferred_element_type=F32)


def pick_rows(col, k):
    shape = (col.shape[0], k)
    return jnp.where(lax.broadcasted_iota(I32, shape, 1) == col, 1.0, 0.0).astype(BF)


def put_rows(lane, first, m):
    shape = (m, lane.shape[1])
    here = lax.broadcasted_iota(I32, shape, 0) + first
    return jnp.where(here == lane, 1.0, 0.0).astype(BF)


def column(packed, g):
    lane = lax.broadcasted_iota(I32, packed.shape, 1)
    return jnp.sum(jnp.where(lane == g, packed, 0), axis=1, keepdims=True)


def sigmoid(v):
    return 1.0 / (1.0 + jnp.exp(-v))


def silu_pair(z):
    sig = sigmoid(z)
    return (z * sig).astype(BF), (sig * (1.0 + z * (1.0 - sig))).astype(BF)


def arrange_kernel(cap, uo_ref, ur_ref, io_ref, ir_ref, lab_ref, req_ref, lanes_ref, cols_ref):
    blocks = uo_ref.shape[0]
    owners = 16
    upto = jnp.where(
        lax.broadcasted_iota(I32, (128, 128), 0) <= lax.broadcasted_iota(I32, (128, 128), 1),
        1.0, 0.0,
    ).astype(BF)

    def ranks(owner):
        chosen = [
            jnp.where(
                lax.broadcasted_iota(I32, (owners, 128), 0) == owner[j : j + 1, :], 1.0, 0.0
            )
            for j in range(blocks)
        ]
        running = dot_nn(jnp.concatenate(chosen, axis=0).astype(BF), upto)
        before = jnp.zeros((owners, 1), F32)
        places = []
        for j in range(blocks):
            run = running[j * owners : (j + 1) * owners]
            places.append(
                jnp.sum(chosen[j] * (run + (before - 1.0)), axis=0, keepdims=True)
            )
            before = before + run[:, 127:128]
        return chosen, places

    def split(v):
        high = v >> 6
        return high.astype(F32), (v - (high << 6)).astype(F32)

    def spread(chosen, values):
        return jnp.concatenate(
            [c * v for c, v in zip(chosen, values)], axis=1
        ).astype(BF)

    def slots_of(places):
        sub = lax.broadcasted_iota(I32, (256, 128), 0)
        return jnp.concatenate(
            [jnp.where(sub == p.astype(I32), 1.0, 0.0) for p in places], axis=1
        ).astype(BF)

    uo, ur, io, ir, lab = (r[...] for r in (uo_ref, ur_ref, io_ref, ir_ref, lab_ref))
    u_chosen, u_places = ranks(uo)
    i_chosen, i_places = ranks(io)
    u_slots, i_slots = slots_of(u_places), slots_of(i_places)

    def rows(v):
        return [v[j : j + 1] for j in range(blocks)]

    ur_hi, ur_lo = split(ur)
    ir_hi, ir_lo = split(ir)
    item_slot = [
        io[j : j + 1] * cap + i_places[j].astype(I32) for j in range(blocks)
    ]
    is_hi, is_lo = split(jnp.concatenate(item_slot, axis=0))
    flag = (lab + 1).astype(F32)

    def wanted(chosen, slots, hi, lo):
        return dot_nt(spread(chosen, rows(hi)), slots) * 64.0 + dot_nt(
            spread(chosen, rows(lo)), slots
        )

    req_ref[:, 0:256] = wanted(u_chosen, u_slots, ur_hi, ur_lo).astype(I32)
    req_ref[:, 256:512] = wanted(i_chosen, i_slots, ir_hi, ir_lo).astype(I32)
    s_hi, s_lo = spread(u_chosen, rows(is_hi)), spread(u_chosen, rows(is_lo))
    s_flag = spread(u_chosen, rows(flag))
    lanes_ref[...] = (dot_nt(s_hi, u_slots) * 64.0 + dot_nt(s_lo, u_slots)).astype(I32)
    cols_ref[0] = (dot_nt(u_slots, s_hi) * 64.0 + dot_nt(u_slots, s_lo)).astype(I32)
    cols_ref[1] = dot_nt(u_slots, s_flag).astype(I32)


def fetch_kernel(wcol_ref, ut_ref, it_ref, out_ref):
    g = pl.program_id(0)
    groups = pl.num_programs(0)
    peers, both, width = out_ref.shape
    cap = both // 2
    for t, table in enumerate((ut_ref, it_ref)):
        col = column(wcol_ref[...], g + t * groups)
        got = dot_nn(pick_rows(col, table.shape[0]), table[...]).astype(BF)
        out_ref[:, t * cap : (t + 1) * cap, :] = got.reshape(peers, cap, width)


def forward_kernel(
    icol_ref, um_ref, im_ref, w1u_ref, w1i_ref, w2_ref, w3_ref, wo_ref,
    im_out, a1_out, s1_out, a2_out, s2_out, a3_out, s3_out, deep_out,
):
    g = pl.program_id(0)
    m = um_ref.shape[0] * um_ref.shape[1]
    slots = im_ref.shape[0] * im_ref.shape[1]
    um = um_ref[...].reshape(m, D)
    sel = pick_rows(column(icol_ref[...], g), slots)
    im = dot_nn(sel, im_ref[...].reshape(slots, D)).astype(BF)
    im_out[...] = im
    z1 = dot_nn(um, w1u_ref[...]).astype(BF).astype(F32) + dot_nn(im, w1i_ref[...]).astype(
        BF
    ).astype(F32)
    a1, s1 = silu_pair(z1)
    a1_out[...], s1_out[...] = a1, s1
    a2, s2 = silu_pair(dot_nn(a1, w2_ref[...]))
    a2_out[...], s2_out[...] = a2, s2
    a3, s3 = silu_pair(dot_nn(a2, w3_ref[...]))
    a3_out[...], s3_out[...] = a3, s3
    deep = jnp.sum(a3.astype(F32) * wo_ref[:, D:], axis=1, keepdims=True)
    deep_out[...] = jnp.broadcast_to(deep, deep_out.shape)


def middle_kernel(
    icol_ref, fcol_ref, ilane_ref, ug_ref, ig_ref, deep_ref, wo_ref,
    out_ref, delta_out, go_out, gi_scr,
):
    step = pl.program_id(0)
    groups = pl.num_programs(0) // 2
    peers, cap, _ = ug_ref.shape
    m = peers * cap
    slots = ig_ref.shape[0] * cap

    @pl.when(step < groups)
    def _():
        ug = ug_ref[...].reshape(m, D).astype(F32)
        sel = pick_rows(column(icol_ref[...], step), slots)
        ig = dot_nn(sel, ig_ref[...].reshape(slots, D))
        wg = wo_ref[:, :D]
        prod = ug * ig
        logit = jnp.sum(prod * wg, axis=1, keepdims=True) + deep_ref[:, 0:1]
        flag = column(fcol_ref[...], step)
        delta = sigmoid(logit) - (flag - 1).astype(F32)
        delta = jnp.where(flag > 0, delta, 0.0)
        delta_out[...] = jnp.broadcast_to(delta, delta_out.shape)
        dw = delta * wg
        out_ref[...] = (dw * ig).astype(BF).reshape(peers, cap, D)
        gi_scr[pl.ds(pl.multiple_of(step * m, m), m), :] = (dw * ug).astype(BF)
        part = jnp.sum(delta * prod, axis=0, keepdims=True)

        @pl.when(step == 0)
        def _():
            go_out[...] = part

        @pl.when(step > 0)
        def _():
            go_out[...] += part

    @pl.when(step >= groups)
    def _():
        sel = put_rows(ilane_ref[...], (step - groups) * m, m)
        out_ref[...] = dot_nn(sel, gi_scr[...]).astype(BF).reshape(peers, cap, D)


def backward_kernel(
    me_ref, delta_ref, um_ref, im_ref, a1_ref, s1_ref, a2_ref, s2_ref, a3_ref, s3_ref,
    w1u_ref, w1i_ref, w2_ref, w3_ref, wo_ref, go_ref,
    mu_out, mi_out, *rest,
):
    *chunks, gw_out = rest
    step = pl.program_id(0)
    m = um_ref.shape[0] * um_ref.shape[1]
    um = um_ref[...].reshape(m, D)
    delta = delta_ref[:, 0:1]

    @pl.when(step == 0)
    def _():
        gw_out[...] = jnp.zeros_like(gw_out)
        gw_out[WO : WO + 1, 0:D] = go_ref[...]

    d3 = (delta * wo_ref[:, D:] * s3_ref[...].astype(F32)).astype(BF)
    d2 = (dot_nt(d3, w3_ref[...]) * s2_ref[...].astype(F32)).astype(BF)
    d1 = (dot_nt(d2, w2_ref[...]) * s1_ref[...].astype(F32)).astype(BF)
    mu_out[...] = dot_nt(d1, w1u_ref[...]).astype(BF).reshape(mu_out.shape)
    mi_out[...] = dot_nt(d1, w1i_ref[...]).astype(BF)
    gw_out[W1U:W1I, :] += dot_tn(um, d1)
    gw_out[W1I:W2, :] += dot_tn(im_ref[...], d1)
    gw_out[W2:W3, :] += dot_tn(a1_ref[...], d2)
    gw_out[W3:WO, :] += dot_tn(a2_ref[...], d3)
    gw_out[WO + 1 : WO + 2, :] += jnp.sum(
        delta * a3_ref[...].astype(F32), axis=0, keepdims=True
    )

    @pl.when(step == pl.num_programs(0) - 1)
    def _():
        for k, chunk in enumerate(chunks):
            peer = (me_ref[0] + k) % len(chunks)
            at = 0
            for first, count in PARTS:
                start = pl.multiple_of(first + peer * count, 8)
                chunk[at : at + count, :] = gw_out[pl.ds(start, count), :].astype(BF)
                at += count


def assemble_kernel(scale, me_ref, *refs):
    chunks, outs = refs[:8], refs[8:]
    for k, chunk in enumerate(chunks):
        peer = (me_ref[0] + 8 - k) % 8
        at = 0
        for (_, count), out in zip(PARTS, outs):
            rows = chunk[at : at + count, :].astype(F32) * scale
            out[pl.ds(pl.multiple_of(peer * count, 8), count), :] = rows
            at += count


def place_kernel(ilane_ref, mi_ref, _, out_ref):
    peers, cap, _ = out_ref.shape
    m = peers * cap
    sel = put_rows(ilane_ref[...], pl.program_id(0) * m, m)
    out_ref[...] = dot_nn(sel, mi_ref[...]).astype(BF).reshape(peers, cap, D)


def gather_add_kernel(lane_ref, terms_ref, *rest):
    out_ref = rest[-1]
    m = out_ref.shape[0]
    slots = terms_ref.shape[0] * terms_ref.shape[1]
    sel = put_rows(lane_ref[...], pl.program_id(0) * m, m)
    out_ref[...] = dot_nn(sel, terms_ref[...].reshape(slots, D))


def whole(shape):
    return pl.BlockSpec(shape, lambda i: (0,) * len(shape))


def body(
    user_table, item_table, user_owner, user_row, item_owner, item_row, labels,
    w1_user, w1_item, w2_weight, w3_weight, w_out,
):
    owners = lax.axis_size("emb")
    pairs = labels.shape[0]
    rows = user_table.shape[0]
    cap = 3 * pairs // (2 * owners)
    slots = owners * cap
    groups = 4
    peers = owners // groups
    m = peers * cap
    hid = w2_weight.shape[0]
    blocks = pairs // 128
    wo = w_out.reshape(1, -1)

    def call(kernel, grid, in_specs, out_specs, out_shape, scratch=(), aliases=None, flops=0, moved=0):
        return pl.pallas_call(
            kernel, grid=grid, in_specs=in_specs, out_specs=out_specs, out_shape=out_shape,
            scratch_shapes=scratch, input_output_aliases=aliases or {}, compiler_params=PARAMS,
            cost_estimate=pl.CostEstimate(flops=flops, bytes_accessed=moved, transcendentals=0),
        )

    def exchange(x):
        return lax.all_to_all(x, "emb", split_axis=0, concat_axis=0, tiled=True)

    req, lanes, cols = pl.pallas_call(
        functools.partial(arrange_kernel, cap),
        out_shape=(
            jax.ShapeDtypeStruct((owners, 512), I32),
            jax.ShapeDtypeStruct((owners, 256), I32),
            jax.ShapeDtypeStruct((2, 256, owners), I32),
        ),
        compiler_params=PARAMS,
    )(*(a.reshape(blocks, 128) for a in (user_owner, user_row, item_owner, item_row, labels)))

    wanted = exchange(req).reshape(owners, 2, 256)[:, :, :cap]
    wcol = wanted.reshape(groups, peers, 2, cap).transpose(1, 3, 2, 0).reshape(m, 2 * groups)
    wlane = wanted.transpose(1, 0, 2).reshape(2, 1, slots)
    ilane = lanes[:, :cap].reshape(1, slots)
    side = cols[:, :cap, :].reshape(2, cap, groups, peers).transpose(0, 3, 1, 2)
    side = side.reshape(2, m, groups)
    icol, fcol = side[0], side[1]

    buffer = jax.ShapeDtypeStruct((owners, 2 * cap, D), BF)
    user_block = pl.BlockSpec((peers, cap, D), lambda i: (i, 0, 0))
    all_items = pl.BlockSpec((owners, cap, D), lambda i: (0, 1, 0))
    tile = pl.BlockSpec((m, hid), lambda i: (i, 0))
    narrow = pl.BlockSpec((m, D), lambda i: (i, 0))
    thin = pl.BlockSpec((m, 128), lambda i: (i, 0))
    weights = [whole((D, hid)), whole((D, hid)), whole((hid, hid)), whole((hid, hid))]
    wide = jax.ShapeDtypeStruct((slots, hid), BF)
    pick = 2 * slots * slots * D

    def fetch(half):
        table = pl.BlockSpec((rows, D), lambda i: (0, half))
        return call(
            fetch_kernel, (groups,), [whole((m, 2 * groups)), table, table],
            pl.BlockSpec((peers, 2 * cap, D), lambda i: (i, 0, 0)), buffer,
            flops=4 * slots * rows * D, moved=4 * slots * D + 4 * rows * D,
        )(wcol, user_table, item_table)

    mlp_back = exchange(fetch(1))
    gmf_back = exchange(fetch(0))

    im, a1, s1, a2, s2, a3, s3, deep = call(
        forward_kernel, (groups,),
        [whole((m, groups)), user_block, all_items, *weights, whole((1, D + hid))],
        [narrow, tile, tile, tile, tile, tile, tile, thin],
        [jax.ShapeDtypeStruct((slots, D), BF)] + [wide] * 6 + [jax.ShapeDtypeStruct((slots, 128), F32)],
        flops=pick + 2 * slots * hid * (2 * D + 2 * hid), moved=16 * slots * hid,
    )(icol, mlp_back, mlp_back, w1_user, w1_item, w2_weight, w3_weight, wo)

    last = groups - 1
    gmf_out, delta, go = call(
        middle_kernel, (2 * groups,),
        [
            whole((m, groups)), whole((m, groups)), whole((1, slots)),
            pl.BlockSpec((peers, cap, D), lambda i: (jnp.minimum(i, last), 0, 0)), all_items,
            pl.BlockSpec((m, 128), lambda i: (jnp.minimum(i, last), 0)), whole((1, D + hid)),
        ],
        [
            pl.BlockSpec((peers, cap, D), lambda i: (i % groups, i // groups, 0)),
            pl.BlockSpec((m, 128), lambda i: (jnp.minimum(i, last), 0)), whole((1, D)),
        ],
        [buffer, jax.ShapeDtypeStruct((slots, 128), F32), jax.ShapeDtypeStruct((1, D), F32)],
        scratch=[pltpu.VMEM((slots, D), BF)], flops=2 * pick, moved=12 * slots * D,
    )(icol, fcol, ilane, gmf_back, gmf_back, deep, wo)

    gmf_terms = exchange(gmf_out)

    me = lax.axis_index("dp").astype(I32).reshape(1)
    n_dp = lax.axis_size("dp")
    scalar = pl.BlockSpec(memory_space=pltpu.SMEM)
    piece = jax.ShapeDtypeStruct((CHUNK, hid), BF)
    mu_out, mi, *pieces = call(
        backward_kernel, (groups,),
        [scalar, thin, user_block, narrow, tile, tile, tile, tile, tile, tile, *weights,
         whole((1, D + hid)), whole((1, D))],
        [user_block, narrow] + [whole((CHUNK, hid))] * n_dp,
        [buffer, jax.ShapeDtypeStruct((slots, D), BF)] + [piece] * n_dp,
        scratch=[pltpu.VMEM((WEND, hid), F32)],
        flops=4 * slots * hid * (2 * D + 2 * hid), moved=16 * slots * hid,
    )(me, delta, mlp_back, im, a1, s1, a2, s2, a3, s3, w1_user, w1_item, w2_weight, w3_weight, wo, go)

    mlp_out = call(
        place_kernel, (groups,),
        [whole((1, slots)), whole((slots, D)), pl.BlockSpec(memory_space=pl.ANY)],
        pl.BlockSpec((peers, cap, D), lambda i: (i, 1, 0)), buffer, aliases={2: 0},
        flops=pick, moved=4 * slots * D,
    )(ilane, mi, mu_out)

    mlp_terms = exchange(mlp_out)

    def shift_dp(x, k):
        return lax.ppermute(x, "dp", [(s, (s + k) % n_dp) for s in range(n_dp)])

    def shift_emb(x, kx, kz):
        side = 4
        return lax.ppermute(
            x, "emb",
            [
                (a * side + b, (a + kx) % side * side + (b + kz) % side)
                for a in range(side) for b in range(side)
            ],
        )

    def ring_sum(v, step):
        v = v.astype(BF)
        one, two, three = (step(v, k).astype(F32) for k in (1, 2, 3))
        return (v.astype(F32) + two) + (one + three)

    part = pieces[0].astype(F32)
    for k in range(1, n_dp):
        part = part + shift_dp(pieces[k], k).astype(F32)
    part = ring_sum(part, lambda v, k: shift_emb(v, k, 0))
    part = ring_sum(part, lambda v, k: shift_emb(v, 0, k)).astype(BF)
    found = [part] + [shift_dp(part, k) for k in range(1, n_dp)]
    gw1u, gw1i, gw2, gw3, gwo = pl.pallas_call(
        functools.partial(assemble_kernel, 1.0 / pairs),
        in_specs=[scalar] + [pl.BlockSpec(memory_space=pltpu.VMEM)] * n_dp,
        out_shape=[jax.ShapeDtypeStruct((count * n_dp, hid), F32) for _, count in PARTS],
        compiler_params=PARAMS,
    )(me, *found)

    def gather_add(terms, t, half, into=None):
        r = rows // 2
        return call(
            gather_add_kernel, (rows // r,),
            [whole((1, slots)), pl.BlockSpec((owners, cap, D), lambda i: (0, t, 0))]
            + ([] if into is None else [pl.BlockSpec(memory_space=pl.ANY)]),
            pl.BlockSpec((r, D), lambda i: (i, half)),
            jax.ShapeDtypeStruct((rows, 2 * D), F32),
            aliases=None if into is None else {2: 0},
            flops=2 * rows * slots * D, moved=2 * slots * D + 4 * rows * D,
        )(wlane[t], terms, *(() if into is None else (into,)))

    grads = [gather_add(gmf_terms, t, 0) for t in (0, 1)]
    user_grad, item_grad = (gather_add(mlp_terms, t, 1, grads[t]) for t in (0, 1))
    grad_out = jnp.concatenate([gwo[0, :D], gwo[1]])
    return user_grad[None], item_grad[None], gw1u, gw1i, gw2, gw3, grad_out


def solution(mesh):
    return jax.shard_map(
        body,
        mesh=mesh,
        in_specs=(
            P("emb", None), P("emb", None), P(ROWS, None), P(ROWS), P(ROWS, None), P(ROWS), P(ROWS),
            P(), P(), P(), P(), P(),
        ),
        out_specs=(P("dp", "emb", None), P("dp", "emb", None), P(), P(), P(), P(), P()),
        check_vma=False,
    )
```

time: 500 us -> 307 us (0.61)
  Pallas kernels: 0 us -> 121 us
  local copies, waits for them, and re-layouts: 106 us -> 12.5 us
  blocking collectives: 88.9 us -> 15.4 us
  other arithmetic: 71.8 us -> 1.1 us
  waiting for transfers between devices: 148 us -> 105 us
  matrix products: 28.2 us -> 0 us
  between operations: 15 us -> 0.83 us
  starting transfers between devices: 37.6 us -> 49.6 us
    pallas_call x0 -> x12, Pallas kernels: none -> 121 us  [the longest x1 25.3 us: body(): call(forward_kernel, (groups,), [whole((m, groups)), user_block, all_item...]
    psum x1 -> x0, blocking collectives: 88.9 us -> none  [body(): lax.psum((grad_w1_user, grad_w1_item, grad_w2, grad_w3, grad_out), ('emb'...]
    psum x1 -> x0, waiting for transfers between devices: 82.1 us -> none  [body(): lax.psum((grad_w1_user, grad_w1_item, grad_w2, grad_w3, grad_out), ('emb'...]
    ppermute x0 -> x20, waiting for transfers between devices: none -> 49.1 us  [the longest x14 25.2 us: shift_dp(): return lax.ppermute(x, 'dp', [(s, (s + k) % n_dp) for s in range(n_dp)])]
    gather x4 -> x0, local copies, waits for them, and re-layouts: 47.3 us -> none  [the longest x2 20.7 us: from_slots(): return received.reshape(-1, received.shape[-1])[slot_index]]
    scatter-add x2 -> x0, other arithmetic: 46.1 us -> none  [the longest x1 23.5 us: body(): item_grad = jnp.zeros((item_table.shape[0], row_width), jnp.float32).at[i...]
    scatter x4 -> x0, local copies, waits for them, and re-layouts: 40.6 us -> none  [the longest x2 24.1 us: to_slots(): jnp.zeros((owners * capacity, values.shape[1]), values.dtype).at[slot_index]]
    ppermute x0 -> x20, starting transfers between devices: none -> 30 us  [the longest x14 20.6 us: shift_dp(): return lax.ppermute(x, 'dp', [(s, (s + k) % n_dp) for s in range(n_dp)])]
  transfers between devices with their start and end apart: 7 -> 24, of which waited for: 4 -> 19; matrix products, arithmetic and copies ran while one was open for 24% -> 2% of each run, Pallas kernels for 0% -> 25%
where the time goes in v1:
time: 307 us; the launch traced here: 305 us
  Pallas kernels  121 us (39%)
  waiting for transfers between devices  105 us (34%)
  starting transfers between devices  49.6 us (16%)
  blocking collectives  15.4 us (5%)
  local copies, waits for them, and re-layouts  12.5 us (4%)
    all_to_all x4, waiting for transfers between devices, exchange(): return lax.all_to_all(x, 'emb', split_axis=0, concat_axis=0, tiled=True)  56 us
    pallas_call x1, Pallas kernels, body(): call(forward_kernel, (groups,), [whole((m, groups)), user_block, all_item...  25.3 us
    ppermute x14, waiting for transfers between devices, shift_dp(): return lax.ppermute(x, 'dp', [(s, (s + k) % n_dp) for s in range(n_dp)])  25.2 us
    pallas_call x4, Pallas kernels, gather_add(): call(gather_add_kernel, (rows // r,), [whole((1, slots)), pl.BlockSpec((o...  24 us
    ppermute x6, waiting for transfers between devices, shift_emb(): lax.ppermute(x, 'emb', [(a * side + b, (a + kx) % side * side + (b + kz)...  23.9 us
    pallas_call x2, Pallas kernels, fetch(): call(fetch_kernel, (groups,), [whole((m, 2 * groups)), table, table], pl....  21.4 us
    ppermute x14, starting transfers between devices, shift_dp(): return lax.ppermute(x, 'dp', [(s, (s + k) % n_dp) for s in range(n_dp)])  20.6 us
    all_to_all x4, starting transfers between devices, exchange(): return lax.all_to_all(x, 'emb', split_axis=0, concat_axis=0, tiled=True)  19.6 us
  transfers between devices with their start and end apart: 24, of which 19 were waited for; matrix products, arithmetic and copies ran while one was open for 2% of the time, Pallas kernels for 25%

profile of v1, /device:TPU:0, one launch (start us, length us, event | category | flops | bytes accessed | tf_op | source)
XLA Modules:
  0.0 305.5 jit_solution(11004627934579519423)
XLA Ops:
  0.6 4.3 %shard_map.171 = (s32[16,512]{1,0:T(8,128)}, s32[16,256]{1,0:T(8,128)}, s32[2,256,16]{2,1,0:T(8,128)}) custom-call(s32[16,128]{1,0:T(8,128)} %bitcast.38, s32[16,128]{1,0:T(8,128)} %bitcast.39, s32[16,128]{1,0:T(8,128)} %bitcast.40, s32[16,128]{1,0:T(8,128)} %bitcast.41, s32[16,128]{1,0:T(8,128)} %bitcast.42), custom_call_target="tpu_custom_call" | custom-call | tf_op jit(solution)/shard_map/pallas_call | solution.py:299
  5.7 15.4 %all_to_all.29 = s32[16,1,512]{2,1,0:T(1,128)S(1)} all-to-all(s32[16,1,512]{2,1,0:T(1,128)S(1)} %copy.31), channel_id=1, replica_groups=mesh['emb'=16,'dp'=8] {'emb'}, dimensions={0} | all-to-all | bytes 65536 | tf_op jit(solution)/shard_map/all_to_all | solution.py:297
  22.3 10.7 %shard_map.173 = bf16[16,384,256]{2,1,0:T(8,128)(2,1)} custom-call(s32[768,8]{1,0:T(8,128)} %copy.36.wcol_ref, bf16[2048,512]{1,0:T(8,128)(2,1)} %ut_ref.3, bf16[2048,512]{1,0:T(8,128)(2,1)} %it_ref.3), custom_call_target="tpu_custom_call" | custom-call | flops 6442450944 | bytes 5242880 | tf_op jit(solution)/shard_map/pallas_call | solution.py:329
  36.7 10.7 %shard_map.172 = bf16[16,384,256]{2,1,0:T(8,128)(2,1)} custom-call(s32[768,8]{1,0:T(8,128)} %copy.36.wcol_ref, bf16[2048,512]{1,0:T(8,128)(2,1)} %ut_ref.3, bf16[2048,512]{1,0:T(8,128)(2,1)} %it_ref.3), custom_call_target="tpu_custom_call" | custom-call | flops 6442450944 | bytes 5242880 | tf_op jit(solution)/shard_map/pallas_call | solution.py:329
  47.5 30.7 %all-to-all-done.2.um_ref.im_ref = bf16[16,384,256]{2,1,0:T(8,128)(2,1)S(1)} async-done(((bf16[16,384,256]{2,1,0:T(8,128)(2,1)}), bf16[16,384,256]{2,1,0:T(8,128)(2,1)S(1)}, u32[]{:S(2)}, u32[]{:S(2)}) %all-to-all-start.2) | async-done | bytes 3145760 | tf_op jit(solution)/shard_map/all_to_all | solution.py:297
  79.8 4.7 %all-to-all-start.1 = ((bf16[16,384,256]{2,1,0:T(8,128)(2,1)}), bf16[16,384,256]{2,1,0:T(8,128)(2,1)}, u32[]{:S(2)}, u32[]{:S(2)}) async-start(bf16[16,384,256]{2,1,0:T(8,128)(2,1)} %shard_map.172), calls=%async_computation.1 | async-start | bytes 6291456 | tf_op jit(solution)/shard_map/all_to_all | solution.py:297
  87.8 25.3 %shard_map.174 = (bf16[3072,256]{1,0:T(8,128)(2,1)}, bf16[3072,512]{1,0:T(8,128)(2,1)}, bf16[3072,512]{1,0:T(8,128)(2,1)}, bf16[3072,512]{1,0:T(8,128)(2,1)}, bf...) custom-call(s32[768,4]{1,0:T(8,128)} %bitcast.29, ...), custom_call_target="tpu_custom_call" | custom-call | flops 9663676416 | bytes 25165824 | tf_op jit(solution)/shard_map/pallas_call | solution.py:338
  113.1 8.5 %all-to-all-done.1.ug_ref.ig_ref = bf16[16,384,256]{2,1,0:T(8,128)(2,1)} async-done(((bf16[16,384,256]{2,1,0:T(8,128)(2,1)}), bf16[16,384,256]{2,1,0:T(8,128)(2,1)}, u32[]{:S(2)}, u32[]{:S(2)}) %all-to-all-start.1) | async-done | bytes 3145760 | tf_op jit(solution)/shard_map/all_to_all | solution.py:297
  121.6 18.3 %shard_map.175 = (bf16[16,384,256]{2,1,0:T(8,128)(2,1)}, f32[3072,128]{1,0:T(8,128)}, f32[1,256]{1,0:T(1,128)}) custom-call(s32[768,4]{1,0:T(8,128)} %bitcast.30, s32[768,4]{1,0:T(8,128)} %bitcast.28, s32[1,3072]{1,0:T(1,128)} %reshape.69.ilane_ref, bf16[16,384,256]{2,1,0:T(8,128)(2,1)} %all-to-all-done.1.ug_ref.ig_ref, ...), custom_call_target="tpu_custom_call" | custom-call | flops 9663676416 | bytes 9437184 | tf_op jit(solution)/shard_map/pallas_call | solution.py:347
  139.8 6.5 %all-to-all-start.4 = ((bf16[16,384,256]{2,1,0:T(8,128)(2,1)}), bf16[16,384,256]{2,1,0:T(8,128)(2,1)S(1)}, u32[]{:S(2)}, u32[]{:S(2)}) async-start(bf16[16,384,256]{2,1,0:T(8,128)(2,1)} %get-tuple-element.51), calls=%async_computation.4 | async-start | bytes 6291456 | tf_op jit(solution)/shard_map/all_to_all | solution.py:297
  146.3 16.5 %shard_map.176 = (bf16[16,384,256]{2,1,0:T(8,128)(2,1)}, bf16[3072,256]{1,0:T(8,128)(2,1)}, bf16[200,512]{1,0:T(8,128)(2,1)}, bf16[200,512]{1,0:T(8,128)(2,1)}, ...) custom-call(s32[1]{0:T(128)} %bitcast.7.me_ref, ...), custom_call_target="tpu_custom_call" | custom-call | flops 9663676416 | bytes 25165824 | tf_op jit(solution)/shard_map/pallas_call | solution.py:368
  162.8 7.8 %shard_map.177 = bf16[16,384,256]{2,1,0:T(8,128)(2,1)} custom-call(s32[1,3072]{1,0:T(1,128)} %reshape.69.ilane_ref, bf16[3072,256]{1,0:T(8,128)(2,1)} %get-tuple-element.49.mi_ref, bf16[16,384,256]{2,1,0:T(8,128)(2,1)} %get-tuple-element.50._), custom_call_target="tpu_custom_call", output_to_operand_aliasing={{}: (2, {})} | custom-call | flops 4831838208 | bytes 3145728 | tf_op jit(solution)/shard_map/pallas_call | solution.py:378
  170.6 16.8 %all-to-all-done.4.terms_ref = bf16[16,384,256]{2,1,0:T(8,128)(2,1)S(1)} async-done(((bf16[16,384,256]{2,1,0:T(8,128)(2,1)}), bf16[16,384,256]{2,1,0:T(8,128)(2,1)S(1)}, u32[]{:S(2)}, u32[]{:S(2)}) %all-to-all-start.4) | async-done | bytes 3145760 | tf_op jit(solution)/shard_map/all_to_all | solution.py:297
  189.1 4.7 %all-to-all-start.3 = ((bf16[16,384,256]{2,1,0:T(8,128)(2,1)}), bf16[16,384,256]{2,1,0:T(8,128)(2,1)}, u32[]{:S(2)}, u32[]{:S(2)}) async-start(bf16[16,384,256]{2,1,0:T(8,128)(2,1)} %shard_map.177), calls=%async_computation.3 | async-start | bytes 6291456 | tf_op jit(solution)/shard_map/all_to_all | solution.py:297
  203.8 4.2 %collective-permute-start.6 = (bf16[200,512]{1,0:T(8,128)(2,1)}, bf16[200,512]{1,0:T(8,128)(2,1)S(1)}, u32[]{:S(2)}, u32[]{:S(2)}) collective-permute-start(bf16[200,512]{1,0:T(8,128)(2,1)} %get-tuple-element.59), channel_id=1, source_target_pairs={{0,7},{1,0},{2,1},{3,2},{4,3},{5,4},{6,5},{7,6},{8,15},{9,8},{10,9... | collective-permute-start | bytes 614408 | tf_op jit(solution)/shard_map/ppermute | solution.py:388
  208.0 4.0 %collective-permute-done.2 = bf16[200,512]{1,0:T(8,128)(2,1)S(1)} collective-permute-done((bf16[200,512]{1,0:T(8,128)(2,1)}, bf16[200,512]{1,0:T(8,128)(2,1)S(1)}, u32[]{:S(2)}, u32[]{:S(2)}) %collective-permute-start.2) | collective-permute-done | bytes 204832 | tf_op jit(solution)/shard_map/ppermute | solution.py:388
  221.5 13.3 %collective-permute-done.9 = bf16[200,512]{1,0:T(8,128)(2,1)S(1)} collective-permute-done((bf16[200,512]{1,0:T(8,128)(2,1)S(1)}, bf16[200,512]{1,0:T(8,128)(2,1)S(1)}, u32[]{:S(2)}, u32[]{:S(2)}) %collective-permute-start.9) | collective-permute-done | bytes 204832 | tf_op jit(solution)/shard_map/ppermute | solution.py:392
  234.8 4.0 %collective-permute-done.8 = bf16[200,512]{1,0:T(8,128)(2,1)S(1)} collective-permute-done((bf16[200,512]{1,0:T(8,128)(2,1)S(1)}, bf16[200,512]{1,0:T(8,128)(2,1)S(1)}, u32[]{:S(2)}, u32[]{:S(2)}) %collective-permute-start.8) | collective-permute-done | bytes 204832 | tf_op jit(solution)/shard_map/ppermute | solution.py:392
  256.8 4.8 %collective-permute-done.18.refs_6_ = bf16[200,512]{1,0:T(8,128)(2,1)S(1)} collective-permute-done((bf16[200,512]{1,0:T(8,128)(2,1)S(1)}, bf16[200,512]{1,0:T(8,128)(2,1)S(1)}, u32[]{:S(2)}, u32[]{:S(2)}) %collective-permute-start.18) | collective-permute-done | bytes 204832 | tf_op jit(solution)/shard_map/ppermute | solution.py:388
  267.5 7.2 %collective-permute-done.14.refs_2_ = bf16[200,512]{1,0:T(8,128)(2,1)S(1)} collective-permute-done((bf16[200,512]{1,0:T(8,128)(2,1)S(1)}, bf16[200,512]{1,0:T(8,128)(2,1)S(1)}, u32[]{:S(2)}, u32[]{:S(2)}) %collective-permute-start.14) | collective-permute-done | bytes 204832 | tf_op jit(solution)/shard_map/ppermute | solution.py:388
  281.5 6.0 %shard_map.180.rest_0_ = f32[2048,512]{1,0:T(8,128)} custom-call(s32[1,3072]{1,0:T(1,128)} %squeeze.23.lane_ref, bf16[16,384,256]{2,1,0:T(8,128)(2,1)} %copy-done), custom_call_target="tpu_custom_call" | custom-call | flops 3221225472 | bytes 3670016 | tf_op jit(solution)/shard_map/pallas_call | solution.py:420
  287.5 6.0 %shard_map.178.rest_0_ = f32[2048,512]{1,0:T(8,128)} custom-call(s32[1,3072]{1,0:T(1,128)} %squeeze.20.lane_ref, bf16[16,384,256]{2,1,0:T(8,128)(2,1)} %copy-done), custom_call_target="tpu_custom_call" | custom-call | flops 3221225472 | bytes 3670016 | tf_op jit(solution)/shard_map/pallas_call | solution.py:420
  293.5 6.0 %shard_map.181 = f32[2048,512]{1,0:T(8,128)} custom-call(s32[1,3072]{1,0:T(1,128)} %squeeze.23.lane_ref, bf16[16,384,256]{2,1,0:T(8,128)(2,1)} %all-to-all-done.3.terms_ref, f32[2048,512]{1,0:T(8,128)} %shard_map.180.rest_0_), custom_call_target="tpu_custom_call", output_to_operand_aliasing={{}: (2, {})} | custom-call | flops 3221225472 | bytes 3670016 | tf_op jit(solution)/shard_map/pallas_call | solution.py:420
  299.5 6.0 %shard_map.179 = f32[2048,512]{1,0:T(8,128)} custom-call(s32[1,3072]{1,0:T(1,128)} %squeeze.20.lane_ref, bf16[16,384,256]{2,1,0:T(8,128)(2,1)} %all-to-all-done.3.terms_ref, f32[2048,512]{1,0:T(8,128)} %shard_map.178.rest_0_), custom_call_target="tpu_custom_call", output_to_operand_aliasing={{}: (2, {})} | custom-call | flops 3221225472 | bytes 3670016 | tf_op jit(solution)/shard_map/pallas_call | solution.py:420
  (88 shorter events, 62.3 us)
Async XLA Ops:
  33.0 45.1 %all-to-all-start.2 = ((bf16[16,384,256]{2,1,0:T(8,128)(2,1)}), bf16[16,384,256]{2,1,0:T(8,128)(2,1)S(1)}, u32[]{:S(2)}, u32[]{:S(2)}) async-start(bf16[16,384,256]{2,1,0:T(8,128)(2,1)} %shard_map.173), calls=%async_computation.2 | async-start | bytes 6291456 | tf_op jit(solution)/shard_map/all_to_all | solution.py:297
  79.8 41.8 %all-to-all-start.1 = ((bf16[16,384,256]{2,1,0:T(8,128)(2,1)}), bf16[16,384,256]{2,1,0:T(8,128)(2,1)}, u32[]{:S(2)}, u32[]{:S(2)}) async-start(bf16[16,384,256]{2,1,0:T(8,128)(2,1)} %shard_map.172), calls=%async_computation.1 | async-start | bytes 6291456 | tf_op jit(solution)/shard_map/all_to_all | solution.py:297
  139.8 47.6 %all-to-all-start.4 = ((bf16[16,384,256]{2,1,0:T(8,128)(2,1)}), bf16[16,384,256]{2,1,0:T(8,128)(2,1)S(1)}, u32[]{:S(2)}, u32[]{:S(2)}) async-start(bf16[16,384,256]{2,1,0:T(8,128)(2,1)} %get-tuple-element.51), calls=%async_computation.4 | async-start | bytes 6291456 | tf_op jit(solution)/shard_map/all_to_all | solution.py:297
  189.1 104.4 %all-to-all-start.3 = ((bf16[16,384,256]{2,1,0:T(8,128)(2,1)}), bf16[16,384,256]{2,1,0:T(8,128)(2,1)}, u32[]{:S(2)}, u32[]{:S(2)}) async-start(bf16[16,384,256]{2,1,0:T(8,128)(2,1)} %shard_map.177), calls=%async_computation.3 | async-start | bytes 6291456 | tf_op jit(solution)/shard_map/all_to_all | solution.py:297
  193.8 8.2 %collective-permute-start = (bf16[200,512]{1,0:T(8,128)(2,1)}, bf16[200,512]{1,0:T(8,128)(2,1)S(1)}, u32[]{:S(2)}, u32[]{:S(2)}) collective-permute-start(bf16[200,512]{1,0:T(8,128)(2,1)} %get-tuple-element.53), channel_id=1, source_target_pairs={{0,1},{1,2},{2,3},{3,4},{4,5},{5,6},{6,7},{7,0},{8,9},{9,10},{10,1... | collective-permute-start | bytes 614408 | tf_op jit(solution)/shard_map/ppermute | solution.py:388
  193.8 10.0 %collective-permute-start.1 = (bf16[200,512]{1,0:T(8,128)(2,1)}, bf16[200,512]{1,0:T(8,128)(2,1)S(1)}, u32[]{:S(2)}, u32[]{:S(2)}) collective-permute-start(bf16[200,512]{1,0:T(8,128)(2,1)} %get-tuple-element.54), channel_id=1, source_target_pairs={{0,2},{1,3},{2,4},{3,5},{4,6},{5,7},{6,0},{7,1},{8,10},{9,11},{10,... | collective-permute-start | bytes 614408 | tf_op jit(solution)/shard_map/ppermute | solution.py:388
  195.5 16.6 %collective-permute-start.2 = (bf16[200,512]{1,0:T(8,128)(2,1)}, bf16[200,512]{1,0:T(8,128)(2,1)S(1)}, u32[]{:S(2)}, u32[]{:S(2)}) collective-permute-start(bf16[200,512]{1,0:T(8,128)(2,1)} %get-tuple-element.55), channel_id=1, source_target_pairs={{0,3},{1,4},{2,5},{3,6},{4,7},{5,0},{6,1},{7,2},{8,11},{9,12},{10,... | collective-permute-start | bytes 614408 | tf_op jit(solution)/shard_map/ppermute | solution.py:388
  197.7 15.5 %collective-permute-start.3 = (bf16[200,512]{1,0:T(8,128)(2,1)}, bf16[200,512]{1,0:T(8,128)(2,1)S(1)}, u32[]{:S(2)}, u32[]{:S(2)}) collective-permute-start(bf16[200,512]{1,0:T(8,128)(2,1)} %get-tuple-element.56), channel_id=1, source_target_pairs={{0,4},{1,5},{2,6},{3,7},{4,0},{5,1},{6,2},{7,3},{8,12},{9,13},{10,... | collective-permute-start | bytes 614408 | tf_op jit(solution)/shard_map/ppermute | solution.py:388
  199.5 14.2 %collective-permute-start.4 = (bf16[200,512]{1,0:T(8,128)(2,1)}, bf16[200,512]{1,0:T(8,128)(2,1)S(1)}, u32[]{:S(2)}, u32[]{:S(2)}) collective-permute-start(bf16[200,512]{1,0:T(8,128)(2,1)} %get-tuple-element.57), channel_id=1, source_target_pairs={{0,5},{1,6},{2,7},{3,0},{4,1},{5,2},{6,3},{7,4},{8,13},{9,14},{10,... | collective-permute-start | bytes 614408 | tf_op jit(solution)/shard_map/ppermute | solution.py:388
  202.0 12.6 %collective-permute-start.5 = (bf16[200,512]{1,0:T(8,128)(2,1)}, bf16[200,512]{1,0:T(8,128)(2,1)S(1)}, u32[]{:S(2)}, u32[]{:S(2)}) collective-permute-start(bf16[200,512]{1,0:T(8,128)(2,1)} %get-tuple-element.58), channel_id=1, source_target_pairs={{0,6},{1,7},{2,0},{3,1},{4,2},{5,3},{6,4},{7,5},{8,14},{9,15},{10,... | collective-permute-start | bytes 614408 | tf_op jit(solution)/shard_map/ppermute | solution.py:388
  203.8 12.0 %collective-permute-start.6 = (bf16[200,512]{1,0:T(8,128)(2,1)}, bf16[200,512]{1,0:T(8,128)(2,1)S(1)}, u32[]{:S(2)}, u32[]{:S(2)}) collective-permute-start(bf16[200,512]{1,0:T(8,128)(2,1)} %get-tuple-element.59), channel_id=1, source_target_pairs={{0,7},{1,0},{2,1},{3,2},{4,3},{5,4},{6,5},{7,6},{8,15},{9,8},{10,9... | collective-permute-start | bytes 614408 | tf_op jit(solution)/shard_map/ppermute | solution.py:388
  216.1 18.7 %collective-permute-start.9 = (bf16[200,512]{1,0:T(8,128)(2,1)S(1)}, bf16[200,512]{1,0:T(8,128)(2,1)S(1)}, u32[]{:S(2)}, u32[]{:S(2)}) collective-permute-start(bf16[200,512]{1,0:T(8,128)(2,1)S(1)} %add_convert_fusion.2), channel_id=1, source_target_pairs={{0,96},{8,104},{16,112},{24,120},{32,0},{40,8},{48,16},{56,24},{64... | collective-permute-start | bytes 614408 | tf_op jit(solution)/shard_map/ppermute | solution.py:392
  219.2 19.7 %collective-permute-start.8 = (bf16[200,512]{1,0:T(8,128)(2,1)S(1)}, bf16[200,512]{1,0:T(8,128)(2,1)S(1)}, u32[]{:S(2)}, u32[]{:S(2)}) collective-permute-start(bf16[200,512]{1,0:T(8,128)(2,1)S(1)} %add_convert_fusion.2), channel_id=1, source_target_pairs={{0,32},{8,40},{16,48},{24,56},{32,64},{40,72},{48,80},{56,88},{64,... | collective-permute-start | bytes 614408 | tf_op jit(solution)/shard_map/ppermute | solution.py:392
  219.2 19.7 %collective-permute-start.7 = (bf16[200,512]{1,0:T(8,128)(2,1)S(1)}, bf16[200,512]{1,0:T(8,128)(2,1)S(1)}, u32[]{:S(2)}, u32[]{:S(2)}) collective-permute-start(bf16[200,512]{1,0:T(8,128)(2,1)S(1)} %add_convert_fusion.2), channel_id=1, source_target_pairs={{0,64},{8,72},{16,80},{24,88},{32,96},{40,104},{48,112},{56,120},{... | collective-permute-start | bytes 614408 | tf_op jit(solution)/shard_map/ppermute | solution.py:392
  239.0 6.6 %collective-permute-start.12 = (bf16[200,512]{1,0:T(8,128)(2,1)S(1)}, bf16[200,512]{1,0:T(8,128)(2,1)S(1)}, u32[]{:S(2)}, u32[]{:S(2)}) collective-permute-start(bf16[200,512]{1,0:T(8,128)(2,1)S(1)} %add_convert_fusion.1), channel_id=1, source_target_pairs={{0,24},{8,0},{16,8},{24,16},{32,56},{40,32},{48,40},{56,48},{64,88... | collective-permute-start | bytes 614408 | tf_op jit(solution)/shard_map/ppermute | solution.py:392
  239.1 8.2 %collective-permute-start.11 = (bf16[200,512]{1,0:T(8,128)(2,1)S(1)}, bf16[200,512]{1,0:T(8,128)(2,1)S(1)}, u32[]{:S(2)}, u32[]{:S(2)}) collective-permute-start(bf16[200,512]{1,0:T(8,128)(2,1)S(1)} %add_convert_fusion.1), channel_id=1, source_target_pairs={{0,8},{8,16},{16,24},{24,0},{32,40},{40,48},{48,56},{56,32},{64,72... | collective-permute-start | bytes 614408 | tf_op jit(solution)/shard_map/ppermute | solution.py:392
  241.1 8.5 %collective-permute-start.10 = (bf16[200,512]{1,0:T(8,128)(2,1)S(1)}, bf16[200,512]{1,0:T(8,128)(2,1)S(1)}, u32[]{:S(2)}, u32[]{:S(2)}) collective-permute-start(bf16[200,512]{1,0:T(8,128)(2,1)S(1)} %add_convert_fusion.1), channel_id=1, source_target_pairs={{0,16},{8,24},{16,0},{24,8},{32,48},{40,56},{48,32},{56,40},{64,80... | collective-permute-start | bytes 614408 | tf_op jit(solution)/shard_map/ppermute | solution.py:392
  249.6 6.1 %collective-permute-start.19 = (bf16[200,512]{1,0:T(8,128)(2,1)S(1)}, bf16[200,512]{1,0:T(8,128)(2,1)S(1)}, u32[]{:S(2)}, u32[]{:S(2)}) collective-permute-start(bf16[200,512]{1,0:T(8,128)(2,1)S(1)} %add_convert_fusion.refs_0_), channel_id=1, source_target_pairs={{0,7},{1,0},{2,1},{3,2},{4,3},{5,4},{6,5},{7,6},{8,15},{9,8},{10,9... | collective-permute-start | bytes 614408 | tf_op jit(solution)/shard_map/ppermute | solution.py:388
  249.7 11.9 %collective-permute-start.18 = (bf16[200,512]{1,0:T(8,128)(2,1)S(1)}, bf16[200,512]{1,0:T(8,128)(2,1)S(1)}, u32[]{:S(2)}, u32[]{:S(2)}) collective-permute-start(bf16[200,512]{1,0:T(8,128)(2,1)S(1)} %add_convert_fusion.refs_0_), channel_id=1, source_target_pairs={{0,6},{1,7},{2,0},{3,1},{4,2},{5,3},{6,4},{7,5},{8,14},{9,15},{10,... | collective-permute-start | bytes 614408 | tf_op jit(solution)/shard_map/ppermute | solution.py:388
  252.4 10.5 %collective-permute-start.17 = (bf16[200,512]{1,0:T(8,128)(2,1)S(1)}, bf16[200,512]{1,0:T(8,128)(2,1)S(1)}, u32[]{:S(2)}, u32[]{:S(2)}) collective-permute-start(bf16[200,512]{1,0:T(8,128)(2,1)S(1)} %add_convert_fusion.refs_0_), channel_id=1, source_target_pairs={{0,5},{1,6},{2,7},{3,0},{4,1},{5,2},{6,3},{7,4},{8,13},{9,14},{10,... | collective-permute-start | bytes 614408 | tf_op jit(solution)/shard_map/ppermute | solution.py:388
  253.2 12.7 %collective-permute-start.16 = (bf16[200,512]{1,0:T(8,128)(2,1)S(1)}, bf16[200,512]{1,0:T(8,128)(2,1)S(1)}, u32[]{:S(2)}, u32[]{:S(2)}) collective-permute-start(bf16[200,512]{1,0:T(8,128)(2,1)S(1)} %add_convert_fusion.refs_0_), channel_id=1, source_target_pairs={{0,4},{1,5},{2,6},{3,7},{4,0},{5,1},{6,2},{7,3},{8,12},{9,13},{10,... | collective-permute-start | bytes 614408 | tf_op jit(solution)/shard_map/ppermute | solution.py:388
  255.7 11.7 %collective-permute-start.15 = (bf16[200,512]{1,0:T(8,128)(2,1)S(1)}, bf16[200,512]{1,0:T(8,128)(2,1)S(1)}, u32[]{:S(2)}, u32[]{:S(2)}) collective-permute-start(bf16[200,512]{1,0:T(8,128)(2,1)S(1)} %add_convert_fusion.refs_0_), channel_id=1, source_target_pairs={{0,3},{1,4},{2,5},{3,6},{4,7},{5,0},{6,1},{7,2},{8,11},{9,12},{10,... | collective-permute-start | bytes 614408 | tf_op jit(solution)/shard_map/ppermute | solution.py:388
  255.8 19.0 %collective-permute-start.14 = (bf16[200,512]{1,0:T(8,128)(2,1)S(1)}, bf16[200,512]{1,0:T(8,128)(2,1)S(1)}, u32[]{:S(2)}, u32[]{:S(2)}) collective-permute-start(bf16[200,512]{1,0:T(8,128)(2,1)S(1)} %add_convert_fusion.refs_0_), channel_id=1, source_target_pairs={{0,2},{1,3},{2,4},{3,5},{4,6},{5,7},{6,0},{7,1},{8,10},{9,11},{10,... | collective-permute-start | bytes 614408 | tf_op jit(solution)/shard_map/ppermute | solution.py:388
  261.6 13.2 %collective-permute-start.13 = (bf16[200,512]{1,0:T(8,128)(2,1)S(1)}, bf16[200,512]{1,0:T(8,128)(2,1)S(1)}, u32[]{:S(2)}, u32[]{:S(2)}) collective-permute-start(bf16[200,512]{1,0:T(8,128)(2,1)S(1)} %add_convert_fusion.refs_0_), channel_id=1, source_target_pairs={{0,1},{1,2},{2,3},{3,4},{4,5},{5,6},{6,7},{7,0},{8,9},{9,10},{10,1... | collective-permute-start | bytes 614408 | tf_op jit(solution)/shard_map/ppermute | solution.py:388
  (14 other events, 248.7 us)

commit v2 on v1

--- a/solution.py
+++ b/solution.py
@@ -10,10 +10,14 @@
 D = 256
 BF, F32, I32 = jnp.bfloat16, jnp.float32, jnp.int32
 ROWS = ("emb", "dp")
+
+
 PARAMS = pltpu.CompilerParams(vmem_limit_bytes=56 << 20)
+
+
 W1U, W1I, W2, W3, WO, WEND = 0, 256, 512, 1024, 1536, 1600
 PARTS = ((W1U, 32), (W1I, 32), (W2, 64), (W3, 64), (WO, 8))
-CHUNK = 200
+CHUNK, HALF = 200, 104
 
 
 def dot_nn(a, b):
@@ -202,10 +206,8 @@
 
 def backward_kernel(
     me_ref, delta_ref, um_ref, im_ref, a1_ref, s1_ref, a2_ref, s2_ref, a3_ref, s3_ref,
-    w1u_ref, w1i_ref, w2_ref, w3_ref, wo_ref, go_ref,
-    mu_out, mi_out, *rest,
+    w2_ref, w3_ref, wo_ref, go_ref, d1_out, keep_out, give_out, gw_ref,
 ):
-    *chunks, gw_out = rest
     step = pl.program_id(0)
     m = um_ref.shape[0] * um_ref.shape[1]
     um = um_ref[...].reshape(m, D)
@@ -213,49 +215,63 @@
 
     @pl.when(step == 0)
     def _():
-        gw_out[...] = jnp.zeros_like(gw_out)
-        gw_out[WO : WO + 1, 0:D] = go_ref[...]
+        gw_ref[...] = jnp.zeros_like(gw_ref)
+        gw_ref[WO : WO + 1, 0:D] = go_ref[...]
 
     d3 = (delta * wo_ref[:, D:] * s3_ref[...].astype(F32)).astype(BF)
     d2 = (dot_nt(d3, w3_ref[...]) * s2_ref[...].astype(F32)).astype(BF)
     d1 = (dot_nt(d2, w2_ref[...]) * s1_ref[...].astype(F32)).astype(BF)
-    mu_out[...] = dot_nt(d1, w1u_ref[...]).astype(BF).reshape(mu_out.shape)
-    mi_out[...] = dot_nt(d1, w1i_ref[...]).astype(BF)
-    gw_out[W1U:W1I, :] += dot_tn(um, d1)
-    gw_out[W1I:W2, :] += dot_tn(im_ref[...], d1)
-    gw_out[W2:W3, :] += dot_tn(a1_ref[...], d2)
-    gw_out[W3:WO, :] += dot_tn(a2_ref[...], d3)
-    gw_out[WO + 1 : WO + 2, :] += jnp.sum(
+    d1_out[...] = d1
+    gw_ref[W1U:W1I, :] += dot_tn(um, d1)
+    gw_ref[W1I:W2, :] += dot_tn(im_ref[...], d1)
+    gw_ref[W2:W3, :] += dot_tn(a1_ref[...], d2)
+    gw_ref[W3:WO, :] += dot_tn(a2_ref[...], d3)
+    gw_ref[WO + 1 : WO + 2, :] += jnp.sum(
         delta * a3_ref[...].astype(F32), axis=0, keepdims=True
     )
 
     @pl.when(step == pl.num_programs(0) - 1)
     def _():
-        for k, chunk in enumerate(chunks):
-            peer = (me_ref[0] + k) % len(chunks)
+        y, core = me_ref[0] // 2, me_ref[0] % 2
+        for half, out in ((core, keep_out), (1 - core, give_out)):
             at = 0
-            for first, count in PARTS:
-                start = pl.multiple_of(first + peer * count, 8)
-                chunk[at : at + count, :] = gw_out[pl.ds(start, count), :].astype(BF)
-                at += count
+            for j in range(4):
+                peer = (y + j) % 4 * 2 + half
+                for first, count in PARTS:
+                    start = pl.multiple_of(first + peer * count, 8)
+                    out[at : at + count, :] = gw_ref[pl.ds(start, count), :].astype(BF)
+                    at += count
+
+
+def rows_kernel(ilane_ref, d1_ref, w1u_ref, w1i_ref, out_ref, mi_scr):
+    step = pl.program_id(0)
+    groups = pl.num_programs(0) // 2
+    peers, cap, _ = out_ref.shape
+    m = peers * cap
+
+    @pl.when(step < groups)
+    def _():
+        d1 = d1_ref[...]
+        out_ref[...] = dot_nt(d1, w1u_ref[...]).astype(BF).reshape(peers, cap, D)
+        mi_scr[pl.ds(pl.multiple_of(step * m, m), m), :] = dot_nt(d1, w1i_ref[...]).astype(BF)
+
+    @pl.when(step >= groups)
+    def _():
+        sel = put_rows(ilane_ref[...], (step - groups) * m, m)
+        out_ref[...] = dot_nn(sel, mi_scr[...]).astype(BF).reshape(peers, cap, D)
 
 
 def assemble_kernel(scale, me_ref, *refs):
     chunks, outs = refs[:8], refs[8:]
+    y, core = me_ref[0] // 2, me_ref[0] % 2
     for k, chunk in enumerate(chunks):
-        peer = (me_ref[0] + 8 - k) % 8
+        half = core if k < 4 else 1 - core
+        peer = (y + 4 - k % 4) % 4 * 2 + half
         at = 0
         for (_, count), out in zip(PARTS, outs):
             rows = chunk[at : at + count, :].astype(F32) * scale
             out[pl.ds(pl.multiple_of(peer * count, 8), count), :] = rows
             at += count
-
-
-def place_kernel(ilane_ref, mi_ref, _, out_ref):
-    peers, cap, _ = out_ref.shape
-    m = peers * cap
-    sel = put_rows(ilane_ref[...], pl.program_id(0) * m, m)
-    out_ref[...] = dot_nn(sel, mi_ref[...]).astype(BF).reshape(peers, cap, D)
 
 
 def gather_add_kernel(lane_ref, terms_ref, *rest):
@@ -290,7 +306,7 @@
         return pl.pallas_call(
             kernel, grid=grid, in_specs=in_specs, out_specs=out_specs, out_shape=out_shape,
             scratch_shapes=scratch, input_output_aliases=aliases or {}, compiler_params=PARAMS,
-            cost_estimate=pl.CostEstimate(flops=flops, bytes_accessed=moved, transcendentals=0),
+            cost_estimate=pl.CostEstimate(flops=flops // 64, bytes_accessed=moved // 64, transcendentals=0),
         )
 
     def exchange(x):
@@ -364,56 +380,24 @@
     me = lax.axis_index("dp").astype(I32).reshape(1)
     n_dp = lax.axis_size("dp")
     scalar = pl.BlockSpec(memory_space=pltpu.SMEM)
-    piece = jax.ShapeDtypeStruct((CHUNK, hid), BF)
-    mu_out, mi, *pieces = call(
+    stack = jax.ShapeDtypeStruct((4 * CHUNK, hid), BF)
+    d1, keep, give = call(
         backward_kernel, (groups,),
-        [scalar, thin, user_block, narrow, tile, tile, tile, tile, tile, tile, *weights,
-         whole((1, D + hid)), whole((1, D))],
-        [user_block, narrow] + [whole((CHUNK, hid))] * n_dp,
-        [buffer, jax.ShapeDtypeStruct((slots, D), BF)] + [piece] * n_dp,
+        [scalar, thin, user_block, narrow, tile, tile, tile, tile, tile, tile,
+         whole((hid, hid)), whole((hid, hid)), whole((1, D + hid)), whole((1, D))],
+        [tile, whole((4 * CHUNK, hid)), whole((4 * CHUNK, hid))], [wide, stack, stack],
         scratch=[pltpu.VMEM((WEND, hid), F32)],
-        flops=4 * slots * hid * (2 * D + 2 * hid), moved=16 * slots * hid,
-    )(me, delta, mlp_back, im, a1, s1, a2, s2, a3, s3, w1_user, w1_item, w2_weight, w3_weight, wo, go)
+        flops=2 * slots * hid * (2 * D + 4 * hid), moved=16 * slots * hid,
+    )(me, delta, mlp_back, im, a1, s1, a2, s2, a3, s3, w2_weight, w3_weight, wo, go)
 
     mlp_out = call(
-        place_kernel, (groups,),
-        [whole((1, slots)), whole((slots, D)), pl.BlockSpec(memory_space=pl.ANY)],
-        pl.BlockSpec((peers, cap, D), lambda i: (i, 1, 0)), buffer, aliases={2: 0},
-        flops=pick, moved=4 * slots * D,
-    )(ilane, mi, mu_out)
-
-    mlp_terms = exchange(mlp_out)
-
-    def shift_dp(x, k):
-        return lax.ppermute(x, "dp", [(s, (s + k) % n_dp) for s in range(n_dp)])
-
-    def shift_emb(x, kx, kz):
-        side = 4
-        return lax.ppermute(
-            x, "emb",
-            [
-                (a * side + b, (a + kx) % side * side + (b + kz) % side)
-                for a in range(side) for b in range(side)
-            ],
-        )
-
-    def ring_sum(v, step):
-        v = v.astype(BF)
-        one, two, three = (step(v, k).astype(F32) for k in (1, 2, 3))
-        return (v.astype(F32) + two) + (one + three)
-
-    part = pieces[0].astype(F32)
-    for k in range(1, n_dp):
-        part = part + shift_dp(pieces[k], k).astype(F32)
-    part = ring_sum(part, lambda v, k: shift_emb(v, k, 0))
-    part = ring_sum(part, lambda v, k: shift_emb(v, 0, k)).astype(BF)
-    found = [part] + [shift_dp(part, k) for k in range(1, n_dp)]
-    gw1u, gw1i, gw2, gw3, gwo = pl.pallas_call(
-        functools.partial(assemble_kernel, 1.0 / pairs),
-        in_specs=[scalar] + [pl.BlockSpec(memory_space=pltpu.VMEM)] * n_dp,
-        out_shape=[jax.ShapeDtypeStruct((count * n_dp, hid), F32) for _, count in PARTS],
-        compiler_params=PARAMS,
-    )(me, *found)
+        rows_kernel, (2 * groups,),
+        [whole((1, slots)), pl.BlockSpec((m, hid), lambda i: (jnp.minimum(i, last), 0)),
+         whole((D, hid)), whole((D, hid))],
+        pl.BlockSpec((peers, cap, D), lambda i: (i % groups, i // groups, 0)), buffer,
+        scratch=[pltpu.VMEM((slots, D), BF)], flops=pick + 4 * slots * hid * D,
+        moved=4 * slots * hid,
+    )(ilane, d1, w1_user, w1_item)
 
     def gather_add(terms, t, half, into=None):
         r = rows // 2
@@ -427,8 +411,65 @@
             flops=2 * rows * slots * D, moved=2 * slots * D + 4 * rows * D,
         )(wlane[t], terms, *(() if into is None else (into,)))
 
-    grads = [gather_add(gmf_terms, t, 0) for t in (0, 1)]
-    user_grad, item_grad = (gather_add(mlp_terms, t, 1, grads[t]) for t in (0, 1))
+    def shift_dp(x, k):
+        return lax.ppermute(x, "dp", [(s, (s + k) % n_dp) for s in range(n_dp)])
+
+    def shift_emb(x, kx, kz):
+        side = 4
+        return lax.ppermute(
+            x, "emb",
+            [
+                (a * side + b, (a + kx) % side * side + (b + kz) % side)
+                for a in range(side) for b in range(side)
+            ],
+        )
+
+    def ring_sum(v, step):
+        v = v.astype(BF)
+        one, two, three = (step(v, k).astype(F32) for k in (1, 2, 3))
+        return (v.astype(F32) + two) + (one + three)
+
+    def swap_core(x):
+        return lax.ppermute(x, "dp", [(s, s ^ 1) for s in range(n_dp)])
+
+    got = swap_core(give)
+    both = [
+        keep[j * CHUNK : (j + 1) * CHUNK].astype(F32) + got[j * CHUNK : (j + 1) * CHUNK].astype(F32)
+        for j in range(4)
+    ]
+    part = both[0]
+    for j in range(1, 4):
+        part = part + shift_dp(both[j].astype(BF), 2 * j).astype(F32)
+    mlp_out, part = lax.optimization_barrier((mlp_out, part))
+
+    def over_x(v, k):
+        return shift_emb(v, k, 0)
+
+    def over_z(v, k):
+        return shift_emb(v, 0, k)
+
+    top, low = part[:HALF], part[HALF:]
+    top, low = ring_sum(top, over_x), ring_sum(low, over_z)
+    top, low = ring_sum(top, over_z), ring_sum(low, over_x)
+    mlp_out, top, low = lax.optimization_barrier((mlp_out, top, low))
+    mlp_terms = exchange(mlp_out)
+    part = jnp.concatenate([top, low]).astype(BF)
+    user_grad = gather_add(gmf_terms, 0, 0)
+    item_grad = gather_add(gmf_terms, 1, 0)
+    found = [part] + [shift_dp(part, 2 * j) for j in range(1, 4)]
+    found = found + [swap_core(v) for v in found]
+    gw1u, gw1i, gw2, gw3, gwo = pl.pallas_call(
+        functools.partial(assemble_kernel, 1.0 / pairs),
+        in_specs=[scalar] + [pl.BlockSpec(memory_space=pltpu.VMEM)] * n_dp,
+        out_shape=[jax.ShapeDtypeStruct((count * n_dp, hid), F32) for _, count in PARTS],
+        compiler_params=PARAMS,
+    )(me, *found)
+
+    mlp_terms, user_grad, item_grad, gw1u, gw1i, gw2, gw3, gwo = lax.optimization_barrier(
+        (mlp_terms, user_grad, item_grad, gw1u, gw1i, gw2, gw3, gwo)
+    )
+    user_grad = gather_add(mlp_terms, 0, 1, user_grad)
+    item_grad = gather_add(mlp_terms, 1, 1, item_grad)
     grad_out = jnp.concatenate([gwo[0, :D], gwo[1]])
     return user_grad[None], item_grad[None], gw1u, gw1i, gw2, gw3, grad_out
 

time: 307 us -> 268 us (0.87)
  waiting for transfers between devices: 105 us -> 64 us
    ppermute x6 -> x12, waiting for transfers between devices: 23.9 us -> 5.62 us  [shift_emb(): lax.ppermute(x, 'emb', [(a * side + b, (a + kx) % side * side + (b + kz)...]
    ppermute x14 -> x6, waiting for transfers between devices: 25.2 us -> 8.11 us  [shift_dp(): return lax.ppermute(x, 'dp', [(s, (s + k) % n_dp) for s in range(n_dp)])]
    ppermute x14 -> x6, starting transfers between devices: 20.6 us -> 8.33 us  [shift_dp(): return lax.ppermute(x, 'dp', [(s, (s + k) % n_dp) for s in range(n_dp)])]
    ppermute x6 -> x12, starting transfers between devices: 9.43 us -> 18.4 us  [shift_emb(): lax.ppermute(x, 'emb', [(a * side + b, (a + kx) % side * side + (b + kz)...]
    all_to_all x4, waiting for transfers between devices: 56 us -> 47.7 us  [exchange(): return lax.all_to_all(x, 'emb', split_axis=0, concat_axis=0, tiled=True)]
    pallas_call x1, Pallas kernels: 7.83 us -> 11 us  [body(): call(rows_kernel, (2 * groups,), [whole((1, slots)), pl.BlockSpec((m, hid...]
  transfers between devices with their start and end apart: 24 -> 27, of which waited for: 19 -> 11; matrix products, arithmetic and copies ran while one was open for 2% -> 3% of each run, Pallas kernels for 25% -> 29%
where the time goes in v2:
time: 268 us; the launch traced here: 267 us
  Pallas kernels  123 us (46%)
  waiting for transfers between devices  64 us (24%)
  starting transfers between devices  46.8 us (17%)
  blocking collectives  15.4 us (6%)
  local copies, waits for them, and re-layouts  13.7 us (5%)
  other arithmetic  3.28 us (1%)
    all_to_all x4, waiting for transfers between devices, exchange(): return lax.all_to_all(x, 'emb', split_axis=0, concat_axis=0, tiled=True)  47.7 us
    pallas_call x1, Pallas kernels, body(): call(forward_kernel, (groups,), [whole((m, groups)), user_block, all_item...  25.2 us
    pallas_call x4, Pallas kernels, gather_add(): call(gather_add_kernel, (rows // r,), [whole((1, slots)), pl.BlockSpec((o...  24 us
    pallas_call x2, Pallas kernels, fetch(): call(fetch_kernel, (groups,), [whole((m, 2 * groups)), table, table], pl....  21.4 us
    all_to_all x4, starting transfers between devices, exchange(): return lax.all_to_all(x, 'emb', split_axis=0, concat_axis=0, tiled=True)  19.9 us
    ppermute x12, starting transfers between devices, shift_emb(): lax.ppermute(x, 'emb', [(a * side + b, (a + kx) % side * side + (b + kz)...  18.4 us
    pallas_call x1, Pallas kernels, body(): call(middle_kernel, (2 * groups,), [whole((m, groups)), whole((m, groups)...  18.3 us
    all_to_all x1, blocking collectives, exchange(): return lax.all_to_all(x, 'emb', split_axis=0, concat_axis=0, tiled=True)  15.4 us
  transfers between devices with their start and end apart: 27, of which 11 were waited for; matrix products, arithmetic and copies ran while one was open for 3% of the time, Pallas kernels for 29%

profile of v2, /device:TPU:0, one launch (start us, length us, event | category | flops | bytes accessed | tf_op | source)
XLA Modules:
  0.0 266.8 jit_solution(12206961218602566230)
XLA Ops:
  0.6 4.3 %shard_map.171 = (s32[16,512]{1,0:T(8,128)}, s32[16,256]{1,0:T(8,128)}, s32[2,256,16]{2,1,0:T(8,128)}) custom-call(s32[16,128]{1,0:T(8,128)} %bitcast.40, s32[16,128]{1,0:T(8,128)} %bitcast.41, s32[16,128]{1,0:T(8,128)} %bitcast.42, s32[16,128]{1,0:T(8,128)} %bitcast.43, s32[16,128]{1,0:T(8,128)} %bitcast.44), custom_call_target="tpu_custom_call" | custom-call | tf_op jit(solution)/shard_map/pallas_call | solution.py:315
  5.7 15.4 %all_to_all.29 = s32[16,1,512]{2,1,0:T(1,128)S(1)} all-to-all(s32[16,1,512]{2,1,0:T(1,128)S(1)} %copy.30), channel_id=1, replica_groups=mesh['emb'=16,'dp'=8] {'emb'}, dimensions={0} | all-to-all | bytes 65536 | tf_op jit(solution)/shard_map/all_to_all | solution.py:313
  22.3 10.7 %shard_map.173 = bf16[16,384,256]{2,1,0:T(8,128)(2,1)} custom-call(s32[768,8]{1,0:T(8,128)} %copy.35.wcol_ref, bf16[2048,512]{1,0:T(8,128)(2,1)} %ut_ref.3, bf16[2048,512]{1,0:T(8,128)(2,1)} %it_ref.3), custom_call_target="tpu_custom_call" | custom-call | flops 100663296 | bytes 81920 | tf_op jit(solution)/shard_map/pallas_call | solution.py:345
  33.0 3.7 %all-to-all-start.2 = ((bf16[16,384,256]{2,1,0:T(8,128)(2,1)}), bf16[16,384,256]{2,1,0:T(8,128)(2,1)S(1)}, u32[]{:S(2)}, u32[]{:S(2)}) async-start(bf16[16,384,256]{2,1,0:T(8,128)(2,1)} %shard_map.173), calls=%async_computation.2 | async-start | bytes 6291456 | tf_op jit(solution)/shard_map/all_to_all | solution.py:313
  36.7 10.7 %shard_map.172 = bf16[16,384,256]{2,1,0:T(8,128)(2,1)} custom-call(s32[768,8]{1,0:T(8,128)} %copy.35.wcol_ref, bf16[2048,512]{1,0:T(8,128)(2,1)} %ut_ref.3, bf16[2048,512]{1,0:T(8,128)(2,1)} %it_ref.3), custom_call_target="tpu_custom_call" | custom-call | flops 100663296 | bytes 81920 | tf_op jit(solution)/shard_map/pallas_call | solution.py:345
  47.5 30.7 %all-to-all-done.2.um_ref.im_ref = bf16[16,384,256]{2,1,0:T(8,128)(2,1)S(1)} async-done(((bf16[16,384,256]{2,1,0:T(8,128)(2,1)}), bf16[16,384,256]{2,1,0:T(8,128)(2,1)S(1)}, u32[]{:S(2)}, u32[]{:S(2)}) %all-to-all-start.2) | async-done | bytes 3145760 | tf_op jit(solution)/shard_map/all_to_all | solution.py:313
  79.8 4.7 %all-to-all-start.1 = ((bf16[16,384,256]{2,1,0:T(8,128)(2,1)}), bf16[16,384,256]{2,1,0:T(8,128)(2,1)}, u32[]{:S(2)}, u32[]{:S(2)}) async-start(bf16[16,384,256]{2,1,0:T(8,128)(2,1)} %shard_map.172), calls=%async_computation.1 | async-start | bytes 6291456 | tf_op jit(solution)/shard_map/all_to_all | solution.py:313
  88.7 25.2 %shard_map.174 = (bf16[3072,256]{1,0:T(8,128)(2,1)}, bf16[3072,512]{1,0:T(8,128)(2,1)}, bf16[3072,512]{1,0:T(8,128)(2,1)}, bf16[3072,512]{1,0:T(8,128)(2,1)}, bf...) custom-call(s32[768,4]{1,0:T(8,128)} %bitcast.30, ...), custom_call_target="tpu_custom_call" | custom-call | flops 150994944 | bytes 393216 | tf_op jit(solution)/shard_map/pallas_call | solution.py:354
  113.9 7.6 %all-to-all-done.1.ug_ref.ig_ref = bf16[16,384,256]{2,1,0:T(8,128)(2,1)} async-done(((bf16[16,384,256]{2,1,0:T(8,128)(2,1)}), bf16[16,384,256]{2,1,0:T(8,128)(2,1)}, u32[]{:S(2)}, u32[]{:S(2)}) %all-to-all-start.1) | async-done | bytes 3145760 | tf_op jit(solution)/shard_map/all_to_all | solution.py:313
  121.6 18.3 %shard_map.175 = (bf16[16,384,256]{2,1,0:T(8,128)(2,1)}, f32[3072,128]{1,0:T(8,128)}, f32[1,256]{1,0:T(1,128)}) custom-call(s32[768,4]{1,0:T(8,128)} %bitcast.31, s32[768,4]{1,0:T(8,128)} %bitcast.32, s32[1,3072]{1,0:T(1,128)} %reshape.69.ilane_ref, bf16[16,384,256]{2,1,0:T(8,128)(2,1)} %all-to-all-done.1.ug_ref.ig_ref, ...), custom_call_target="tpu_custom_call" | custom-call | flops 150994944 | bytes 147456 | tf_op jit(solution)/shard_map/pallas_call | solution.py:363
  139.8 6.5 %all-to-all-start.4 = ((bf16[16,384,256]{2,1,0:T(8,128)(2,1)}), bf16[16,384,256]{2,1,0:T(8,128)(2,1)S(1)}, u32[]{:S(2)}, u32[]{:S(2)}) async-start(bf16[16,384,256]{2,1,0:T(8,128)(2,1)} %get-tuple-element.61), calls=%async_computation.4 | async-start | bytes 6291456 | tf_op jit(solution)/shard_map/all_to_all | solution.py:313
  146.3 15.2 %shard_map.176 = (bf16[3072,512]{1,0:T(8,128)(2,1)}, bf16[800,512]{1,0:T(8,128)(2,1)}, bf16[800,512]{1,0:T(8,128)(2,1)}) custom-call(s32[1]{0:T(128)} %bitcast.7.me_ref, f32[3072,128]{1,0:T(8,128)} %get-tuple-element.46.delta_ref, bf16[16,384,256]{2,1,0:T(8,128)(2,1)} %copy-done, bf16[3072,256]{1,0:T(8,128)(2,1)} %get-tuple-element.47.im_ref, ...), custom_call_target="tpu_custom_call" | custom-call | flops 125829120 | bytes 393216 | tf_op jit(solution)/shard_map/pallas_call | solution.py:384
  170.7 11.0 %shard_map.177 = bf16[16,384,256]{2,1,0:T(8,128)(2,1)} custom-call(s32[1,3072]{1,0:T(1,128)} %reshape.69.ilane_ref, bf16[3072,512]{1,0:T(8,128)(2,1)} %get-tuple-element.55.d1_ref, bf16[256,512]{1,0:T(8,128)(2,1)} %w1u_ref.3, bf16[256,512]{1,0:T(8,128)(2,1)} %w1i_ref.3), custom_call_target="tpu_custom_call" | custom-call | flops 100663296 | bytes 98304 | tf_op jit(solution)/shard_map/pallas_call | solution.py:393
  190.5 2.7 %collective-permute-start.4 = (bf16[104,512]{1,0:T(8,128)(2,1)S(1)}, bf16[104,512]{1,0:T(8,128)(2,1)S(1)}, u32[]{:S(2)}, u32[]{:S(2)}) collective-permute-start(bf16[104,512]{1,0:T(8,128)(2,1)S(1)} %slice.92), channel_id=1, source_target_pairs={{0,64},{8,72},{16,80},{24,88},{32,96},{40,104},{48,112},{56,120},{... | collective-permute-start | bytes 319496 | tf_op jit(solution)/shard_map/ppermute | solution.py:419
  204.4 2.8 %collective-permute-done.8 = bf16[104,512]{1,0:T(8,128)(2,1)S(1)} collective-permute-done((bf16[104,512]{1,0:T(8,128)(2,1)S(1)}, bf16[104,512]{1,0:T(8,128)(2,1)S(1)}, u32[]{:S(2)}, u32[]{:S(2)}) %collective-permute-start.8) | collective-permute-done | bytes 106528 | tf_op jit(solution)/shard_map/ppermute | solution.py:419
  208.9 5.0 %all-to-all-start.3 = ((bf16[16,384,256]{2,1,0:T(8,128)(2,1)}), bf16[16,384,256]{2,1,0:T(8,128)(2,1)}, u32[]{:S(2)}, u32[]{:S(2)}) async-start(bf16[16,384,256]{2,1,0:T(8,128)(2,1)} %shard_map.177), calls=%async_computation.3 | async-start | bytes 6291456 | tf_op jit(solution)/shard_map/all_to_all | solution.py:313
  217.0 3.2 %collective-permute-done.18.refs_3_ = bf16[200,512]{1,0:T(8,128)(2,1)S(1)} collective-permute-done((bf16[200,512]{1,0:T(8,128)(2,1)S(1)}, bf16[200,512]{1,0:T(8,128)(2,1)S(1)}, u32[]{:S(2)}, u32[]{:S(2)}) %collective-permute-start.18) | collective-permute-done | bytes 204832 | tf_op jit(solution)/shard_map/ppermute | solution.py:415
  220.2 2.9 %collective-permute-done.17.refs_2_ = bf16[200,512]{1,0:T(8,128)(2,1)S(1)} collective-permute-done((bf16[200,512]{1,0:T(8,128)(2,1)S(1)}, bf16[200,512]{1,0:T(8,128)(2,1)S(1)}, u32[]{:S(2)}, u32[]{:S(2)}) %collective-permute-start.17) | collective-permute-done | bytes 204832 | tf_op jit(solution)/shard_map/ppermute | solution.py:415
  228.1 3.4 %shard_map.180 = (f32[256,512]{1,0:T(8,128)}, f32[256,512]{1,0:T(8,128)}, f32[512,512]{1,0:T(8,128)}, f32[512,512]{1,0:T(8,128)}, f32[64,512]{1,0:T(8,128)}) custom-call(s32[1]{0:T(128)} %bitcast.7.me_ref, bf16[200,512]{1,0:T(8,128)(2,1)} %copy-done.2, bf16[200,512]{1,0:T(8,128)(2,1)} %copy-done.5, bf16[200,512]{1,0:T(8,128)(2,1)} %copy-done.4, ...), custom_call_target="tpu_custom_call" | custom-call | tf_op jit(solution)/shard_map/pallas_call | solution.py:461
  231.4 6.0 %shard_map.179.rest_0_ = f32[2048,512]{1,0:T(8,128)} custom-call(s32[1,3072]{1,0:T(1,128)} %squeeze.23.lane_ref, bf16[16,384,256]{2,1,0:T(8,128)(2,1)} %copy-done.1), custom_call_target="tpu_custom_call" | custom-call | flops 50331648 | bytes 57344 | tf_op jit(solution)/shard_map/pallas_call | solution.py:404
  237.4 6.0 %shard_map.178.rest_0_ = f32[2048,512]{1,0:T(8,128)} custom-call(s32[1,3072]{1,0:T(1,128)} %squeeze.20.lane_ref, bf16[16,384,256]{2,1,0:T(8,128)(2,1)} %copy-done.1), custom_call_target="tpu_custom_call" | custom-call | flops 50331648 | bytes 57344 | tf_op jit(solution)/shard_map/pallas_call | solution.py:404
  243.4 9.4 %all-to-all-done.3.terms_ref = bf16[16,384,256]{2,1,0:T(8,128)(2,1)} async-done(((bf16[16,384,256]{2,1,0:T(8,128)(2,1)}), bf16[16,384,256]{2,1,0:T(8,128)(2,1)}, u32[]{:S(2)}, u32[]{:S(2)}) %all-to-all-start.3) | async-done | bytes 3145760 | tf_op jit(solution)/shard_map/all_to_all | solution.py:313
  254.2 6.0 %shard_map.181 = f32[2048,512]{1,0:T(8,128)} custom-call(s32[1,3072]{1,0:T(1,128)} %squeeze.20.lane_ref, bf16[16,384,256]{2,1,0:T(8,128)(2,1)} %all-to-all-done.3.terms_ref, f32[2048,512]{1,0:T(8,128)} %shard_map.178.rest_0_), custom_call_target="tpu_custom_call", output_to_operand_aliasing={{}: (2, {})} | custom-call | flops 50331648 | bytes 57344 | tf_op jit(solution)/shard_map/pallas_call | solution.py:404
  260.2 6.0 %shard_map.182 = f32[2048,512]{1,0:T(8,128)} custom-call(s32[1,3072]{1,0:T(1,128)} %squeeze.23.lane_ref, bf16[16,384,256]{2,1,0:T(8,128)(2,1)} %all-to-all-done.3.terms_ref, f32[2048,512]{1,0:T(8,128)} %shard_map.179.rest_0_), custom_call_target="tpu_custom_call", output_to_operand_aliasing={{}: (2, {})} | custom-call | flops 50331648 | bytes 57344 | tf_op jit(solution)/shard_map/pallas_call | solution.py:404
  (96 shorter events, 48.7 us)
Async XLA Ops:
  33.0 45.1 %all-to-all-start.2 = ((bf16[16,384,256]{2,1,0:T(8,128)(2,1)}), bf16[16,384,256]{2,1,0:T(8,128)(2,1)S(1)}, u32[]{:S(2)}, u32[]{:S(2)}) async-start(bf16[16,384,256]{2,1,0:T(8,128)(2,1)} %shard_map.173), calls=%async_computation.2 | async-start | bytes 6291456 | tf_op jit(solution)/shard_map/all_to_all | solution.py:313
  79.8 41.8 %all-to-all-start.1 = ((bf16[16,384,256]{2,1,0:T(8,128)(2,1)}), bf16[16,384,256]{2,1,0:T(8,128)(2,1)}, u32[]{:S(2)}, u32[]{:S(2)}) async-start(bf16[16,384,256]{2,1,0:T(8,128)(2,1)} %shard_map.172), calls=%async_computation.1 | async-start | bytes 6291456 | tf_op jit(solution)/shard_map/all_to_all | solution.py:313
  139.8 67.4 %all-to-all-start.4 = ((bf16[16,384,256]{2,1,0:T(8,128)(2,1)}), bf16[16,384,256]{2,1,0:T(8,128)(2,1)S(1)}, u32[]{:S(2)}, u32[]{:S(2)}) async-start(bf16[16,384,256]{2,1,0:T(8,128)(2,1)} %get-tuple-element.61), calls=%async_computation.4 | async-start | bytes 6291456 | tf_op jit(solution)/shard_map/all_to_all | solution.py:313
  165.4 16.3 %collective-permute-start.1 = (bf16[200,512]{1,0:T(8,128)(2,1)S(1)}, bf16[200,512]{1,0:T(8,128)(2,1)S(1)}, u32[]{:S(2)}, u32[]{:S(2)}) collective-permute-start(bf16[200,512]{1,0:T(8,128)(2,1)S(1)} %get-tuple-element.77), channel_id=1, source_target_pairs={{0,2},{1,3},{2,4},{3,5},{4,6},{5,7},{6,0},{7,1},{8,10},{9,11},{10,... | collective-permute-start | bytes 614408 | tf_op jit(solution)/shard_map/ppermute | solution.py:415
  167.1 14.7 %collective-permute-start.3 = (bf16[200,512]{1,0:T(8,128)(2,1)S(1)}, bf16[200,512]{1,0:T(8,128)(2,1)S(1)}, u32[]{:S(2)}, u32[]{:S(2)}) collective-permute-start(bf16[200,512]{1,0:T(8,128)(2,1)S(1)} %get-tuple-element.78), channel_id=1, source_target_pairs={{0,6},{1,7},{2,0},{3,1},{4,2},{5,3},{6,4},{7,5},{8,14},{9,15},{10,... | collective-permute-start | bytes 614408 | tf_op jit(solution)/shard_map/ppermute | solution.py:415
  168.8 13.0 %collective-permute-start.2 = (bf16[200,512]{1,0:T(8,128)(2,1)S(1)}, bf16[200,512]{1,0:T(8,128)(2,1)S(1)}, u32[]{:S(2)}, u32[]{:S(2)}) collective-permute-start(bf16[200,512]{1,0:T(8,128)(2,1)S(1)} %get-tuple-element.79), channel_id=1, source_target_pairs={{0,4},{1,5},{2,6},{3,7},{4,0},{5,1},{6,2},{7,3},{8,12},{9,13},{10,... | collective-permute-start | bytes 614408 | tf_op jit(solution)/shard_map/ppermute | solution.py:415
  182.9 10.3 %collective-permute-start.11 = (bf16[96,512]{1,0:T(8,128)(2,1)S(1)}, bf16[96,512]{1,0:T(8,128)(2,1)S(1)}, u32[]{:S(2)}, u32[]{:S(2)}) collective-permute-start(bf16[96,512]{1,0:T(8,128)(2,1)S(1)} %slice.93), channel_id=1, source_target_pairs={{0,8},{8,16},{16,24},{24,0},{32,40},{40,48},{48,56},{56,32},{64,72... | collective-permute-start | bytes 294920 | tf_op jit(solution)/shard_map/ppermute | solution.py:419
  184.8 9.8 %collective-permute-start.10 = (bf16[96,512]{1,0:T(8,128)(2,1)S(1)}, bf16[96,512]{1,0:T(8,128)(2,1)S(1)}, u32[]{:S(2)}, u32[]{:S(2)}) collective-permute-start(bf16[96,512]{1,0:T(8,128)(2,1)S(1)} %slice.93), channel_id=1, source_target_pairs={{0,16},{8,24},{16,0},{24,8},{32,48},{40,56},{48,32},{56,40},{64,80... | collective-permute-start | bytes 294920 | tf_op jit(solution)/shard_map/ppermute | solution.py:419
  187.5 7.2 %collective-permute-start.12 = (bf16[96,512]{1,0:T(8,128)(2,1)S(1)}, bf16[96,512]{1,0:T(8,128)(2,1)S(1)}, u32[]{:S(2)}, u32[]{:S(2)}) collective-permute-start(bf16[96,512]{1,0:T(8,128)(2,1)S(1)} %slice.93), channel_id=1, source_target_pairs={{0,24},{8,0},{16,8},{24,16},{32,56},{40,32},{48,40},{56,48},{64,88... | collective-permute-start | bytes 294920 | tf_op jit(solution)/shard_map/ppermute | solution.py:419
  189.0 7.8 %collective-permute-start.5 = (bf16[104,512]{1,0:T(8,128)(2,1)S(1)}, bf16[104,512]{1,0:T(8,128)(2,1)S(1)}, u32[]{:S(2)}, u32[]{:S(2)}) collective-permute-start(bf16[104,512]{1,0:T(8,128)(2,1)S(1)} %slice.92), channel_id=1, source_target_pairs={{0,32},{8,40},{16,48},{24,56},{32,64},{40,72},{48,80},{56,88},{64,... | collective-permute-start | bytes 319496 | tf_op jit(solution)/shard_map/ppermute | solution.py:419
  190.5 7.4 %collective-permute-start.4 = (bf16[104,512]{1,0:T(8,128)(2,1)S(1)}, bf16[104,512]{1,0:T(8,128)(2,1)S(1)}, u32[]{:S(2)}, u32[]{:S(2)}) collective-permute-start(bf16[104,512]{1,0:T(8,128)(2,1)S(1)} %slice.92), channel_id=1, source_target_pairs={{0,64},{8,72},{16,80},{24,88},{32,96},{40,104},{48,112},{56,120},{... | collective-permute-start | bytes 319496 | tf_op jit(solution)/shard_map/ppermute | solution.py:419
  193.2 5.3 %collective-permute-start.6 = (bf16[104,512]{1,0:T(8,128)(2,1)S(1)}, bf16[104,512]{1,0:T(8,128)(2,1)S(1)}, u32[]{:S(2)}, u32[]{:S(2)}) collective-permute-start(bf16[104,512]{1,0:T(8,128)(2,1)S(1)} %slice.92), channel_id=1, source_target_pairs={{0,96},{8,104},{16,112},{24,120},{32,0},{40,8},{48,16},{56,24},{64... | collective-permute-start | bytes 319496 | tf_op jit(solution)/shard_map/ppermute | solution.py:419
  194.7 5.9 %collective-permute-start.15 = (bf16[96,512]{1,0:T(8,128)(2,1)S(1)}, bf16[96,512]{1,0:T(8,128)(2,1)S(1)}, u32[]{:S(2)}, u32[]{:S(2)}) collective-permute-start(bf16[96,512]{1,0:T(8,128)(2,1)S(1)} %add_convert_fusion.4), channel_id=1, source_target_pairs={{0,96},{8,104},{16,112},{24,120},{32,0},{40,8},{48,16},{56,24},{64... | collective-permute-start | bytes 294920 | tf_op jit(solution)/shard_map/ppermute | solution.py:419
  194.9 7.1 %collective-permute-start.14 = (bf16[96,512]{1,0:T(8,128)(2,1)S(1)}, bf16[96,512]{1,0:T(8,128)(2,1)S(1)}, u32[]{:S(2)}, u32[]{:S(2)}) collective-permute-start(bf16[96,512]{1,0:T(8,128)(2,1)S(1)} %add_convert_fusion.4), channel_id=1, source_target_pairs={{0,32},{8,40},{16,48},{24,56},{32,64},{40,72},{48,80},{56,88},{64,... | collective-permute-start | bytes 294920 | tf_op jit(solution)/shard_map/ppermute | solution.py:419
  196.8 6.1 %collective-permute-start.13 = (bf16[96,512]{1,0:T(8,128)(2,1)S(1)}, bf16[96,512]{1,0:T(8,128)(2,1)S(1)}, u32[]{:S(2)}, u32[]{:S(2)}) collective-permute-start(bf16[96,512]{1,0:T(8,128)(2,1)S(1)} %add_convert_fusion.4), channel_id=1, source_target_pairs={{0,64},{8,72},{16,80},{24,88},{32,96},{40,104},{48,112},{56,120},{... | collective-permute-start | bytes 294920 | tf_op jit(solution)/shard_map/ppermute | solution.py:419
  198.5 5.8 %collective-permute-start.9 = (bf16[104,512]{1,0:T(8,128)(2,1)S(1)}, bf16[104,512]{1,0:T(8,128)(2,1)S(1)}, u32[]{:S(2)}, u32[]{:S(2)}) collective-permute-start(bf16[104,512]{1,0:T(8,128)(2,1)S(1)} %add_convert_fusion.3), channel_id=1, source_target_pairs={{0,24},{8,0},{16,8},{24,16},{32,56},{40,32},{48,40},{56,48},{64,88... | collective-permute-start | bytes 319496 | tf_op jit(solution)/shard_map/ppermute | solution.py:419
  200.1 7.1 %collective-permute-start.8 = (bf16[104,512]{1,0:T(8,128)(2,1)S(1)}, bf16[104,512]{1,0:T(8,128)(2,1)S(1)}, u32[]{:S(2)}, u32[]{:S(2)}) collective-permute-start(bf16[104,512]{1,0:T(8,128)(2,1)S(1)} %add_convert_fusion.3), channel_id=1, source_target_pairs={{0,8},{8,16},{16,24},{24,0},{32,40},{40,48},{48,56},{56,32},{64,72... | collective-permute-start | bytes 319496 | tf_op jit(solution)/shard_map/ppermute | solution.py:419
  200.6 6.5 %collective-permute-start.7 = (bf16[104,512]{1,0:T(8,128)(2,1)S(1)}, bf16[104,512]{1,0:T(8,128)(2,1)S(1)}, u32[]{:S(2)}, u32[]{:S(2)}) collective-permute-start(bf16[104,512]{1,0:T(8,128)(2,1)S(1)} %add_convert_fusion.3), channel_id=1, source_target_pairs={{0,16},{8,24},{16,0},{24,8},{32,48},{40,56},{48,32},{56,40},{64,80... | collective-permute-start | bytes 319496 | tf_op jit(solution)/shard_map/ppermute | solution.py:419
  208.9 43.9 %all-to-all-start.3 = ((bf16[16,384,256]{2,1,0:T(8,128)(2,1)}), bf16[16,384,256]{2,1,0:T(8,128)(2,1)}, u32[]{:S(2)}, u32[]{:S(2)}) async-start(bf16[16,384,256]{2,1,0:T(8,128)(2,1)} %shard_map.177), calls=%async_computation.3 | async-start | bytes 6291456 | tf_op jit(solution)/shard_map/all_to_all | solution.py:313
  214.0 6.2 %collective-permute-start.18 = (bf16[200,512]{1,0:T(8,128)(2,1)S(1)}, bf16[200,512]{1,0:T(8,128)(2,1)S(1)}, u32[]{:S(2)}, u32[]{:S(2)}) collective-permute-start(bf16[200,512]{1,0:T(8,128)(2,1)S(1)} %pad_maximum_fusion.refs_0_), channel_id=1, source_target_pairs={{0,6},{1,7},{2,0},{3,1},{4,2},{5,3},{6,4},{7,5},{8,14},{9,15},{10,... | collective-permute-start | bytes 614408 | tf_op jit(solution)/shard_map/ppermute | solution.py:415
  215.3 7.7 %collective-permute-start.17 = (bf16[200,512]{1,0:T(8,128)(2,1)S(1)}, bf16[200,512]{1,0:T(8,128)(2,1)S(1)}, u32[]{:S(2)}, u32[]{:S(2)}) collective-permute-start(bf16[200,512]{1,0:T(8,128)(2,1)S(1)} %pad_maximum_fusion.refs_0_), channel_id=1, source_target_pairs={{0,4},{1,5},{2,6},{3,7},{4,0},{5,1},{6,2},{7,3},{8,12},{9,13},{10,... | collective-permute-start | bytes 614408 | tf_op jit(solution)/shard_map/ppermute | solution.py:415
  216.8 8.4 %collective-permute-start.16 = (bf16[200,512]{1,0:T(8,128)(2,1)S(1)}, bf16[200,512]{1,0:T(8,128)(2,1)S(1)}, u32[]{:S(2)}, u32[]{:S(2)}) collective-permute-start(bf16[200,512]{1,0:T(8,128)(2,1)S(1)} %pad_maximum_fusion.refs_0_), channel_id=1, source_target_pairs={{0,2},{1,3},{2,4},{3,5},{4,6},{5,7},{6,0},{7,1},{8,10},{9,11},{10,... | collective-permute-start | bytes 614408 | tf_op jit(solution)/shard_map/ppermute | solution.py:415
  217.0 9.5 %collective-permute-start.19 = (bf16[200,512]{1,0:T(8,128)(2,1)S(1)}, bf16[200,512]{1,0:T(8,128)(2,1)S(1)}, u32[]{:S(2)}, u32[]{:S(2)}) collective-permute-start(bf16[200,512]{1,0:T(8,128)(2,1)S(1)} %pad_maximum_fusion.refs_0_), channel_id=1, source_target_pairs={{0,1},{1,0},{2,3},{3,2},{4,5},{5,4},{6,7},{7,6},{8,9},{9,8},{10,11... | collective-permute-start | bytes 614408 | tf_op jit(solution)/shard_map/ppermute | solution.py:433
  220.2 6.3 %collective-permute-start.22 = (bf16[200,512]{1,0:T(8,128)(2,1)S(1)}, bf16[200,512]{1,0:T(8,128)(2,1)S(1)}, u32[]{:S(2)}, u32[]{:S(2)}) collective-permute-start(bf16[200,512]{1,0:T(8,128)(2,1)S(1)} %collective-permute-done.18.refs_3_), channel_id=1, source_target_pairs={{0,1},{1,0},{2,3},{3,2},{4,5},{5,4},{6,7},{7,6},{8,9},{9,8},{10,11... | collective-permute-start | bytes 614408 | tf_op jit(solution)/shard_map/ppermute | solution.py:433
  (15 other events, 112.6 us)

commit v3 on v2

--- a/solution.py
+++ b/solution.py
@@ -12,7 +12,7 @@
 ROWS = ("emb", "dp")
 
 
-PARAMS = pltpu.CompilerParams(vmem_limit_bytes=56 << 20)
+PARAMS = pltpu.CompilerParams(vmem_limit_bytes=63 << 20)
 
 
 W1U, W1I, W2, W3, WO, WEND = 0, 256, 512, 1024, 1536, 1600
@@ -119,8 +119,11 @@
             spread(chosen, rows(lo)), slots
         )
 
-    req_ref[:, 0:256] = wanted(u_chosen, u_slots, ur_hi, ur_lo).astype(I32)
-    req_ref[:, 256:512] = wanted(i_chosen, i_slots, ir_hi, ir_lo).astype(I32)
+    req = jnp.concatenate(
+        [wanted(u_chosen, u_slots, ur_hi, ur_lo), wanted(i_chosen, i_slots, ir_hi, ir_lo)], axis=1
+    ).astype(I32)
+    for o in range(owners):
+        req_ref[o] = req[o : o + 1]
     s_hi, s_lo = spread(u_chosen, rows(is_hi)), spread(u_chosen, rows(is_lo))
     s_flag = spread(u_chosen, rows(flag))
     lanes_ref[...] = (dot_nt(s_hi, u_slots) * 64.0 + dot_nt(s_lo, u_slots)).astype(I32)
@@ -128,13 +131,15 @@
     cols_ref[1] = dot_nt(u_slots, s_flag).astype(I32)
 
 
-def fetch_kernel(wcol_ref, ut_ref, it_ref, out_ref):
-    g = pl.program_id(0)
-    groups = pl.num_programs(0)
+def fetch_kernel(asked_ref, ut_ref, it_ref, out_ref):
     peers, both, width = out_ref.shape
     cap = both // 2
+    first = pl.program_id(0) * peers
+    rows = [asked_ref[first + q] for q in range(peers)]
     for t, table in enumerate((ut_ref, it_ref)):
-        col = column(wcol_ref[...], g + t * groups)
+        lanes = jnp.concatenate([r[:, t * 256 : (t + 1) * 256] for r in rows + rows], axis=0)
+        cols = jnp.transpose(lanes)
+        col = jnp.concatenate([cols[:cap, q : q + 1] for q in range(peers)], axis=0)
         got = dot_nn(pick_rows(col, table.shape[0]), table[...]).astype(BF)
         out_ref[:, t * cap : (t + 1) * cap, :] = got.reshape(peers, cap, width)
 
@@ -275,11 +280,21 @@
 
 
 def gather_add_kernel(lane_ref, terms_ref, *rest):
-    out_ref = rest[-1]
-    m = out_ref.shape[0]
+    user_out, item_out = rest[-2:]
+    step = pl.program_id(0)
+    steps = pl.num_programs(0) // 2
+    m = user_out.shape[0]
     slots = terms_ref.shape[0] * terms_ref.shape[1]
-    sel = put_rows(lane_ref[...], pl.program_id(0) * m, m)
-    out_ref[...] = dot_nn(sel, terms_ref[...].reshape(slots, D))
+    sel = put_rows(lane_ref[0], step % steps * m, m)
+    got = dot_nn(sel, terms_ref[...].reshape(slots, D))
+
+    @pl.when(step < steps)
+    def _():
+        user_out[...] = got
+
+    @pl.when(step >= steps)
+    def _():
+        item_out[...] = got
 
 
 def whole(shape):
@@ -315,15 +330,15 @@
     req, lanes, cols = pl.pallas_call(
         functools.partial(arrange_kernel, cap),
         out_shape=(
-            jax.ShapeDtypeStruct((owners, 512), I32),
+            jax.ShapeDtypeStruct((owners, 1, 512), I32),
             jax.ShapeDtypeStruct((owners, 256), I32),
             jax.ShapeDtypeStruct((2, 256, owners), I32),
         ),
         compiler_params=PARAMS,
     )(*(a.reshape(blocks, 128) for a in (user_owner, user_row, item_owner, item_row, labels)))
 
-    wanted = exchange(req).reshape(owners, 2, 256)[:, :, :cap]
-    wcol = wanted.reshape(groups, peers, 2, cap).transpose(1, 3, 2, 0).reshape(m, 2 * groups)
+    asked = exchange(req)
+    wanted = asked.reshape(owners, 2, 256)[:, :, :cap]
     wlane = wanted.transpose(1, 0, 2).reshape(2, 1, slots)
     ilane = lanes[:, :cap].reshape(1, slots)
     side = cols[:, :cap, :].reshape(2, cap, groups, peers).transpose(0, 3, 1, 2)
@@ -343,10 +358,10 @@
     def fetch(half):
         table = pl.BlockSpec((rows, D), lambda i: (0, half))
         return call(
-            fetch_kernel, (groups,), [whole((m, 2 * groups)), table, table],
+            fetch_kernel, (groups,), [whole((owners, 1, 512)), table, table],
             pl.BlockSpec((peers, 2 * cap, D), lambda i: (i, 0, 0)), buffer,
             flops=4 * slots * rows * D, moved=4 * slots * D + 4 * rows * D,
-        )(wcol, user_table, item_table)
+        )(asked, user_table, item_table)
 
     mlp_back = exchange(fetch(1))
     gmf_back = exchange(fetch(0))
@@ -381,11 +396,15 @@
     n_dp = lax.axis_size("dp")
     scalar = pl.BlockSpec(memory_space=pltpu.SMEM)
     stack = jax.ShapeDtypeStruct((4 * CHUNK, hid), BF)
+    fine = groups
+    small_tile = pl.BlockSpec((slots // fine, hid), lambda i: (i, 0))
     d1, keep, give = call(
-        backward_kernel, (groups,),
-        [scalar, thin, user_block, narrow, tile, tile, tile, tile, tile, tile,
+        backward_kernel, (fine,),
+        [scalar, pl.BlockSpec((slots // fine, 128), lambda i: (i, 0)),
+         pl.BlockSpec((owners // fine, cap, D), lambda i: (i, 0, 0)),
+         pl.BlockSpec((slots // fine, D), lambda i: (i, 0)), *[small_tile] * 6,
          whole((hid, hid)), whole((hid, hid)), whole((1, D + hid)), whole((1, D))],
-        [tile, whole((4 * CHUNK, hid)), whole((4 * CHUNK, hid))], [wide, stack, stack],
+        [small_tile, whole((4 * CHUNK, hid)), whole((4 * CHUNK, hid))], [wide, stack, stack],
         scratch=[pltpu.VMEM((WEND, hid), F32)],
         flops=2 * slots * hid * (2 * D + 4 * hid), moved=16 * slots * hid,
     )(me, delta, mlp_back, im, a1, s1, a2, s2, a3, s3, w2_weight, w3_weight, wo, go)
@@ -399,17 +418,20 @@
         moved=4 * slots * hid,
     )(ilane, d1, w1_user, w1_item)
 
-    def gather_add(terms, t, half, into=None):
-        r = rows // 2
+    def gather_add(terms, half, *into):
+        steps = 4
+        r = rows // steps
+        grad = jax.ShapeDtypeStruct((rows, 2 * D), F32)
         return call(
-            gather_add_kernel, (rows // r,),
-            [whole((1, slots)), pl.BlockSpec((owners, cap, D), lambda i: (0, t, 0))]
-            + ([] if into is None else [pl.BlockSpec(memory_space=pl.ANY)]),
-            pl.BlockSpec((r, D), lambda i: (i, half)),
-            jax.ShapeDtypeStruct((rows, 2 * D), F32),
-            aliases=None if into is None else {2: 0},
-            flops=2 * rows * slots * D, moved=2 * slots * D + 4 * rows * D,
-        )(wlane[t], terms, *(() if into is None else (into,)))
+            gather_add_kernel, (2 * steps,),
+            [pl.BlockSpec((1, 1, slots), lambda i: (i // steps, 0, 0)),
+             pl.BlockSpec((owners, cap, D), lambda i: (0, i // steps, 0))]
+            + [pl.BlockSpec(memory_space=pl.ANY)] * len(into),
+            [pl.BlockSpec((r, D), lambda i: (jnp.minimum(i, steps - 1), half)),
+             pl.BlockSpec((r, D), lambda i: (jnp.maximum(i - steps, 0), half))],
+            [grad, grad], aliases={2 + k: k for k in range(len(into))},
+            flops=4 * rows * slots * D, moved=4 * slots * D + 8 * rows * D,
+        )(wlane, terms, *into)
 
     def shift_dp(x, k):
         return lax.ppermute(x, "dp", [(s, (s + k) % n_dp) for s in range(n_dp)])
@@ -454,8 +476,7 @@
     mlp_out, top, low = lax.optimization_barrier((mlp_out, top, low))
     mlp_terms = exchange(mlp_out)
     part = jnp.concatenate([top, low]).astype(BF)
-    user_grad = gather_add(gmf_terms, 0, 0)
-    item_grad = gather_add(gmf_terms, 1, 0)
+    user_grad, item_grad = gather_add(gmf_terms, 0)
     found = [part] + [shift_dp(part, 2 * j) for j in range(1, 4)]
     found = found + [swap_core(v) for v in found]
     gw1u, gw1i, gw2, gw3, gwo = pl.pallas_call(
@@ -465,12 +486,11 @@
         compiler_params=PARAMS,
     )(me, *found)
 
-    mlp_terms, user_grad, item_grad, gw1u, gw1i, gw2, gw3, gwo = lax.optimization_barrier(
-        (mlp_terms, user_grad, item_grad, gw1u, gw1i, gw2, gw3, gwo)
+    grad_out = jnp.concatenate([gwo[0, :D], gwo[1]])
+    mlp_terms, user_grad, item_grad, grad_out = lax.optimization_barrier(
+        (mlp_terms, user_grad, item_grad, grad_out)
     )
-    user_grad = gather_add(mlp_terms, 0, 1, user_grad)
-    item_grad = gather_add(mlp_terms, 1, 1, item_grad)
-    grad_out = jnp.concatenate([gwo[0, :D], gwo[1]])
+    user_grad, item_grad = gather_add(mlp_terms, 1, user_grad, item_grad)
     return user_grad[None], item_grad[None], gw1u, gw1i, gw2, gw3, grad_out
 
 

time: 268 us -> 262 us (0.978)
  local copies, waits for them, and re-layouts: 13.7 us -> 6.95 us
    unnamed x25 -> x23, local copies, waits for them, and re-layouts: 4.81 us -> 1.48 us
    pallas_call x7 -> x5, Pallas kernels: 60.6 us -> 60 us  [the longest x2 22.7 us: gather_add(): call(gather_add_kernel, (2 * steps,), [pl.BlockSpec((1, 1, slots), lambda...]
  transfers between devices with their start and end apart: 27 -> 27, of which waited for: 11 -> 11; matrix products, arithmetic and copies ran while one was open for 3% -> 4% of each run, Pallas kernels for 29% -> 30%
where the time goes in v3:
time: 262 us; the launch traced here: 261 us
  Pallas kernels  122 us (47%)
  waiting for transfers between devices  63.3 us (24%)
  starting transfers between devices  47.5 us (18%)
  blocking collectives  15.7 us (6%)
  local copies, waits for them, and re-layouts  6.95 us (3%)
  other arithmetic  4.33 us (2%)
    all_to_all x4, waiting for transfers between devices, exchange(): return lax.all_to_all(x, 'emb', split_axis=0, concat_axis=0, tiled=True)  47.6 us
    pallas_call x1, Pallas kernels, body(): call(forward_kernel, (groups,), [whole((m, groups)), user_block, all_item...  25.3 us
    pallas_call x2, Pallas kernels, gather_add(): call(gather_add_kernel, (2 * steps,), [pl.BlockSpec((1, 1, slots), lambda...  22.7 us
    pallas_call x2, Pallas kernels, fetch(): call(fetch_kernel, (groups,), [whole((owners, 1, 512)), table, table], pl...  22.1 us
    all_to_all x4, starting transfers between devices, exchange(): return lax.all_to_all(x, 'emb', split_axis=0, concat_axis=0, tiled=True)  20.7 us
    ppermute x12, starting transfers between devices, shift_emb(): lax.ppermute(x, 'emb', [(a * side + b, (a + kx) % side * side + (b + kz)...  18.4 us
    pallas_call x1, Pallas kernels, body(): call(middle_kernel, (2 * groups,), [whole((m, groups)), whole((m, groups)...  18.3 us
    all_to_all x1, blocking collectives, exchange(): return lax.all_to_all(x, 'emb', split_axis=0, concat_axis=0, tiled=True)  15.7 us
  transfers between devices with their start and end apart: 27, of which 11 were waited for; matrix products, arithmetic and copies ran while one was open for 4% of the time, Pallas kernels for 30%

profile of v3, /device:TPU:0, one launch (start us, length us, event | category | flops | bytes accessed | tf_op | source)
XLA Modules:
  0.0 260.9 jit_solution(2553069475824581673)
XLA Ops:
  0.6 4.3 %shard_map.171 = (s32[16,1,512]{2,1,0:T(1,128)}, s32[16,256]{1,0:T(8,128)}, s32[2,256,16]{2,1,0:T(8,128)}) custom-call(s32[16,128]{1,0:T(8,128)} %bitcast.29, s32[16,128]{1,0:T(8,128)} %bitcast.30, s32[16,128]{1,0:T(8,128)} %bitcast.31, s32[16,128]{1,0:T(8,128)} %bitcast.32, s32[16,128]{1,0:T(8,128)} %bitcast.33), custom_call_target="tpu_custom_call" | custom-call | tf_op jit(solution)/shard_map/pallas_call | solution.py:330
  4.9 15.7 %all_to_all.25.asked_ref = s32[16,1,512]{2,1,0:T(1,128)} all-to-all(s32[16,1,512]{2,1,0:T(1,128)} %get-tuple-element.42), channel_id=1, replica_groups=mesh['emb'=16,'dp'=8] {'emb'}, dimensions={0} | all-to-all | bytes 65536 | tf_op jit(solution)/shard_map/all_to_all | solution.py:328
  20.6 11.1 %shard_map.173 = bf16[16,384,256]{2,1,0:T(8,128)(2,1)} custom-call(s32[16,1,512]{2,1,0:T(1,128)} %all_to_all.25.asked_ref, bf16[2048,512]{1,0:T(8,128)(2,1)} %ut_ref.3, bf16[2048,512]{1,0:T(8,128)(2,1)} %it_ref.3), custom_call_target="tpu_custom_call" | custom-call | flops 100663296 | bytes 81920 | tf_op jit(solution)/shard_map/pallas_call | solution.py:360
  31.7 4.5 %all-to-all-start.2 = ((bf16[16,384,256]{2,1,0:T(8,128)(2,1)}), bf16[16,384,256]{2,1,0:T(8,128)(2,1)}, u32[]{:S(2)}, u32[]{:S(2)}) async-start(bf16[16,384,256]{2,1,0:T(8,128)(2,1)} %shard_map.173), calls=%async_computation.2 | async-start | bytes 6291456 | tf_op jit(solution)/shard_map/all_to_all | solution.py:328
  36.2 11.1 %shard_map.172 = bf16[16,384,256]{2,1,0:T(8,128)(2,1)} custom-call(s32[16,1,512]{2,1,0:T(1,128)} %all_to_all.25.asked_ref, bf16[2048,512]{1,0:T(8,128)(2,1)} %ut_ref.3, bf16[2048,512]{1,0:T(8,128)(2,1)} %it_ref.3), custom_call_target="tpu_custom_call" | custom-call | flops 100663296 | bytes 81920 | tf_op jit(solution)/shard_map/pallas_call | solution.py:360
  47.3 30.1 %all-to-all-done.2.um_ref.im_ref = bf16[16,384,256]{2,1,0:T(8,128)(2,1)} async-done(((bf16[16,384,256]{2,1,0:T(8,128)(2,1)}), bf16[16,384,256]{2,1,0:T(8,128)(2,1)}, u32[]{:S(2)}, u32[]{:S(2)}) %all-to-all-start.2) | async-done | bytes 3145760 | tf_op jit(solution)/shard_map/all_to_all | solution.py:328
  77.3 4.7 %all-to-all-start.1 = ((bf16[16,384,256]{2,1,0:T(8,128)(2,1)}), bf16[16,384,256]{2,1,0:T(8,128)(2,1)}, u32[]{:S(2)}, u32[]{:S(2)}) async-start(bf16[16,384,256]{2,1,0:T(8,128)(2,1)} %shard_map.172), calls=%async_computation.1 | async-start | bytes 6291456 | tf_op jit(solution)/shard_map/all_to_all | solution.py:328
  85.3 25.3 %shard_map.174 = (bf16[3072,256]{1,0:T(8,128)(2,1)}, bf16[3072,512]{1,0:T(8,128)(2,1)}, bf16[3072,512]{1,0:T(8,128)(2,1)}, bf16[3072,512]{1,0:T(8,128)(2,1)}, bf...) custom-call(s32[768,4]{1,0:T(8,128)} %bitcast.22, ...), custom_call_target="tpu_custom_call" | custom-call | flops 150994944 | bytes 393216 | tf_op jit(solution)/shard_map/pallas_call | solution.py:369
  110.7 8.5 %all-to-all-done.1.ug_ref.ig_ref = bf16[16,384,256]{2,1,0:T(8,128)(2,1)} async-done(((bf16[16,384,256]{2,1,0:T(8,128)(2,1)}), bf16[16,384,256]{2,1,0:T(8,128)(2,1)}, u32[]{:S(2)}, u32[]{:S(2)}) %all-to-all-start.1) | async-done | bytes 3145760 | tf_op jit(solution)/shard_map/all_to_all | solution.py:328
  119.2 18.3 %shard_map.175 = (bf16[16,384,256]{2,1,0:T(8,128)(2,1)}, f32[3072,128]{1,0:T(8,128)}, f32[1,256]{1,0:T(1,128)}) custom-call(s32[768,4]{1,0:T(8,128)} %bitcast.23, s32[768,4]{1,0:T(8,128)} %bitcast.24, s32[1,3072]{1,0:T(1,128)} %reshape.59.ilane_ref, bf16[16,384,256]{2,1,0:T(8,128)(2,1)} %all-to-all-done.1.ug_ref.ig_ref, ...), custom_call_target="tpu_custom_call" | custom-call | flops 150994944 | bytes 147456 | tf_op jit(solution)/shard_map/pallas_call | solution.py:378
  137.5 6.5 %all-to-all-start.4 = ((bf16[16,384,256]{2,1,0:T(8,128)(2,1)}), bf16[16,384,256]{2,1,0:T(8,128)(2,1)}, u32[]{:S(2)}, u32[]{:S(2)}) async-start(bf16[16,384,256]{2,1,0:T(8,128)(2,1)} %get-tuple-element.61), calls=%async_computation.4 | async-start | bytes 6291456 | tf_op jit(solution)/shard_map/all_to_all | solution.py:328
  143.9 15.2 %shard_map.176 = (bf16[3072,512]{1,0:T(8,128)(2,1)}, bf16[800,512]{1,0:T(8,128)(2,1)}, bf16[800,512]{1,0:T(8,128)(2,1)}) custom-call(s32[1]{0:T(128)} %bitcast.6.me_ref, f32[3072,128]{1,0:T(8,128)} %get-tuple-element.46.delta_ref, bf16[16,384,256]{2,1,0:T(8,128)(2,1)} %all-to-all-done.2.um_ref.im_ref, bf16[3072,256]{1,0:T(8,128)(2,1)} %get-tuple-element.47.im_ref, ...), custom_call_target="tpu_custom_call" | custom-call | flops 125829120 | bytes 393216 | tf_op jit(solution)/shard_map/pallas_call | solution.py:401
  159.2 2.5 collective-permute-done
  169.0 11.1 %shard_map.177 = bf16[16,384,256]{2,1,0:T(8,128)(2,1)} custom-call(s32[1,3072]{1,0:T(1,128)} %reshape.59.ilane_ref, bf16[3072,512]{1,0:T(8,128)(2,1)} %get-tuple-element.55.d1_ref, bf16[256,512]{1,0:T(8,128)(2,1)} %w1u_ref.3, bf16[256,512]{1,0:T(8,128)(2,1)} %w1i_ref.3), custom_call_target="tpu_custom_call" | custom-call | flops 100663296 | bytes 98304 | tf_op jit(solution)/shard_map/pallas_call | solution.py:412
  183.4 2.7 %collective-permute-start.10 = (bf16[96,512]{1,0:T(8,128)(2,1)S(1)}, bf16[96,512]{1,0:T(8,128)(2,1)S(1)}, u32[]{:S(2)}, u32[]{:S(2)}) collective-permute-start(bf16[96,512]{1,0:T(8,128)(2,1)S(1)} %slice.80), channel_id=1, source_target_pairs={{0,16},{8,24},{16,0},{24,8},{32,48},{40,56},{48,32},{56,40},{64,80... | collective-permute-start | bytes 294920 | tf_op jit(solution)/shard_map/ppermute | solution.py:441
  189.1 2.7 %collective-permute-start.4 = (bf16[104,512]{1,0:T(8,128)(2,1)S(1)}, bf16[104,512]{1,0:T(8,128)(2,1)S(1)}, u32[]{:S(2)}, u32[]{:S(2)}) collective-permute-start(bf16[104,512]{1,0:T(8,128)(2,1)S(1)} %slice.79), channel_id=1, source_target_pairs={{0,64},{8,72},{16,80},{24,88},{32,96},{40,104},{48,112},{56,120},{... | collective-permute-start | bytes 319496 | tf_op jit(solution)/shard_map/ppermute | solution.py:441
  202.9 2.7 %collective-permute-done.8 = bf16[104,512]{1,0:T(8,128)(2,1)S(1)} collective-permute-done((bf16[104,512]{1,0:T(8,128)(2,1)S(1)}, bf16[104,512]{1,0:T(8,128)(2,1)S(1)}, u32[]{:S(2)}, u32[]{:S(2)}) %collective-permute-start.8) | collective-permute-done | bytes 106528 | tf_op jit(solution)/shard_map/ppermute | solution.py:441
  205.8 5.0 %all-to-all-start.3 = ((bf16[16,384,256]{2,1,0:T(8,128)(2,1)}), bf16[16,384,256]{2,1,0:T(8,128)(2,1)}, u32[]{:S(2)}, u32[]{:S(2)}) async-start(bf16[16,384,256]{2,1,0:T(8,128)(2,1)} %shard_map.177), calls=%async_computation.3 | async-start | bytes 6291456 | tf_op jit(solution)/shard_map/all_to_all | solution.py:328
  213.9 3.1 %collective-permute-done.18.refs_3_ = bf16[200,512]{1,0:T(8,128)(2,1)S(1)} collective-permute-done((bf16[200,512]{1,0:T(8,128)(2,1)S(1)}, bf16[200,512]{1,0:T(8,128)(2,1)S(1)}, u32[]{:S(2)}, u32[]{:S(2)}) %collective-permute-start.18) | collective-permute-done | bytes 204832 | tf_op jit(solution)/shard_map/ppermute | solution.py:437
  217.0 2.4 collective-permute-done.17.refs_2_
  223.8 3.4 %shard_map.179 = (f32[256,512]{1,0:T(8,128)}, f32[256,512]{1,0:T(8,128)}, f32[512,512]{1,0:T(8,128)}, f32[512,512]{1,0:T(8,128)}, f32[64,512]{1,0:T(8,128)}) custom-call(s32[1]{0:T(128)} %bitcast.6.me_ref, bf16[200,512]{1,0:T(8,128)(2,1)} %copy-done, bf16[200,512]{1,0:T(8,128)(2,1)} %copy-done.4, bf16[200,512]{1,0:T(8,128)(2,1)} %copy-done.3, ...), custom_call_target="tpu_custom_call" | custom-call | tf_op jit(solution)/shard_map/pallas_call | solution.py:482
  229.2 11.3 %shard_map.178 = (f32[2048,512]{1,0:T(8,128)}, f32[2048,512]{1,0:T(8,128)}) custom-call(s32[2,1,3072]{2,1,0:T(1,128)} %reshape.58.lane_ref, bf16[16,384,256]{2,1,0:T(8,128)(2,1)} %all-to-all-done.4.terms_ref), custom_call_target="tpu_custom_call" | custom-call | flops 100663296 | bytes 114688 | tf_op jit(solution)/shard_map/pallas_call | solution.py:425
  240.6 9.0 %all-to-all-done.3.terms_ref = bf16[16,384,256]{2,1,0:T(8,128)(2,1)} async-done(((bf16[16,384,256]{2,1,0:T(8,128)(2,1)}), bf16[16,384,256]{2,1,0:T(8,128)(2,1)}, u32[]{:S(2)}, u32[]{:S(2)}) %all-to-all-start.3) | async-done | bytes 3145760 | tf_op jit(solution)/shard_map/all_to_all | solution.py:328
  249.6 11.3 %shard_map.180 = (f32[2048,512]{1,0:T(8,128)}, f32[2048,512]{1,0:T(8,128)}) custom-call(s32[2,1,3072]{2,1,0:T(1,128)} %reshape.58.lane_ref, bf16[16,384,256]{2,1,0:T(8,128)(2,1)} %all-to-all-done.3.terms_ref, f32[2048,512]{1,0:T(8,128)} %get-tuple-element.68.rest_0_, f32[2048,512]{1,0:T(8,128)} %get-tuple-element.69.rest_1_), custom_call_target="tpu_custom_call", output_to_operand_aliasing={{0}: (2, {}), {1}: (3, {})} | custom-call | flops 100663296 | bytes 114688 | tf_op jit(solution)/shard_map/pallas_call | solution.py:425
  (86 shorter events, 37.7 us)
Async XLA Ops:
  31.7 45.6 %all-to-all-start.2 = ((bf16[16,384,256]{2,1,0:T(8,128)(2,1)}), bf16[16,384,256]{2,1,0:T(8,128)(2,1)}, u32[]{:S(2)}, u32[]{:S(2)}) async-start(bf16[16,384,256]{2,1,0:T(8,128)(2,1)} %shard_map.173), calls=%async_computation.2 | async-start | bytes 6291456 | tf_op jit(solution)/shard_map/all_to_all | solution.py:328
  77.3 41.9 %all-to-all-start.1 = ((bf16[16,384,256]{2,1,0:T(8,128)(2,1)}), bf16[16,384,256]{2,1,0:T(8,128)(2,1)}, u32[]{:S(2)}, u32[]{:S(2)}) async-start(bf16[16,384,256]{2,1,0:T(8,128)(2,1)} %shard_map.172), calls=%async_computation.1 | async-start | bytes 6291456 | tf_op jit(solution)/shard_map/all_to_all | solution.py:328
  137.5 68.3 %all-to-all-start.4 = ((bf16[16,384,256]{2,1,0:T(8,128)(2,1)}), bf16[16,384,256]{2,1,0:T(8,128)(2,1)}, u32[]{:S(2)}, u32[]{:S(2)}) async-start(bf16[16,384,256]{2,1,0:T(8,128)(2,1)} %get-tuple-element.61), calls=%async_computation.4 | async-start | bytes 6291456 | tf_op jit(solution)/shard_map/all_to_all | solution.py:328
  163.7 16.3 %collective-permute-start.1 = (bf16[200,512]{1,0:T(8,128)(2,1)}, bf16[200,512]{1,0:T(8,128)(2,1)}, u32[]{:S(2)}, u32[]{:S(2)}) collective-permute-start(bf16[200,512]{1,0:T(8,128)(2,1)} %get-tuple-element.77), channel_id=1, source_target_pairs={{0,2},{1,3},{2,4},{3,5},{4,6},{5,7},{6,0},{7,1},{8,10},{9,11},{10,... | collective-permute-start | bytes 614408 | tf_op jit(solution)/shard_map/ppermute | solution.py:437
  165.4 14.7 %collective-permute-start.3 = (bf16[200,512]{1,0:T(8,128)(2,1)}, bf16[200,512]{1,0:T(8,128)(2,1)}, u32[]{:S(2)}, u32[]{:S(2)}) collective-permute-start(bf16[200,512]{1,0:T(8,128)(2,1)} %get-tuple-element.78), channel_id=1, source_target_pairs={{0,6},{1,7},{2,0},{3,1},{4,2},{5,3},{6,4},{7,5},{8,14},{9,15},{10,... | collective-permute-start | bytes 614408 | tf_op jit(solution)/shard_map/ppermute | solution.py:437
  167.0 13.1 %collective-permute-start.2 = (bf16[200,512]{1,0:T(8,128)(2,1)}, bf16[200,512]{1,0:T(8,128)(2,1)}, u32[]{:S(2)}, u32[]{:S(2)}) collective-permute-start(bf16[200,512]{1,0:T(8,128)(2,1)} %get-tuple-element.79), channel_id=1, source_target_pairs={{0,4},{1,5},{2,6},{3,7},{4,0},{5,1},{6,2},{7,3},{8,12},{9,13},{10,... | collective-permute-start | bytes 614408 | tf_op jit(solution)/shard_map/ppermute | solution.py:437
  181.4 10.3 %collective-permute-start.11 = (bf16[96,512]{1,0:T(8,128)(2,1)S(1)}, bf16[96,512]{1,0:T(8,128)(2,1)S(1)}, u32[]{:S(2)}, u32[]{:S(2)}) collective-permute-start(bf16[96,512]{1,0:T(8,128)(2,1)S(1)} %slice.80), channel_id=1, source_target_pairs={{0,8},{8,16},{16,24},{24,0},{32,40},{40,48},{48,56},{56,32},{64,72... | collective-permute-start | bytes 294920 | tf_op jit(solution)/shard_map/ppermute | solution.py:441
  183.4 9.8 %collective-permute-start.10 = (bf16[96,512]{1,0:T(8,128)(2,1)S(1)}, bf16[96,512]{1,0:T(8,128)(2,1)S(1)}, u32[]{:S(2)}, u32[]{:S(2)}) collective-permute-start(bf16[96,512]{1,0:T(8,128)(2,1)S(1)} %slice.80), channel_id=1, source_target_pairs={{0,16},{8,24},{16,0},{24,8},{32,48},{40,56},{48,32},{56,40},{64,80... | collective-permute-start | bytes 294920 | tf_op jit(solution)/shard_map/ppermute | solution.py:441
  186.0 7.2 %collective-permute-start.12 = (bf16[96,512]{1,0:T(8,128)(2,1)S(1)}, bf16[96,512]{1,0:T(8,128)(2,1)S(1)}, u32[]{:S(2)}, u32[]{:S(2)}) collective-permute-start(bf16[96,512]{1,0:T(8,128)(2,1)S(1)} %slice.80), channel_id=1, source_target_pairs={{0,24},{8,0},{16,8},{24,16},{32,56},{40,32},{48,40},{56,48},{64,88... | collective-permute-start | bytes 294920 | tf_op jit(solution)/shard_map/ppermute | solution.py:441
  187.5 7.8 %collective-permute-start.5 = (bf16[104,512]{1,0:T(8,128)(2,1)S(1)}, bf16[104,512]{1,0:T(8,128)(2,1)S(1)}, u32[]{:S(2)}, u32[]{:S(2)}) collective-permute-start(bf16[104,512]{1,0:T(8,128)(2,1)S(1)} %slice.79), channel_id=1, source_target_pairs={{0,32},{8,40},{16,48},{24,56},{32,64},{40,72},{48,80},{56,88},{64,... | collective-permute-start | bytes 319496 | tf_op jit(solution)/shard_map/ppermute | solution.py:441
  189.1 7.4 %collective-permute-start.4 = (bf16[104,512]{1,0:T(8,128)(2,1)S(1)}, bf16[104,512]{1,0:T(8,128)(2,1)S(1)}, u32[]{:S(2)}, u32[]{:S(2)}) collective-permute-start(bf16[104,512]{1,0:T(8,128)(2,1)S(1)} %slice.79), channel_id=1, source_target_pairs={{0,64},{8,72},{16,80},{24,88},{32,96},{40,104},{48,112},{56,120},{... | collective-permute-start | bytes 319496 | tf_op jit(solution)/shard_map/ppermute | solution.py:441
  191.7 5.2 %collective-permute-start.6 = (bf16[104,512]{1,0:T(8,128)(2,1)S(1)}, bf16[104,512]{1,0:T(8,128)(2,1)S(1)}, u32[]{:S(2)}, u32[]{:S(2)}) collective-permute-start(bf16[104,512]{1,0:T(8,128)(2,1)S(1)} %slice.79), channel_id=1, source_target_pairs={{0,96},{8,104},{16,112},{24,120},{32,0},{40,8},{48,16},{56,24},{64... | collective-permute-start | bytes 319496 | tf_op jit(solution)/shard_map/ppermute | solution.py:441
  193.3 5.9 %collective-permute-start.15 = (bf16[96,512]{1,0:T(8,128)(2,1)S(1)}, bf16[96,512]{1,0:T(8,128)(2,1)S(1)}, u32[]{:S(2)}, u32[]{:S(2)}) collective-permute-start(bf16[96,512]{1,0:T(8,128)(2,1)S(1)} %add_convert_fusion.4), channel_id=1, source_target_pairs={{0,96},{8,104},{16,112},{24,120},{32,0},{40,8},{48,16},{56,24},{64... | collective-permute-start | bytes 294920 | tf_op jit(solution)/shard_map/ppermute | solution.py:441
  193.5 7.1 %collective-permute-start.14 = (bf16[96,512]{1,0:T(8,128)(2,1)S(1)}, bf16[96,512]{1,0:T(8,128)(2,1)S(1)}, u32[]{:S(2)}, u32[]{:S(2)}) collective-permute-start(bf16[96,512]{1,0:T(8,128)(2,1)S(1)} %add_convert_fusion.4), channel_id=1, source_target_pairs={{0,32},{8,40},{16,48},{24,56},{32,64},{40,72},{48,80},{56,88},{64,... | collective-permute-start | bytes 294920 | tf_op jit(solution)/shard_map/ppermute | solution.py:441
  195.4 6.1 %collective-permute-start.13 = (bf16[96,512]{1,0:T(8,128)(2,1)S(1)}, bf16[96,512]{1,0:T(8,128)(2,1)S(1)}, u32[]{:S(2)}, u32[]{:S(2)}) collective-permute-start(bf16[96,512]{1,0:T(8,128)(2,1)S(1)} %add_convert_fusion.4), channel_id=1, source_target_pairs={{0,64},{8,72},{16,80},{24,88},{32,96},{40,104},{48,112},{56,120},{... | collective-permute-start | bytes 294920 | tf_op jit(solution)/shard_map/ppermute | solution.py:441
  197.0 5.9 %collective-permute-start.9 = (bf16[104,512]{1,0:T(8,128)(2,1)S(1)}, bf16[104,512]{1,0:T(8,128)(2,1)S(1)}, u32[]{:S(2)}, u32[]{:S(2)}) collective-permute-start(bf16[104,512]{1,0:T(8,128)(2,1)S(1)} %add_convert_fusion.3), channel_id=1, source_target_pairs={{0,24},{8,0},{16,8},{24,16},{32,56},{40,32},{48,40},{56,48},{64,88... | collective-permute-start | bytes 319496 | tf_op jit(solution)/shard_map/ppermute | solution.py:441
  198.6 7.1 %collective-permute-start.8 = (bf16[104,512]{1,0:T(8,128)(2,1)S(1)}, bf16[104,512]{1,0:T(8,128)(2,1)S(1)}, u32[]{:S(2)}, u32[]{:S(2)}) collective-permute-start(bf16[104,512]{1,0:T(8,128)(2,1)S(1)} %add_convert_fusion.3), channel_id=1, source_target_pairs={{0,8},{8,16},{16,24},{24,0},{32,40},{40,48},{48,56},{56,32},{64,72... | collective-permute-start | bytes 319496 | tf_op jit(solution)/shard_map/ppermute | solution.py:441
  199.1 6.5 %collective-permute-start.7 = (bf16[104,512]{1,0:T(8,128)(2,1)S(1)}, bf16[104,512]{1,0:T(8,128)(2,1)S(1)}, u32[]{:S(2)}, u32[]{:S(2)}) collective-permute-start(bf16[104,512]{1,0:T(8,128)(2,1)S(1)} %add_convert_fusion.3), channel_id=1, source_target_pairs={{0,16},{8,24},{16,0},{24,8},{32,48},{40,56},{48,32},{56,40},{64,80... | collective-permute-start | bytes 319496 | tf_op jit(solution)/shard_map/ppermute | solution.py:441
  205.8 43.8 %all-to-all-start.3 = ((bf16[16,384,256]{2,1,0:T(8,128)(2,1)}), bf16[16,384,256]{2,1,0:T(8,128)(2,1)}, u32[]{:S(2)}, u32[]{:S(2)}) async-start(bf16[16,384,256]{2,1,0:T(8,128)(2,1)} %shard_map.177), calls=%async_computation.3 | async-start | bytes 6291456 | tf_op jit(solution)/shard_map/all_to_all | solution.py:328
  210.8 6.1 %collective-permute-start.18 = (bf16[200,512]{1,0:T(8,128)(2,1)S(1)}, bf16[200,512]{1,0:T(8,128)(2,1)S(1)}, u32[]{:S(2)}, u32[]{:S(2)}) collective-permute-start(bf16[200,512]{1,0:T(8,128)(2,1)S(1)} %pad_maximum_fusion.refs_0_), channel_id=1, source_target_pairs={{0,6},{1,7},{2,0},{3,1},{4,2},{5,3},{6,4},{7,5},{8,14},{9,15},{10,... | collective-permute-start | bytes 614408 | tf_op jit(solution)/shard_map/ppermute | solution.py:437
  212.0 7.4 %collective-permute-start.17 = (bf16[200,512]{1,0:T(8,128)(2,1)S(1)}, bf16[200,512]{1,0:T(8,128)(2,1)S(1)}, u32[]{:S(2)}, u32[]{:S(2)}) collective-permute-start(bf16[200,512]{1,0:T(8,128)(2,1)S(1)} %pad_maximum_fusion.refs_0_), channel_id=1, source_target_pairs={{0,4},{1,5},{2,6},{3,7},{4,0},{5,1},{6,2},{7,3},{8,12},{9,13},{10,... | collective-permute-start | bytes 614408 | tf_op jit(solution)/shard_map/ppermute | solution.py:437
  213.7 7.8 %collective-permute-start.16 = (bf16[200,512]{1,0:T(8,128)(2,1)S(1)}, bf16[200,512]{1,0:T(8,128)(2,1)S(1)}, u32[]{:S(2)}, u32[]{:S(2)}) collective-permute-start(bf16[200,512]{1,0:T(8,128)(2,1)S(1)} %pad_maximum_fusion.refs_0_), channel_id=1, source_target_pairs={{0,2},{1,3},{2,4},{3,5},{4,6},{5,7},{6,0},{7,1},{8,10},{9,11},{10,... | collective-permute-start | bytes 614408 | tf_op jit(solution)/shard_map/ppermute | solution.py:437
  213.9 8.4 %collective-permute-start.19 = (bf16[200,512]{1,0:T(8,128)(2,1)S(1)}, bf16[200,512]{1,0:T(8,128)(2,1)S(1)}, u32[]{:S(2)}, u32[]{:S(2)}) collective-permute-start(bf16[200,512]{1,0:T(8,128)(2,1)S(1)} %pad_maximum_fusion.refs_0_), channel_id=1, source_target_pairs={{0,1},{1,0},{2,3},{3,2},{4,5},{5,4},{6,7},{7,6},{8,9},{9,8},{10,11... | collective-permute-start | bytes 614408 | tf_op jit(solution)/shard_map/ppermute | solution.py:455
  217.0 5.4 %collective-permute-start.22 = (bf16[200,512]{1,0:T(8,128)(2,1)S(1)}, bf16[200,512]{1,0:T(8,128)(2,1)S(1)}, u32[]{:S(2)}, u32[]{:S(2)}) collective-permute-start(bf16[200,512]{1,0:T(8,128)(2,1)S(1)} %collective-permute-done.18.refs_3_), channel_id=1, source_target_pairs={{0,1},{1,0},{2,3},{3,2},{4,5},{5,4},{6,7},{7,6},{8,9},{9,8},{10,11... | collective-permute-start | bytes 614408 | tf_op jit(solution)/shard_map/ppermute | solution.py:455
  (14 other events, 158.4 us)

commit v4 on v3

--- a/solution.py
+++ b/solution.py
@@ -169,44 +169,41 @@
 
 
 def middle_kernel(
-    icol_ref, fcol_ref, ilane_ref, ug_ref, ig_ref, deep_ref, wo_ref,
-    out_ref, delta_out, go_out, gi_scr,
+    icol_ref, fcol_ref, ug_ref, ig_ref, deep_ref, wo_ref, gu_out, gi_out, delta_out, go_out
 ):
     step = pl.program_id(0)
-    groups = pl.num_programs(0) // 2
     peers, cap, _ = ug_ref.shape
     m = peers * cap
     slots = ig_ref.shape[0] * cap
-
-    @pl.when(step < groups)
-    def _():
-        ug = ug_ref[...].reshape(m, D).astype(F32)
-        sel = pick_rows(column(icol_ref[...], step), slots)
-        ig = dot_nn(sel, ig_ref[...].reshape(slots, D))
-        wg = wo_ref[:, :D]
-        prod = ug * ig
-        logit = jnp.sum(prod * wg, axis=1, keepdims=True) + deep_ref[:, 0:1]
-        flag = column(fcol_ref[...], step)
-        delta = sigmoid(logit) - (flag - 1).astype(F32)
-        delta = jnp.where(flag > 0, delta, 0.0)
-        delta_out[...] = jnp.broadcast_to(delta, delta_out.shape)
-        dw = delta * wg
-        out_ref[...] = (dw * ig).astype(BF).reshape(peers, cap, D)
-        gi_scr[pl.ds(pl.multiple_of(step * m, m), m), :] = (dw * ug).astype(BF)
-        part = jnp.sum(delta * prod, axis=0, keepdims=True)
-
-        @pl.when(step == 0)
-        def _():
-            go_out[...] = part
-
-        @pl.when(step > 0)
-        def _():
-            go_out[...] += part
-
-    @pl.when(step >= groups)
-    def _():
-        sel = put_rows(ilane_ref[...], (step - groups) * m, m)
-        out_ref[...] = dot_nn(sel, gi_scr[...]).astype(BF).reshape(peers, cap, D)
+    ug = ug_ref[...].reshape(m, D).astype(F32)
+    sel = pick_rows(column(icol_ref[...], step), slots)
+    ig = dot_nn(sel, ig_ref[...].reshape(slots, D))
+    wg = wo_ref[:, :D]
+    prod = ug * ig
+    logit = jnp.sum(prod * wg, axis=1, keepdims=True) + deep_ref[:, 0:1]
+    flag = column(fcol_ref[...], step)
+    delta = sigmoid(logit) - (flag - 1).astype(F32)
+    delta = jnp.where(flag > 0, delta, 0.0)
+    delta_out[...] = jnp.broadcast_to(delta, delta_out.shape)
+    dw = delta * wg
+    gu_out[...] = (dw * ig).astype(BF).reshape(peers, cap, D)
+    gi_out[...] = (dw * ug).astype(BF)
+    part = jnp.sum(delta * prod, axis=0, keepdims=True)
+
+    @pl.when(step == 0)
+    def _():
+        go_out[...] = part
+
+    @pl.when(step > 0)
+    def _():
+        go_out[...] += part
+
+
+def place_kernel(ilane_ref, g_ref, out_ref):
+    peers, cap, _ = out_ref.shape
+    m = peers * cap
+    sel = put_rows(ilane_ref[...], pl.program_id(0) * m, m)
+    out_ref[...] = dot_nn(sel, g_ref[...]).astype(BF).reshape(peers, cap, D)
 
 
 def backward_kernel(
@@ -279,22 +276,21 @@
             at += count
 
 
-def gather_add_kernel(lane_ref, terms_ref, *rest):
+def gather_add_kernel(lane_ref, user_ref, item_ref, *rest):
     user_out, item_out = rest[-2:]
     step = pl.program_id(0)
     steps = pl.num_programs(0) // 2
     m = user_out.shape[0]
-    slots = terms_ref.shape[0] * terms_ref.shape[1]
+    slots = user_ref.shape[0] * user_ref.shape[1]
     sel = put_rows(lane_ref[0], step % steps * m, m)
-    got = dot_nn(sel, terms_ref[...].reshape(slots, D))
 
     @pl.when(step < steps)
     def _():
-        user_out[...] = got
+        user_out[...] = dot_nn(sel, user_ref[...].reshape(slots, D))
 
     @pl.when(step >= steps)
     def _():
-        item_out[...] = got
+        item_out[...] = dot_nn(sel, item_ref[...].reshape(slots, D))
 
 
 def whole(shape):
@@ -375,22 +371,24 @@
     )(icol, mlp_back, mlp_back, w1_user, w1_item, w2_weight, w3_weight, wo)
 
     last = groups - 1
-    gmf_out, delta, go = call(
-        middle_kernel, (2 * groups,),
-        [
-            whole((m, groups)), whole((m, groups)), whole((1, slots)),
-            pl.BlockSpec((peers, cap, D), lambda i: (jnp.minimum(i, last), 0, 0)), all_items,
-            pl.BlockSpec((m, 128), lambda i: (jnp.minimum(i, last), 0)), whole((1, D + hid)),
-        ],
-        [
-            pl.BlockSpec((peers, cap, D), lambda i: (i % groups, i // groups, 0)),
-            pl.BlockSpec((m, 128), lambda i: (jnp.minimum(i, last), 0)), whole((1, D)),
-        ],
-        [buffer, jax.ShapeDtypeStruct((slots, 128), F32), jax.ShapeDtypeStruct((1, D), F32)],
-        scratch=[pltpu.VMEM((slots, D), BF)], flops=2 * pick, moved=12 * slots * D,
-    )(icol, fcol, ilane, gmf_back, gmf_back, deep, wo)
-
-    gmf_terms = exchange(gmf_out)
+    single = jax.ShapeDtypeStruct((owners, cap, D), BF)
+    gu_out, gi, delta, go = call(
+        middle_kernel, (groups,),
+        [whole((m, groups)), whole((m, groups)), user_block, all_items, thin, whole((1, D + hid))],
+        [user_block, narrow, thin, whole((1, D))],
+        [single, jax.ShapeDtypeStruct((slots, D), BF), jax.ShapeDtypeStruct((slots, 128), F32),
+         jax.ShapeDtypeStruct((1, D), F32)],
+        flops=pick, moved=12 * slots * D,
+    )(icol, fcol, gmf_back, gmf_back, deep, wo)
+
+    gu_terms = exchange(gu_out)
+    gi_out = call(
+        place_kernel, (groups,), [whole((1, slots)), whole((slots, D))], user_block, single,
+        flops=pick, moved=4 * slots * D,
+    )(ilane, gi)
+    gi_out, gu_terms = lax.optimization_barrier((gi_out, gu_terms))
+    gi_terms = exchange(gi_out)
+    last = groups - 1
 
     me = lax.axis_index("dp").astype(I32).reshape(1)
     n_dp = lax.axis_size("dp")
@@ -418,20 +416,20 @@
         moved=4 * slots * hid,
     )(ilane, d1, w1_user, w1_item)
 
-    def gather_add(terms, half, *into):
+    def gather_add(user_terms, item_terms, at, half, *into):
         steps = 4
         r = rows // steps
         grad = jax.ShapeDtypeStruct((rows, 2 * D), F32)
         return call(
             gather_add_kernel, (2 * steps,),
             [pl.BlockSpec((1, 1, slots), lambda i: (i // steps, 0, 0)),
-             pl.BlockSpec((owners, cap, D), lambda i: (0, i // steps, 0))]
+             whole((owners, cap, D)), pl.BlockSpec((owners, cap, D), lambda i: (0, at, 0))]
             + [pl.BlockSpec(memory_space=pl.ANY)] * len(into),
             [pl.BlockSpec((r, D), lambda i: (jnp.minimum(i, steps - 1), half)),
              pl.BlockSpec((r, D), lambda i: (jnp.maximum(i - steps, 0), half))],
-            [grad, grad], aliases={2 + k: k for k in range(len(into))},
+            [grad, grad], aliases={3 + k: k for k in range(len(into))},
             flops=4 * rows * slots * D, moved=4 * slots * D + 8 * rows * D,
-        )(wlane, terms, *into)
+        )(wlane, user_terms, item_terms, *into)
 
     def shift_dp(x, k):
         return lax.ppermute(x, "dp", [(s, (s + k) % n_dp) for s in range(n_dp)])
@@ -476,7 +474,7 @@
     mlp_out, top, low = lax.optimization_barrier((mlp_out, top, low))
     mlp_terms = exchange(mlp_out)
     part = jnp.concatenate([top, low]).astype(BF)
-    user_grad, item_grad = gather_add(gmf_terms, 0)
+    user_grad, item_grad = gather_add(gu_terms, gi_terms, 0, 0)
     found = [part] + [shift_dp(part, 2 * j) for j in range(1, 4)]
     found = found + [swap_core(v) for v in found]
     gw1u, gw1i, gw2, gw3, gwo = pl.pallas_call(
@@ -490,7 +488,7 @@
     mlp_terms, user_grad, item_grad, grad_out = lax.optimization_barrier(
         (mlp_terms, user_grad, item_grad, grad_out)
     )
-    user_grad, item_grad = gather_add(mlp_terms, 1, user_grad, item_grad)
+    user_grad, item_grad = gather_add(mlp_terms, mlp_terms, 1, 1, user_grad, item_grad)
     return user_grad[None], item_grad[None], gw1u, gw1i, gw2, gw3, grad_out
 
 

time: 262 us -> 276 us (1.053)
  starting transfers between devices: 47.5 us -> 58.2 us
    all_to_all x4 -> x5, starting transfers between devices: 20.7 us -> 30.6 us  [exchange(): return lax.all_to_all(x, 'emb', split_axis=0, concat_axis=0, tiled=True)]
    pallas_call x1 -> x2, Pallas kernels: 18.3 us -> 20.1 us  [the longest x1 12.3 us: body(): call(middle_kernel, (groups,), [whole((m, groups)), whole((m, groups)), u...]
    all_to_all x4 -> x5, waiting for transfers between devices: 47.6 us -> 47.3 us  [exchange(): return lax.all_to_all(x, 'emb', split_axis=0, concat_axis=0, tiled=True)]
  transfers between devices with their start and end apart: 27 -> 28, of which waited for: 11 -> 12; matrix products, arithmetic and copies ran while one was open for 4% -> 4% of each run, Pallas kernels for 30% -> 31%
where the time goes in v4:
time: 276 us; the launch traced here: 275 us
  Pallas kernels  124 us (45%)
  waiting for transfers between devices  64.5 us (23%)
  starting transfers between devices  58.2 us (21%)
  blocking collectives  15.7 us (6%)
  local copies, waits for them, and re-layouts  6.88 us (2%)
  other arithmetic  4.32 us (2%)
    all_to_all x5, waiting for transfers between devices, exchange(): return lax.all_to_all(x, 'emb', split_axis=0, concat_axis=0, tiled=True)  47.3 us
    all_to_all x5, starting transfers between devices, exchange(): return lax.all_to_all(x, 'emb', split_axis=0, concat_axis=0, tiled=True)  30.6 us
    pallas_call x1, Pallas kernels, body(): call(forward_kernel, (groups,), [whole((m, groups)), user_block, all_item...  25.3 us
    pallas_call x2, Pallas kernels, gather_add(): call(gather_add_kernel, (2 * steps,), [pl.BlockSpec((1, 1, slots), lambda...  23 us
    pallas_call x2, Pallas kernels, fetch(): call(fetch_kernel, (groups,), [whole((owners, 1, 512)), table, table], pl...  22.1 us
    ppermute x12, starting transfers between devices, shift_emb(): lax.ppermute(x, 'emb', [(a * side + b, (a + kx) % side * side + (b + kz)...  19.5 us
    all_to_all x1, blocking collectives, exchange(): return lax.all_to_all(x, 'emb', split_axis=0, concat_axis=0, tiled=True)  15.7 us
    pallas_call x1, Pallas kernels, body(): call(backward_kernel, (fine,), [scalar, pl.BlockSpec((slots // fine, 128)...  15.2 us
  transfers between devices with their start and end apart: 28, of which 12 were waited for; matrix products, arithmetic and copies ran while one was open for 4% of the time, Pallas kernels for 31%

profile of v4, /device:TPU:0, one launch (start us, length us, event | category | flops | bytes accessed | tf_op | source)
XLA Modules:
  0.0 274.8 jit_solution(1271733261146926549)
XLA Ops:
  0.6 4.3 %shard_map.171 = (s32[16,1,512]{2,1,0:T(1,128)}, s32[16,256]{1,0:T(8,128)}, s32[2,256,16]{2,1,0:T(8,128)}) custom-call(s32[16,128]{1,0:T(8,128)} %bitcast.29, s32[16,128]{1,0:T(8,128)} %bitcast.30, s32[16,128]{1,0:T(8,128)} %bitcast.31, s32[16,128]{1,0:T(8,128)} %bitcast.32, s32[16,128]{1,0:T(8,128)} %bitcast.33), custom_call_target="tpu_custom_call" | custom-call | tf_op jit(solution)/shard_map/pallas_call | solution.py:326
  4.9 15.7 %all_to_all.30.asked_ref = s32[16,1,512]{2,1,0:T(1,128)} all-to-all(s32[16,1,512]{2,1,0:T(1,128)} %get-tuple-element.45), channel_id=1, replica_groups=mesh['emb'=16,'dp'=8] {'emb'}, dimensions={0} | all-to-all | bytes 65536 | tf_op jit(solution)/shard_map/all_to_all | solution.py:324
  20.6 11.1 %shard_map.173 = bf16[16,384,256]{2,1,0:T(8,128)(2,1)} custom-call(s32[16,1,512]{2,1,0:T(1,128)} %all_to_all.30.asked_ref, bf16[2048,512]{1,0:T(8,128)(2,1)} %ut_ref.3, bf16[2048,512]{1,0:T(8,128)(2,1)} %it_ref.3), custom_call_target="tpu_custom_call" | custom-call | flops 100663296 | bytes 81920 | tf_op jit(solution)/shard_map/pallas_call | solution.py:356
  31.7 4.5 %all-to-all-start.2 = ((bf16[16,384,256]{2,1,0:T(8,128)(2,1)}), bf16[16,384,256]{2,1,0:T(8,128)(2,1)}, u32[]{:S(2)}, u32[]{:S(2)}) async-start(bf16[16,384,256]{2,1,0:T(8,128)(2,1)} %shard_map.173), calls=%async_computation.2 | async-start | bytes 6291456 | tf_op jit(solution)/shard_map/all_to_all | solution.py:324
  36.2 11.1 %shard_map.172 = bf16[16,384,256]{2,1,0:T(8,128)(2,1)} custom-call(s32[16,1,512]{2,1,0:T(1,128)} %all_to_all.30.asked_ref, bf16[2048,512]{1,0:T(8,128)(2,1)} %ut_ref.3, bf16[2048,512]{1,0:T(8,128)(2,1)} %it_ref.3), custom_call_target="tpu_custom_call" | custom-call | flops 100663296 | bytes 81920 | tf_op jit(solution)/shard_map/pallas_call | solution.py:356
  47.3 30.4 %all-to-all-done.2.um_ref.im_ref = bf16[16,384,256]{2,1,0:T(8,128)(2,1)} async-done(((bf16[16,384,256]{2,1,0:T(8,128)(2,1)}), bf16[16,384,256]{2,1,0:T(8,128)(2,1)}, u32[]{:S(2)}, u32[]{:S(2)}) %all-to-all-start.2) | async-done | bytes 3145760 | tf_op jit(solution)/shard_map/all_to_all | solution.py:324
  77.7 4.7 %all-to-all-start.1 = ((bf16[16,384,256]{2,1,0:T(8,128)(2,1)}), bf16[16,384,256]{2,1,0:T(8,128)(2,1)}, u32[]{:S(2)}, u32[]{:S(2)}) async-start(bf16[16,384,256]{2,1,0:T(8,128)(2,1)} %shard_map.172), calls=%async_computation.1 | async-start | bytes 6291456 | tf_op jit(solution)/shard_map/all_to_all | solution.py:324
  85.0 25.3 %shard_map.174 = (bf16[3072,256]{1,0:T(8,128)(2,1)}, bf16[3072,512]{1,0:T(8,128)(2,1)}, bf16[3072,512]{1,0:T(8,128)(2,1)}, bf16[3072,512]{1,0:T(8,128)(2,1)}, bf...) custom-call(s32[768,4]{1,0:T(8,128)} %bitcast.22, ...), custom_call_target="tpu_custom_call" | custom-call | flops 150994944 | bytes 393216 | tf_op jit(solution)/shard_map/pallas_call | solution.py:365
  110.3 9.2 %all-to-all-done.1.ug_ref.ig_ref = bf16[16,384,256]{2,1,0:T(8,128)(2,1)} async-done(((bf16[16,384,256]{2,1,0:T(8,128)(2,1)}), bf16[16,384,256]{2,1,0:T(8,128)(2,1)}, u32[]{:S(2)}, u32[]{:S(2)}) %all-to-all-start.1) | async-done | bytes 3145760 | tf_op jit(solution)/shard_map/all_to_all | solution.py:324
  119.5 12.3 %shard_map.175 = (bf16[16,192,256]{2,1,0:T(8,128)(2,1)}, bf16[3072,256]{1,0:T(8,128)(2,1)}, f32[3072,128]{1,0:T(8,128)}, f32[1,256]{1,0:T(1,128)}) custom-call(s32[768,4]{1,0:T(8,128)} %bitcast.23, s32[768,4]{1,0:T(8,128)} %bitcast.24, bf16[16,384,256]{2,1,0:T(8,128)(2,1)} %all-to-all-done.1.ug_ref.ig_ref, ...), custom_call_target="tpu_custom_call" | custom-call | flops 75497472 | bytes 147456 | tf_op jit(solution)/shard_map/pallas_call | solution.py:375
  131.8 6.5 %all-to-all-start.4 = ((bf16[16,192,256]{2,1,0:T(8,128)(2,1)}), bf16[16,192,256]{2,1,0:T(8,128)(2,1)}, u32[]{:S(2)}, u32[]{:S(2)}) async-start(bf16[16,192,256]{2,1,0:T(8,128)(2,1)} %get-tuple-element.65), calls=%async_computation.4 | async-start | bytes 3145728 | tf_op jit(solution)/shard_map/all_to_all | solution.py:324
  138.3 15.2 %shard_map.176 = (bf16[3072,512]{1,0:T(8,128)(2,1)}, bf16[800,512]{1,0:T(8,128)(2,1)}, bf16[800,512]{1,0:T(8,128)(2,1)}) custom-call(s32[1]{0:T(128)} %bitcast.6.me_ref, f32[3072,128]{1,0:T(8,128)} %get-tuple-element.49.delta_ref, bf16[16,384,256]{2,1,0:T(8,128)(2,1)} %all-to-all-done.2.um_ref.im_ref, bf16[3072,256]{1,0:T(8,128)(2,1)} %get-tuple-element.50.im_ref, ...), custom_call_target="tpu_custom_call" | custom-call | flops 125829120 | bytes 393216 | tf_op jit(solution)/shard_map/pallas_call | solution.py:399
  164.0 7.7 %shard_map.178 = bf16[16,192,256]{2,1,0:T(8,128)(2,1)} custom-call(s32[1,3072]{1,0:T(1,128)} %reshape.59.ilane_ref, bf16[3072,256]{1,0:T(8,128)(2,1)} %get-tuple-element.64.g_ref), custom_call_target="tpu_custom_call" | custom-call | flops 75497472 | bytes 49152 | tf_op jit(solution)/shard_map/pallas_call | solution.py:385
  171.8 7.2 %all-to-all-start.5 = ((bf16[16,192,256]{2,1,0:T(8,128)(2,1)}), bf16[16,192,256]{2,1,0:T(8,128)(2,1)}, u32[]{:S(2)}, u32[]{:S(2)}) async-start(bf16[16,192,256]{2,1,0:T(8,128)(2,1)} %shard_map.178), calls=%async_computation.5 | async-start | bytes 3145728 | tf_op jit(solution)/shard_map/all_to_all | solution.py:324
  179.0 11.1 %shard_map.177 = bf16[16,384,256]{2,1,0:T(8,128)(2,1)} custom-call(s32[1,3072]{1,0:T(1,128)} %reshape.59.ilane_ref, bf16[3072,512]{1,0:T(8,128)(2,1)} %get-tuple-element.58.d1_ref, bf16[256,512]{1,0:T(8,128)(2,1)} %w1u_ref.3, bf16[256,512]{1,0:T(8,128)(2,1)} %w1i_ref.3), custom_call_target="tpu_custom_call" | custom-call | flops 100663296 | bytes 98304 | tf_op jit(solution)/shard_map/pallas_call | solution.py:410
  193.4 2.7 collective-permute-start.10
  199.1 2.7 collective-permute-start.4
  203.5 2.9 %collective-permute-done.10 = bf16[96,512]{1,0:T(8,128)(2,1)S(1)} collective-permute-done((bf16[96,512]{1,0:T(8,128)(2,1)S(1)}, bf16[96,512]{1,0:T(8,128)(2,1)S(1)}, u32[]{:S(2)}, u32[]{:S(2)}) %collective-permute-start.10) | collective-permute-done | bytes 98336 | tf_op jit(solution)/shard_map/ppermute | solution.py:439
  218.2 7.7 %all-to-all-start.3 = ((bf16[16,384,256]{2,1,0:T(8,128)(2,1)}), bf16[16,384,256]{2,1,0:T(8,128)(2,1)}, u32[]{:S(2)}, u32[]{:S(2)}) async-start(bf16[16,384,256]{2,1,0:T(8,128)(2,1)} %shard_map.177), calls=%async_computation.3 | async-start | bytes 6291456 | tf_op jit(solution)/shard_map/all_to_all | solution.py:324
  228.7 3.0 %collective-permute-done.18.refs_3_ = bf16[200,512]{1,0:T(8,128)(2,1)S(1)} collective-permute-done((bf16[200,512]{1,0:T(8,128)(2,1)S(1)}, bf16[200,512]{1,0:T(8,128)(2,1)S(1)}, u32[]{:S(2)}, u32[]{:S(2)}) %collective-permute-start.18) | collective-permute-done | bytes 204832 | tf_op jit(solution)/shard_map/ppermute | solution.py:435
  238.7 3.4 %shard_map.180 = (f32[256,512]{1,0:T(8,128)}, f32[256,512]{1,0:T(8,128)}, f32[512,512]{1,0:T(8,128)}, f32[512,512]{1,0:T(8,128)}, f32[64,512]{1,0:T(8,128)}) custom-call(s32[1]{0:T(128)} %bitcast.6.me_ref, bf16[200,512]{1,0:T(8,128)(2,1)} %copy-done, bf16[200,512]{1,0:T(8,128)(2,1)} %copy-done.4, bf16[200,512]{1,0:T(8,128)(2,1)} %copy-done.3, ...), custom_call_target="tpu_custom_call" | custom-call | tf_op jit(solution)/shard_map/pallas_call | solution.py:480
  244.1 11.4 %shard_map.179 = (f32[2048,512]{1,0:T(8,128)}, f32[2048,512]{1,0:T(8,128)}) custom-call(s32[2,1,3072]{2,1,0:T(1,128)} %reshape.58.lane_ref, bf16[16,192,256]{2,1,0:T(8,128)(2,1)} %all-to-all-done.4.user_ref, bf16[16,192,256]{2,1,0:T(8,128)(2,1)} %all-to-all-done.5.item_ref), custom_call_target="tpu_custom_call" | custom-call | flops 100663296 | bytes 114688 | tf_op jit(solution)/shard_map/pallas_call | solution.py:423
  255.6 7.7 %all-to-all-done.3.user_ref.item_ref = bf16[16,384,256]{2,1,0:T(8,128)(2,1)} async-done(((bf16[16,384,256]{2,1,0:T(8,128)(2,1)}), bf16[16,384,256]{2,1,0:T(8,128)(2,1)}, u32[]{:S(2)}, u32[]{:S(2)}) %all-to-all-start.3) | async-done | bytes 3145760 | tf_op jit(solution)/shard_map/all_to_all | solution.py:324
  263.3 11.5 %shard_map.181 = (f32[2048,512]{1,0:T(8,128)}, f32[2048,512]{1,0:T(8,128)}) custom-call(s32[2,1,3072]{2,1,0:T(1,128)} %reshape.58.lane_ref, bf16[16,384,256]{2,1,0:T(8,128)(2,1)} %all-to-all-done.3.user_ref.item_ref, bf16[16,384,256]{2,1,0:T(8,128)(2,1)} %all-to-all-done.3.user_ref.item_ref, ...), custom_call_target="tpu_custom_call", output_to_operand_aliasing={{0}: (3, {}), {1}: (4, {})} | custom-call | flops 100663296 | bytes 114688 | tf_op jit(solution)/shard_map/pallas_call | solution.py:423
  (89 shorter events, 44.8 us)
Async XLA Ops:
  31.7 46.0 %all-to-all-start.2 = ((bf16[16,384,256]{2,1,0:T(8,128)(2,1)}), bf16[16,384,256]{2,1,0:T(8,128)(2,1)}, u32[]{:S(2)}, u32[]{:S(2)}) async-start(bf16[16,384,256]{2,1,0:T(8,128)(2,1)} %shard_map.173), calls=%async_computation.2 | async-start | bytes 6291456 | tf_op jit(solution)/shard_map/all_to_all | solution.py:324
  77.7 41.8 %all-to-all-start.1 = ((bf16[16,384,256]{2,1,0:T(8,128)(2,1)}), bf16[16,384,256]{2,1,0:T(8,128)(2,1)}, u32[]{:S(2)}, u32[]{:S(2)}) async-start(bf16[16,384,256]{2,1,0:T(8,128)(2,1)} %shard_map.172), calls=%async_computation.1 | async-start | bytes 6291456 | tf_op jit(solution)/shard_map/all_to_all | solution.py:324
  131.8 40.0 %all-to-all-start.4 = ((bf16[16,192,256]{2,1,0:T(8,128)(2,1)}), bf16[16,192,256]{2,1,0:T(8,128)(2,1)}, u32[]{:S(2)}, u32[]{:S(2)}) async-start(bf16[16,192,256]{2,1,0:T(8,128)(2,1)} %get-tuple-element.65), calls=%async_computation.4 | async-start | bytes 3145728 | tf_op jit(solution)/shard_map/all_to_all | solution.py:324
  158.1 31.9 %collective-permute-start.1 = (bf16[200,512]{1,0:T(8,128)(2,1)}, bf16[200,512]{1,0:T(8,128)(2,1)}, u32[]{:S(2)}, u32[]{:S(2)}) collective-permute-start(bf16[200,512]{1,0:T(8,128)(2,1)} %get-tuple-element.83), channel_id=1, source_target_pairs={{0,2},{1,3},{2,4},{3,5},{4,6},{5,7},{6,0},{7,1},{8,10},{9,11},{10,... | collective-permute-start | bytes 614408 | tf_op jit(solution)/shard_map/ppermute | solution.py:435
  159.7 30.4 %collective-permute-start.3 = (bf16[200,512]{1,0:T(8,128)(2,1)}, bf16[200,512]{1,0:T(8,128)(2,1)}, u32[]{:S(2)}, u32[]{:S(2)}) collective-permute-start(bf16[200,512]{1,0:T(8,128)(2,1)} %get-tuple-element.84), channel_id=1, source_target_pairs={{0,6},{1,7},{2,0},{3,1},{4,2},{5,3},{6,4},{7,5},{8,14},{9,15},{10,... | collective-permute-start | bytes 614408 | tf_op jit(solution)/shard_map/ppermute | solution.py:435
  161.3 28.7 %collective-permute-start.2 = (bf16[200,512]{1,0:T(8,128)(2,1)}, bf16[200,512]{1,0:T(8,128)(2,1)}, u32[]{:S(2)}, u32[]{:S(2)}) collective-permute-start(bf16[200,512]{1,0:T(8,128)(2,1)} %get-tuple-element.85), channel_id=1, source_target_pairs={{0,4},{1,5},{2,6},{3,7},{4,0},{5,1},{6,2},{7,3},{8,12},{9,13},{10,... | collective-permute-start | bytes 614408 | tf_op jit(solution)/shard_map/ppermute | solution.py:435
  171.8 46.4 %all-to-all-start.5 = ((bf16[16,192,256]{2,1,0:T(8,128)(2,1)}), bf16[16,192,256]{2,1,0:T(8,128)(2,1)}, u32[]{:S(2)}, u32[]{:S(2)}) async-start(bf16[16,192,256]{2,1,0:T(8,128)(2,1)} %shard_map.178), calls=%async_computation.5 | async-start | bytes 3145728 | tf_op jit(solution)/shard_map/all_to_all | solution.py:324
  191.4 10.3 %collective-permute-start.11 = (bf16[96,512]{1,0:T(8,128)(2,1)S(1)}, bf16[96,512]{1,0:T(8,128)(2,1)S(1)}, u32[]{:S(2)}, u32[]{:S(2)}) collective-permute-start(bf16[96,512]{1,0:T(8,128)(2,1)S(1)} %slice.80), channel_id=1, source_target_pairs={{0,8},{8,16},{16,24},{24,0},{32,40},{40,48},{48,56},{56,32},{64,72... | collective-permute-start | bytes 294920 | tf_op jit(solution)/shard_map/ppermute | solution.py:439
  193.4 13.0 %collective-permute-start.10 = (bf16[96,512]{1,0:T(8,128)(2,1)S(1)}, bf16[96,512]{1,0:T(8,128)(2,1)S(1)}, u32[]{:S(2)}, u32[]{:S(2)}) collective-permute-start(bf16[96,512]{1,0:T(8,128)(2,1)S(1)} %slice.80), channel_id=1, source_target_pairs={{0,16},{8,24},{16,0},{24,8},{32,48},{40,56},{48,32},{56,40},{64,80... | collective-permute-start | bytes 294920 | tf_op jit(solution)/shard_map/ppermute | solution.py:439
  196.0 10.3 %collective-permute-start.12 = (bf16[96,512]{1,0:T(8,128)(2,1)S(1)}, bf16[96,512]{1,0:T(8,128)(2,1)S(1)}, u32[]{:S(2)}, u32[]{:S(2)}) collective-permute-start(bf16[96,512]{1,0:T(8,128)(2,1)S(1)} %slice.80), channel_id=1, source_target_pairs={{0,24},{8,0},{16,8},{24,16},{32,56},{40,32},{48,40},{56,48},{64,88... | collective-permute-start | bytes 294920 | tf_op jit(solution)/shard_map/ppermute | solution.py:439
  197.5 11.0 %collective-permute-start.5 = (bf16[104,512]{1,0:T(8,128)(2,1)S(1)}, bf16[104,512]{1,0:T(8,128)(2,1)S(1)}, u32[]{:S(2)}, u32[]{:S(2)}) collective-permute-start(bf16[104,512]{1,0:T(8,128)(2,1)S(1)} %slice.79), channel_id=1, source_target_pairs={{0,32},{8,40},{16,48},{24,56},{32,64},{40,72},{48,80},{56,88},{64,... | collective-permute-start | bytes 319496 | tf_op jit(solution)/shard_map/ppermute | solution.py:439
  199.1 10.6 %collective-permute-start.4 = (bf16[104,512]{1,0:T(8,128)(2,1)S(1)}, bf16[104,512]{1,0:T(8,128)(2,1)S(1)}, u32[]{:S(2)}, u32[]{:S(2)}) collective-permute-start(bf16[104,512]{1,0:T(8,128)(2,1)S(1)} %slice.79), channel_id=1, source_target_pairs={{0,64},{8,72},{16,80},{24,88},{32,96},{40,104},{48,112},{56,120},{... | collective-permute-start | bytes 319496 | tf_op jit(solution)/shard_map/ppermute | solution.py:439
  201.7 8.0 %collective-permute-start.6 = (bf16[104,512]{1,0:T(8,128)(2,1)S(1)}, bf16[104,512]{1,0:T(8,128)(2,1)S(1)}, u32[]{:S(2)}, u32[]{:S(2)}) collective-permute-start(bf16[104,512]{1,0:T(8,128)(2,1)S(1)} %slice.79), channel_id=1, source_target_pairs={{0,96},{8,104},{16,112},{24,120},{32,0},{40,8},{48,16},{56,24},{64... | collective-permute-start | bytes 319496 | tf_op jit(solution)/shard_map/ppermute | solution.py:439
  207.2 7.9 %collective-permute-start.14 = (bf16[96,512]{1,0:T(8,128)(2,1)S(1)}, bf16[96,512]{1,0:T(8,128)(2,1)S(1)}, u32[]{:S(2)}, u32[]{:S(2)}) collective-permute-start(bf16[96,512]{1,0:T(8,128)(2,1)S(1)} %add_convert_fusion.4), channel_id=1, source_target_pairs={{0,32},{8,40},{16,48},{24,56},{32,64},{40,72},{48,80},{56,88},{64,... | collective-permute-start | bytes 294920 | tf_op jit(solution)/shard_map/ppermute | solution.py:439
  208.5 6.6 %collective-permute-start.13 = (bf16[96,512]{1,0:T(8,128)(2,1)S(1)}, bf16[96,512]{1,0:T(8,128)(2,1)S(1)}, u32[]{:S(2)}, u32[]{:S(2)}) collective-permute-start(bf16[96,512]{1,0:T(8,128)(2,1)S(1)} %add_convert_fusion.4), channel_id=1, source_target_pairs={{0,64},{8,72},{16,80},{24,88},{32,96},{40,104},{48,112},{56,120},{... | collective-permute-start | bytes 294920 | tf_op jit(solution)/shard_map/ppermute | solution.py:439
  209.8 5.5 %collective-permute-start.9 = (bf16[104,512]{1,0:T(8,128)(2,1)S(1)}, bf16[104,512]{1,0:T(8,128)(2,1)S(1)}, u32[]{:S(2)}, u32[]{:S(2)}) collective-permute-start(bf16[104,512]{1,0:T(8,128)(2,1)S(1)} %add_convert_fusion.3), channel_id=1, source_target_pairs={{0,24},{8,0},{16,8},{24,16},{32,56},{40,32},{48,40},{56,48},{64,88... | collective-permute-start | bytes 319496 | tf_op jit(solution)/shard_map/ppermute | solution.py:439
  210.8 6.1 %collective-permute-start.8 = (bf16[104,512]{1,0:T(8,128)(2,1)S(1)}, bf16[104,512]{1,0:T(8,128)(2,1)S(1)}, u32[]{:S(2)}, u32[]{:S(2)}) collective-permute-start(bf16[104,512]{1,0:T(8,128)(2,1)S(1)} %add_convert_fusion.3), channel_id=1, source_target_pairs={{0,8},{8,16},{16,24},{24,0},{32,40},{40,48},{48,56},{56,32},{64,72... | collective-permute-start | bytes 319496 | tf_op jit(solution)/shard_map/ppermute | solution.py:439
  211.9 6.2 %collective-permute-start.7 = (bf16[104,512]{1,0:T(8,128)(2,1)S(1)}, bf16[104,512]{1,0:T(8,128)(2,1)S(1)}, u32[]{:S(2)}, u32[]{:S(2)}) collective-permute-start(bf16[104,512]{1,0:T(8,128)(2,1)S(1)} %add_convert_fusion.3), channel_id=1, source_target_pairs={{0,16},{8,24},{16,0},{24,8},{32,48},{40,56},{48,32},{56,40},{64,80... | collective-permute-start | bytes 319496 | tf_op jit(solution)/shard_map/ppermute | solution.py:439
  218.2 45.1 %all-to-all-start.3 = ((bf16[16,384,256]{2,1,0:T(8,128)(2,1)}), bf16[16,384,256]{2,1,0:T(8,128)(2,1)}, u32[]{:S(2)}, u32[]{:S(2)}) async-start(bf16[16,384,256]{2,1,0:T(8,128)(2,1)} %shard_map.177), calls=%async_computation.3 | async-start | bytes 6291456 | tf_op jit(solution)/shard_map/all_to_all | solution.py:324
  225.9 5.8 %collective-permute-start.18 = (bf16[200,512]{1,0:T(8,128)(2,1)S(1)}, bf16[200,512]{1,0:T(8,128)(2,1)S(1)}, u32[]{:S(2)}, u32[]{:S(2)}) collective-permute-start(bf16[200,512]{1,0:T(8,128)(2,1)S(1)} %pad_maximum_fusion.refs_0_), channel_id=1, source_target_pairs={{0,6},{1,7},{2,0},{3,1},{4,2},{5,3},{6,4},{7,5},{8,14},{9,15},{10,... | collective-permute-start | bytes 614408 | tf_op jit(solution)/shard_map/ppermute | solution.py:435
  227.0 7.3 %collective-permute-start.17 = (bf16[200,512]{1,0:T(8,128)(2,1)S(1)}, bf16[200,512]{1,0:T(8,128)(2,1)S(1)}, u32[]{:S(2)}, u32[]{:S(2)}) collective-permute-start(bf16[200,512]{1,0:T(8,128)(2,1)S(1)} %pad_maximum_fusion.refs_0_), channel_id=1, source_target_pairs={{0,4},{1,5},{2,6},{3,7},{4,0},{5,1},{6,2},{7,3},{8,12},{9,13},{10,... | collective-permute-start | bytes 614408 | tf_op jit(solution)/shard_map/ppermute | solution.py:435
  228.7 7.8 %collective-permute-start.16 = (bf16[200,512]{1,0:T(8,128)(2,1)S(1)}, bf16[200,512]{1,0:T(8,128)(2,1)S(1)}, u32[]{:S(2)}, u32[]{:S(2)}) collective-permute-start(bf16[200,512]{1,0:T(8,128)(2,1)S(1)} %pad_maximum_fusion.refs_0_), channel_id=1, source_target_pairs={{0,2},{1,3},{2,4},{3,5},{4,6},{5,7},{6,0},{7,1},{8,10},{9,11},{10,... | collective-permute-start | bytes 614408 | tf_op jit(solution)/shard_map/ppermute | solution.py:435
  228.7 8.6 %collective-permute-start.19 = (bf16[200,512]{1,0:T(8,128)(2,1)S(1)}, bf16[200,512]{1,0:T(8,128)(2,1)S(1)}, u32[]{:S(2)}, u32[]{:S(2)}) collective-permute-start(bf16[200,512]{1,0:T(8,128)(2,1)S(1)} %pad_maximum_fusion.refs_0_), channel_id=1, source_target_pairs={{0,1},{1,0},{2,3},{3,2},{4,5},{5,4},{6,7},{7,6},{8,9},{9,8},{10,11... | collective-permute-start | bytes 614408 | tf_op jit(solution)/shard_map/ppermute | solution.py:453
  231.7 5.6 %collective-permute-start.22 = (bf16[200,512]{1,0:T(8,128)(2,1)S(1)}, bf16[200,512]{1,0:T(8,128)(2,1)S(1)}, u32[]{:S(2)}, u32[]{:S(2)}) collective-permute-start(bf16[200,512]{1,0:T(8,128)(2,1)S(1)} %collective-permute-done.18.refs_3_), channel_id=1, source_target_pairs={{0,1},{1,0},{2,3},{3,2},{4,5},{5,4},{6,7},{7,6},{8,9},{9,8},{10,11... | collective-permute-start | bytes 614408 | tf_op jit(solution)/shard_map/ppermute | solution.py:453
  (15 other events, 155.9 us)

commit v5 on v3

--- a/solution.py
+++ b/solution.py
@@ -419,7 +419,7 @@
     )(ilane, d1, w1_user, w1_item)
 
     def gather_add(terms, half, *into):
-        steps = 4
+        steps = 2
         r = rows // steps
         grad = jax.ShapeDtypeStruct((rows, 2 * D), F32)
         return call(
@@ -447,7 +447,7 @@
         )
 
     def ring_sum(v, step):
-        v = v.astype(BF)
+        v = lax.optimization_barrier(v.astype(BF))
         one, two, three = (step(v, k).astype(F32) for k in (1, 2, 3))
         return (v.astype(F32) + two) + (one + three)
 

time: 262 us -> 260 us (level)
  transfers between devices with their start and end apart: 27 -> 27, of which waited for: 11 -> 11; matrix products, arithmetic and copies ran while one was open for 4% -> 4% of each run, Pallas kernels for 30% -> 29%
where the time goes in v5:
time: 260 us; the launch traced here: 259 us
  Pallas kernels  120 us (46%)
  waiting for transfers between devices  62 us (24%)
  starting transfers between devices  49 us (19%)
  blocking collectives  15.7 us (6%)
  local copies, waits for them, and re-layouts  6.95 us (3%)
  other arithmetic  4.32 us (2%)
    all_to_all x4, waiting for transfers between devices, exchange(): return lax.all_to_all(x, 'emb', split_axis=0, concat_axis=0, tiled=True)  47 us
    pallas_call x1, Pallas kernels, body(): call(forward_kernel, (groups,), [whole((m, groups)), user_block, all_item...  25.3 us
    pallas_call x2, Pallas kernels, fetch(): call(fetch_kernel, (groups,), [whole((owners, 1, 512)), table, table], pl...  22.1 us
    pallas_call x2, Pallas kernels, gather_add(): call(gather_add_kernel, (2 * steps,), [pl.BlockSpec((1, 1, slots), lambda...  20.6 us
    ppermute x12, starting transfers between devices, shift_emb(): lax.ppermute(x, 'emb', [(a * side + b, (a + kx) % side * side + (b + kz)...  20.5 us
    all_to_all x4, starting transfers between devices, exchange(): return lax.all_to_all(x, 'emb', split_axis=0, concat_axis=0, tiled=True)  20.1 us
    pallas_call x1, Pallas kernels, body(): call(middle_kernel, (2 * groups,), [whole((m, groups)), whole((m, groups)...  18.3 us
    all_to_all x1, blocking collectives, exchange(): return lax.all_to_all(x, 'emb', split_axis=0, concat_axis=0, tiled=True)  15.7 us
  transfers between devices with their start and end apart: 27, of which 11 were waited for; matrix products, arithmetic and copies ran while one was open for 4% of the time, Pallas kernels for 29%

profile of v5, /device:TPU:0, one launch (start us, length us, event | category | flops | bytes accessed | tf_op | source)
XLA Modules:
  0.0 259.1 jit_solution(5219850235144318099)
XLA Ops:
  0.6 4.3 %shard_map.171 = (s32[16,1,512]{2,1,0:T(1,128)}, s32[16,256]{1,0:T(8,128)}, s32[2,256,16]{2,1,0:T(8,128)}) custom-call(s32[16,128]{1,0:T(8,128)} %bitcast.29, s32[16,128]{1,0:T(8,128)} %bitcast.30, s32[16,128]{1,0:T(8,128)} %bitcast.31, s32[16,128]{1,0:T(8,128)} %bitcast.32, s32[16,128]{1,0:T(8,128)} %bitcast.33), custom_call_target="tpu_custom_call" | custom-call | tf_op jit(solution)/shard_map/pallas_call | solution.py:330
  4.9 15.7 %all_to_all.25.asked_ref = s32[16,1,512]{2,1,0:T(1,128)} all-to-all(s32[16,1,512]{2,1,0:T(1,128)} %get-tuple-element.42), channel_id=1, replica_groups=mesh['emb'=16,'dp'=8] {'emb'}, dimensions={0} | all-to-all | bytes 65536 | tf_op jit(solution)/shard_map/all_to_all | solution.py:328
  20.6 11.1 %shard_map.173 = bf16[16,384,256]{2,1,0:T(8,128)(2,1)} custom-call(s32[16,1,512]{2,1,0:T(1,128)} %all_to_all.25.asked_ref, bf16[2048,512]{1,0:T(8,128)(2,1)} %ut_ref.3, bf16[2048,512]{1,0:T(8,128)(2,1)} %it_ref.3), custom_call_target="tpu_custom_call" | custom-call | flops 100663296 | bytes 81920 | tf_op jit(solution)/shard_map/pallas_call | solution.py:360
  31.7 4.5 %all-to-all-start.2 = ((bf16[16,384,256]{2,1,0:T(8,128)(2,1)}), bf16[16,384,256]{2,1,0:T(8,128)(2,1)}, u32[]{:S(2)}, u32[]{:S(2)}) async-start(bf16[16,384,256]{2,1,0:T(8,128)(2,1)} %shard_map.173), calls=%async_computation.2 | async-start | bytes 6291456 | tf_op jit(solution)/shard_map/all_to_all | solution.py:328
  36.2 11.1 %shard_map.172 = bf16[16,384,256]{2,1,0:T(8,128)(2,1)} custom-call(s32[16,1,512]{2,1,0:T(1,128)} %all_to_all.25.asked_ref, bf16[2048,512]{1,0:T(8,128)(2,1)} %ut_ref.3, bf16[2048,512]{1,0:T(8,128)(2,1)} %it_ref.3), custom_call_target="tpu_custom_call" | custom-call | flops 100663296 | bytes 81920 | tf_op jit(solution)/shard_map/pallas_call | solution.py:360
  47.3 30.1 %all-to-all-done.2.um_ref.im_ref = bf16[16,384,256]{2,1,0:T(8,128)(2,1)} async-done(((bf16[16,384,256]{2,1,0:T(8,128)(2,1)}), bf16[16,384,256]{2,1,0:T(8,128)(2,1)}, u32[]{:S(2)}, u32[]{:S(2)}) %all-to-all-start.2) | async-done | bytes 3145760 | tf_op jit(solution)/shard_map/all_to_all | solution.py:328
  77.3 4.7 %all-to-all-start.1 = ((bf16[16,384,256]{2,1,0:T(8,128)(2,1)}), bf16[16,384,256]{2,1,0:T(8,128)(2,1)}, u32[]{:S(2)}, u32[]{:S(2)}) async-start(bf16[16,384,256]{2,1,0:T(8,128)(2,1)} %shard_map.172), calls=%async_computation.1 | async-start | bytes 6291456 | tf_op jit(solution)/shard_map/all_to_all | solution.py:328
  85.3 25.3 %shard_map.174 = (bf16[3072,256]{1,0:T(8,128)(2,1)}, bf16[3072,512]{1,0:T(8,128)(2,1)}, bf16[3072,512]{1,0:T(8,128)(2,1)}, bf16[3072,512]{1,0:T(8,128)(2,1)}, bf...) custom-call(s32[768,4]{1,0:T(8,128)} %bitcast.22, ...), custom_call_target="tpu_custom_call" | custom-call | flops 150994944 | bytes 393216 | tf_op jit(solution)/shard_map/pallas_call | solution.py:369
  110.7 8.5 %all-to-all-done.1.ug_ref.ig_ref = bf16[16,384,256]{2,1,0:T(8,128)(2,1)} async-done(((bf16[16,384,256]{2,1,0:T(8,128)(2,1)}), bf16[16,384,256]{2,1,0:T(8,128)(2,1)}, u32[]{:S(2)}, u32[]{:S(2)}) %all-to-all-start.1) | async-done | bytes 3145760 | tf_op jit(solution)/shard_map/all_to_all | solution.py:328
  119.2 18.3 %shard_map.175 = (bf16[16,384,256]{2,1,0:T(8,128)(2,1)}, f32[3072,128]{1,0:T(8,128)}, f32[1,256]{1,0:T(1,128)}) custom-call(s32[768,4]{1,0:T(8,128)} %bitcast.23, s32[768,4]{1,0:T(8,128)} %bitcast.24, s32[1,3072]{1,0:T(1,128)} %reshape.59.ilane_ref, bf16[16,384,256]{2,1,0:T(8,128)(2,1)} %all-to-all-done.1.ug_ref.ig_ref, ...), custom_call_target="tpu_custom_call" | custom-call | flops 150994944 | bytes 147456 | tf_op jit(solution)/shard_map/pallas_call | solution.py:378
  137.5 6.5 %all-to-all-start.4 = ((bf16[16,384,256]{2,1,0:T(8,128)(2,1)}), bf16[16,384,256]{2,1,0:T(8,128)(2,1)}, u32[]{:S(2)}, u32[]{:S(2)}) async-start(bf16[16,384,256]{2,1,0:T(8,128)(2,1)} %get-tuple-element.61), calls=%async_computation.4 | async-start | bytes 6291456 | tf_op jit(solution)/shard_map/all_to_all | solution.py:328
  143.9 15.2 %shard_map.176 = (bf16[3072,512]{1,0:T(8,128)(2,1)}, bf16[800,512]{1,0:T(8,128)(2,1)}, bf16[800,512]{1,0:T(8,128)(2,1)}) custom-call(s32[1]{0:T(128)} %bitcast.6.me_ref, f32[3072,128]{1,0:T(8,128)} %get-tuple-element.46.delta_ref, bf16[16,384,256]{2,1,0:T(8,128)(2,1)} %all-to-all-done.2.um_ref.im_ref, bf16[3072,256]{1,0:T(8,128)(2,1)} %get-tuple-element.47.im_ref, ...), custom_call_target="tpu_custom_call" | custom-call | flops 125829120 | bytes 393216 | tf_op jit(solution)/shard_map/pallas_call | solution.py:401
  159.2 2.5 collective-permute-done
  169.0 11.1 %shard_map.177 = bf16[16,384,256]{2,1,0:T(8,128)(2,1)} custom-call(s32[1,3072]{1,0:T(1,128)} %reshape.59.ilane_ref, bf16[3072,512]{1,0:T(8,128)(2,1)} %get-tuple-element.55.d1_ref, bf16[256,512]{1,0:T(8,128)(2,1)} %w1u_ref.3, bf16[256,512]{1,0:T(8,128)(2,1)} %w1i_ref.3), custom_call_target="tpu_custom_call" | custom-call | flops 100663296 | bytes 98304 | tf_op jit(solution)/shard_map/pallas_call | solution.py:412
  181.4 3.1 %collective-permute-start.12 = (bf16[96,512]{1,0:T(8,128)(2,1)S(1)}, bf16[96,512]{1,0:T(8,128)(2,1)S(1)}, u32[]{:S(2)}, u32[]{:S(2)}) collective-permute-start(bf16[96,512]{1,0:T(8,128)(2,1)S(1)} %slice.80), channel_id=1, source_target_pairs={{0,24},{8,0},{16,8},{24,16},{32,56},{40,32},{48,40},{56,48},{64,88... | collective-permute-start | bytes 294920 | tf_op jit(solution)/shard_map/ppermute | solution.py:441
  186.9 2.7 %collective-permute-start.6 = (bf16[104,512]{1,0:T(8,128)(2,1)S(1)}, bf16[104,512]{1,0:T(8,128)(2,1)S(1)}, u32[]{:S(2)}, u32[]{:S(2)}) collective-permute-start(bf16[104,512]{1,0:T(8,128)(2,1)S(1)} %slice.79), channel_id=1, source_target_pairs={{0,96},{8,104},{16,112},{24,120},{32,0},{40,8},{48,16},{56,24},{64... | collective-permute-start | bytes 319496 | tf_op jit(solution)/shard_map/ppermute | solution.py:441
  192.0 2.4 collective-permute-start.15
  207.1 4.5 %all-to-all-start.3 = ((bf16[16,384,256]{2,1,0:T(8,128)(2,1)}), bf16[16,384,256]{2,1,0:T(8,128)(2,1)}, u32[]{:S(2)}, u32[]{:S(2)}) async-start(bf16[16,384,256]{2,1,0:T(8,128)(2,1)} %shard_map.177), calls=%async_computation.3 | async-start | bytes 6291456 | tf_op jit(solution)/shard_map/all_to_all | solution.py:328
  214.7 2.8 %collective-permute-done.18.refs_3_ = bf16[200,512]{1,0:T(8,128)(2,1)S(1)} collective-permute-done((bf16[200,512]{1,0:T(8,128)(2,1)S(1)}, bf16[200,512]{1,0:T(8,128)(2,1)S(1)}, u32[]{:S(2)}, u32[]{:S(2)}) %collective-permute-start.18) | collective-permute-done | bytes 204832 | tf_op jit(solution)/shard_map/ppermute | solution.py:437
  217.5 2.7 %collective-permute-done.17.refs_2_ = bf16[200,512]{1,0:T(8,128)(2,1)S(1)} collective-permute-done((bf16[200,512]{1,0:T(8,128)(2,1)S(1)}, bf16[200,512]{1,0:T(8,128)(2,1)S(1)}, u32[]{:S(2)}, u32[]{:S(2)}) %collective-permute-start.17) | collective-permute-done | bytes 204832 | tf_op jit(solution)/shard_map/ppermute | solution.py:437
  224.6 3.4 %shard_map.179 = (f32[256,512]{1,0:T(8,128)}, f32[256,512]{1,0:T(8,128)}, f32[512,512]{1,0:T(8,128)}, f32[512,512]{1,0:T(8,128)}, f32[64,512]{1,0:T(8,128)}) custom-call(s32[1]{0:T(128)} %bitcast.6.me_ref, bf16[200,512]{1,0:T(8,128)(2,1)} %copy-done, bf16[200,512]{1,0:T(8,128)(2,1)} %copy-done.4, bf16[200,512]{1,0:T(8,128)(2,1)} %copy-done.3, ...), custom_call_target="tpu_custom_call" | custom-call | tf_op jit(solution)/shard_map/pallas_call | solution.py:482
  230.0 10.3 %shard_map.178 = (f32[2048,512]{1,0:T(8,128)}, f32[2048,512]{1,0:T(8,128)}) custom-call(s32[2,1,3072]{2,1,0:T(1,128)} %reshape.58.lane_ref, bf16[16,384,256]{2,1,0:T(8,128)(2,1)} %all-to-all-done.4.terms_ref), custom_call_target="tpu_custom_call" | custom-call | flops 100663296 | bytes 114688 | tf_op jit(solution)/shard_map/pallas_call | solution.py:425
  240.3 8.4 %all-to-all-done.3.terms_ref = bf16[16,384,256]{2,1,0:T(8,128)(2,1)} async-done(((bf16[16,384,256]{2,1,0:T(8,128)(2,1)}), bf16[16,384,256]{2,1,0:T(8,128)(2,1)}, u32[]{:S(2)}, u32[]{:S(2)}) %all-to-all-start.3) | async-done | bytes 3145760 | tf_op jit(solution)/shard_map/all_to_all | solution.py:328
  248.8 10.3 %shard_map.180 = (f32[2048,512]{1,0:T(8,128)}, f32[2048,512]{1,0:T(8,128)}) custom-call(s32[2,1,3072]{2,1,0:T(1,128)} %reshape.58.lane_ref, bf16[16,384,256]{2,1,0:T(8,128)(2,1)} %all-to-all-done.3.terms_ref, f32[2048,512]{1,0:T(8,128)} %get-tuple-element.68.rest_0_, f32[2048,512]{1,0:T(8,128)} %get-tuple-element.69.rest_1_), custom_call_target="tpu_custom_call", output_to_operand_aliasing={{0}: (2, {}), {1}: (3, {})} | custom-call | flops 100663296 | bytes 114688 | tf_op jit(solution)/shard_map/pallas_call | solution.py:425
  (86 shorter events, 38.8 us)
Async XLA Ops:
  31.7 45.6 %all-to-all-start.2 = ((bf16[16,384,256]{2,1,0:T(8,128)(2,1)}), bf16[16,384,256]{2,1,0:T(8,128)(2,1)}, u32[]{:S(2)}, u32[]{:S(2)}) async-start(bf16[16,384,256]{2,1,0:T(8,128)(2,1)} %shard_map.173), calls=%async_computation.2 | async-start | bytes 6291456 | tf_op jit(solution)/shard_map/all_to_all | solution.py:328
  77.3 41.9 %all-to-all-start.1 = ((bf16[16,384,256]{2,1,0:T(8,128)(2,1)}), bf16[16,384,256]{2,1,0:T(8,128)(2,1)}, u32[]{:S(2)}, u32[]{:S(2)}) async-start(bf16[16,384,256]{2,1,0:T(8,128)(2,1)} %shard_map.172), calls=%async_computation.1 | async-start | bytes 6291456 | tf_op jit(solution)/shard_map/all_to_all | solution.py:328
  137.5 69.7 %all-to-all-start.4 = ((bf16[16,384,256]{2,1,0:T(8,128)(2,1)}), bf16[16,384,256]{2,1,0:T(8,128)(2,1)}, u32[]{:S(2)}, u32[]{:S(2)}) async-start(bf16[16,384,256]{2,1,0:T(8,128)(2,1)} %get-tuple-element.61), calls=%async_computation.4 | async-start | bytes 6291456 | tf_op jit(solution)/shard_map/all_to_all | solution.py:328
  163.7 16.3 %collective-permute-start.1 = (bf16[200,512]{1,0:T(8,128)(2,1)}, bf16[200,512]{1,0:T(8,128)(2,1)}, u32[]{:S(2)}, u32[]{:S(2)}) collective-permute-start(bf16[200,512]{1,0:T(8,128)(2,1)} %get-tuple-element.77), channel_id=1, source_target_pairs={{0,2},{1,3},{2,4},{3,5},{4,6},{5,7},{6,0},{7,1},{8,10},{9,11},{10,... | collective-permute-start | bytes 614408 | tf_op jit(solution)/shard_map/ppermute | solution.py:437
  165.4 14.7 %collective-permute-start.3 = (bf16[200,512]{1,0:T(8,128)(2,1)}, bf16[200,512]{1,0:T(8,128)(2,1)}, u32[]{:S(2)}, u32[]{:S(2)}) collective-permute-start(bf16[200,512]{1,0:T(8,128)(2,1)} %get-tuple-element.78), channel_id=1, source_target_pairs={{0,6},{1,7},{2,0},{3,1},{4,2},{5,3},{6,4},{7,5},{8,14},{9,15},{10,... | collective-permute-start | bytes 614408 | tf_op jit(solution)/shard_map/ppermute | solution.py:437
  167.0 13.1 %collective-permute-start.2 = (bf16[200,512]{1,0:T(8,128)(2,1)}, bf16[200,512]{1,0:T(8,128)(2,1)}, u32[]{:S(2)}, u32[]{:S(2)}) collective-permute-start(bf16[200,512]{1,0:T(8,128)(2,1)} %get-tuple-element.79), channel_id=1, source_target_pairs={{0,4},{1,5},{2,6},{3,7},{4,0},{5,1},{6,2},{7,3},{8,12},{9,13},{10,... | collective-permute-start | bytes 614408 | tf_op jit(solution)/shard_map/ppermute | solution.py:437
  181.4 8.2 %collective-permute-start.12 = (bf16[96,512]{1,0:T(8,128)(2,1)S(1)}, bf16[96,512]{1,0:T(8,128)(2,1)S(1)}, u32[]{:S(2)}, u32[]{:S(2)}) collective-permute-start(bf16[96,512]{1,0:T(8,128)(2,1)S(1)} %slice.80), channel_id=1, source_target_pairs={{0,24},{8,0},{16,8},{24,16},{32,56},{40,32},{48,40},{56,48},{64,88... | collective-permute-start | bytes 294920 | tf_op jit(solution)/shard_map/ppermute | solution.py:441
  184.6 7.4 %collective-permute-start.11 = (bf16[96,512]{1,0:T(8,128)(2,1)S(1)}, bf16[96,512]{1,0:T(8,128)(2,1)S(1)}, u32[]{:S(2)}, u32[]{:S(2)}) collective-permute-start(bf16[96,512]{1,0:T(8,128)(2,1)S(1)} %slice.80), channel_id=1, source_target_pairs={{0,8},{8,16},{16,24},{24,0},{32,40},{40,48},{48,56},{56,32},{64,72... | collective-permute-start | bytes 294920 | tf_op jit(solution)/shard_map/ppermute | solution.py:441
  184.6 7.4 %collective-permute-start.10 = (bf16[96,512]{1,0:T(8,128)(2,1)S(1)}, bf16[96,512]{1,0:T(8,128)(2,1)S(1)}, u32[]{:S(2)}, u32[]{:S(2)}) collective-permute-start(bf16[96,512]{1,0:T(8,128)(2,1)S(1)} %slice.80), channel_id=1, source_target_pairs={{0,16},{8,24},{16,0},{24,8},{32,48},{40,56},{48,32},{56,40},{64,80... | collective-permute-start | bytes 294920 | tf_op jit(solution)/shard_map/ppermute | solution.py:441
  186.9 7.5 %collective-permute-start.6 = (bf16[104,512]{1,0:T(8,128)(2,1)S(1)}, bf16[104,512]{1,0:T(8,128)(2,1)S(1)}, u32[]{:S(2)}, u32[]{:S(2)}) collective-permute-start(bf16[104,512]{1,0:T(8,128)(2,1)S(1)} %slice.79), channel_id=1, source_target_pairs={{0,96},{8,104},{16,112},{24,120},{32,0},{40,8},{48,16},{56,24},{64... | collective-permute-start | bytes 319496 | tf_op jit(solution)/shard_map/ppermute | solution.py:441
  189.7 7.8 %collective-permute-start.5 = (bf16[104,512]{1,0:T(8,128)(2,1)S(1)}, bf16[104,512]{1,0:T(8,128)(2,1)S(1)}, u32[]{:S(2)}, u32[]{:S(2)}) collective-permute-start(bf16[104,512]{1,0:T(8,128)(2,1)S(1)} %slice.79), channel_id=1, source_target_pairs={{0,32},{8,40},{16,48},{24,56},{32,64},{40,72},{48,80},{56,88},{64,... | collective-permute-start | bytes 319496 | tf_op jit(solution)/shard_map/ppermute | solution.py:441
  189.7 7.8 %collective-permute-start.4 = (bf16[104,512]{1,0:T(8,128)(2,1)S(1)}, bf16[104,512]{1,0:T(8,128)(2,1)S(1)}, u32[]{:S(2)}, u32[]{:S(2)}) collective-permute-start(bf16[104,512]{1,0:T(8,128)(2,1)S(1)} %slice.79), channel_id=1, source_target_pairs={{0,64},{8,72},{16,80},{24,88},{32,96},{40,104},{48,112},{56,120},{... | collective-permute-start | bytes 319496 | tf_op jit(solution)/shard_map/ppermute | solution.py:441
  192.0 8.8 %collective-permute-start.15 = (bf16[96,512]{1,0:T(8,128)(2,1)S(1)}, bf16[96,512]{1,0:T(8,128)(2,1)S(1)}, u32[]{:S(2)}, u32[]{:S(2)}) collective-permute-start(bf16[96,512]{1,0:T(8,128)(2,1)S(1)} %add_convert_fusion.4), channel_id=1, source_target_pairs={{0,96},{8,104},{16,112},{24,120},{32,0},{40,8},{48,16},{56,24},{64... | collective-permute-start | bytes 294920 | tf_op jit(solution)/shard_map/ppermute | solution.py:441
  194.4 8.4 %collective-permute-start.14 = (bf16[96,512]{1,0:T(8,128)(2,1)S(1)}, bf16[96,512]{1,0:T(8,128)(2,1)S(1)}, u32[]{:S(2)}, u32[]{:S(2)}) collective-permute-start(bf16[96,512]{1,0:T(8,128)(2,1)S(1)} %add_convert_fusion.4), channel_id=1, source_target_pairs={{0,32},{8,40},{16,48},{24,56},{32,64},{40,72},{48,80},{56,88},{64,... | collective-permute-start | bytes 294920 | tf_op jit(solution)/shard_map/ppermute | solution.py:441
  194.4 8.4 %collective-permute-start.13 = (bf16[96,512]{1,0:T(8,128)(2,1)S(1)}, bf16[96,512]{1,0:T(8,128)(2,1)S(1)}, u32[]{:S(2)}, u32[]{:S(2)}) collective-permute-start(bf16[96,512]{1,0:T(8,128)(2,1)S(1)} %add_convert_fusion.4), channel_id=1, source_target_pairs={{0,64},{8,72},{16,80},{24,88},{32,96},{40,104},{48,112},{56,120},{... | collective-permute-start | bytes 294920 | tf_op jit(solution)/shard_map/ppermute | solution.py:441
  197.5 5.9 %collective-permute-start.9 = (bf16[104,512]{1,0:T(8,128)(2,1)S(1)}, bf16[104,512]{1,0:T(8,128)(2,1)S(1)}, u32[]{:S(2)}, u32[]{:S(2)}) collective-permute-start(bf16[104,512]{1,0:T(8,128)(2,1)S(1)} %add_convert_fusion.3), channel_id=1, source_target_pairs={{0,24},{8,0},{16,8},{24,16},{32,56},{40,32},{48,40},{56,48},{64,88... | collective-permute-start | bytes 319496 | tf_op jit(solution)/shard_map/ppermute | solution.py:441
  199.2 5.9 %collective-permute-start.8 = (bf16[104,512]{1,0:T(8,128)(2,1)S(1)}, bf16[104,512]{1,0:T(8,128)(2,1)S(1)}, u32[]{:S(2)}, u32[]{:S(2)}) collective-permute-start(bf16[104,512]{1,0:T(8,128)(2,1)S(1)} %add_convert_fusion.3), channel_id=1, source_target_pairs={{0,8},{8,16},{16,24},{24,0},{32,40},{40,48},{48,56},{56,32},{64,72... | collective-permute-start | bytes 319496 | tf_op jit(solution)/shard_map/ppermute | solution.py:441
  200.8 6.2 %collective-permute-start.7 = (bf16[104,512]{1,0:T(8,128)(2,1)S(1)}, bf16[104,512]{1,0:T(8,128)(2,1)S(1)}, u32[]{:S(2)}, u32[]{:S(2)}) collective-permute-start(bf16[104,512]{1,0:T(8,128)(2,1)S(1)} %add_convert_fusion.3), channel_id=1, source_target_pairs={{0,16},{8,24},{16,0},{24,8},{32,48},{40,56},{48,32},{56,40},{64,80... | collective-permute-start | bytes 319496 | tf_op jit(solution)/shard_map/ppermute | solution.py:441
  207.1 41.7 %all-to-all-start.3 = ((bf16[16,384,256]{2,1,0:T(8,128)(2,1)}), bf16[16,384,256]{2,1,0:T(8,128)(2,1)}, u32[]{:S(2)}, u32[]{:S(2)}) async-start(bf16[16,384,256]{2,1,0:T(8,128)(2,1)} %shard_map.177), calls=%async_computation.3 | async-start | bytes 6291456 | tf_op jit(solution)/shard_map/all_to_all | solution.py:328
  211.7 5.8 %collective-permute-start.18 = (bf16[200,512]{1,0:T(8,128)(2,1)S(1)}, bf16[200,512]{1,0:T(8,128)(2,1)S(1)}, u32[]{:S(2)}, u32[]{:S(2)}) collective-permute-start(bf16[200,512]{1,0:T(8,128)(2,1)S(1)} %pad_maximum_fusion.refs_0_), channel_id=1, source_target_pairs={{0,6},{1,7},{2,0},{3,1},{4,2},{5,3},{6,4},{7,5},{8,14},{9,15},{10,... | collective-permute-start | bytes 614408 | tf_op jit(solution)/shard_map/ppermute | solution.py:437
  212.8 7.3 %collective-permute-start.17 = (bf16[200,512]{1,0:T(8,128)(2,1)S(1)}, bf16[200,512]{1,0:T(8,128)(2,1)S(1)}, u32[]{:S(2)}, u32[]{:S(2)}) collective-permute-start(bf16[200,512]{1,0:T(8,128)(2,1)S(1)} %pad_maximum_fusion.refs_0_), channel_id=1, source_target_pairs={{0,4},{1,5},{2,6},{3,7},{4,0},{5,1},{6,2},{7,3},{8,12},{9,13},{10,... | collective-permute-start | bytes 614408 | tf_op jit(solution)/shard_map/ppermute | solution.py:437
  214.5 7.8 %collective-permute-start.16 = (bf16[200,512]{1,0:T(8,128)(2,1)S(1)}, bf16[200,512]{1,0:T(8,128)(2,1)S(1)}, u32[]{:S(2)}, u32[]{:S(2)}) collective-permute-start(bf16[200,512]{1,0:T(8,128)(2,1)S(1)} %pad_maximum_fusion.refs_0_), channel_id=1, source_target_pairs={{0,2},{1,3},{2,4},{3,5},{4,6},{5,7},{6,0},{7,1},{8,10},{9,11},{10,... | collective-permute-start | bytes 614408 | tf_op jit(solution)/shard_map/ppermute | solution.py:437
  214.7 8.4 %collective-permute-start.19 = (bf16[200,512]{1,0:T(8,128)(2,1)S(1)}, bf16[200,512]{1,0:T(8,128)(2,1)S(1)}, u32[]{:S(2)}, u32[]{:S(2)}) collective-permute-start(bf16[200,512]{1,0:T(8,128)(2,1)S(1)} %pad_maximum_fusion.refs_0_), channel_id=1, source_target_pairs={{0,1},{1,0},{2,3},{3,2},{4,5},{5,4},{6,7},{7,6},{8,9},{9,8},{10,11... | collective-permute-start | bytes 614408 | tf_op jit(solution)/shard_map/ppermute | solution.py:455
  217.5 5.6 %collective-permute-start.22 = (bf16[200,512]{1,0:T(8,128)(2,1)S(1)}, bf16[200,512]{1,0:T(8,128)(2,1)S(1)}, u32[]{:S(2)}, u32[]{:S(2)}) collective-permute-start(bf16[200,512]{1,0:T(8,128)(2,1)S(1)} %collective-permute-done.18.refs_3_), channel_id=1, source_target_pairs={{0,1},{1,0},{2,3},{3,2},{4,5},{5,4},{6,7},{7,6},{8,9},{9,8},{10,11... | collective-permute-start | bytes 614408 | tf_op jit(solution)/shard_map/ppermute | solution.py:455
  (14 other events, 158.1 us)

commit v6 on v5

--- a/solution.py
+++ b/solution.py
@@ -57,7 +57,7 @@
     return (z * sig).astype(BF), (sig * (1.0 + z * (1.0 - sig))).astype(BF)
 
 
-def arrange_kernel(cap, uo_ref, ur_ref, io_ref, ir_ref, lab_ref, req_ref, lanes_ref, cols_ref):
+def arrange_kernel(cap, ask, uo_ref, ur_ref, io_ref, ir_ref, lab_ref, *outs):
     blocks = uo_ref.shape[0]
     owners = 16
     upto = jnp.where(
@@ -119,11 +119,14 @@
             spread(chosen, rows(lo)), slots
         )
 
-    req = jnp.concatenate(
-        [wanted(u_chosen, u_slots, ur_hi, ur_lo), wanted(i_chosen, i_slots, ir_hi, ir_lo)], axis=1
-    ).astype(I32)
-    for o in range(owners):
-        req_ref[o] = req[o : o + 1]
+    if ask:
+        req = jnp.concatenate(
+            [wanted(u_chosen, u_slots, ur_hi, ur_lo), wanted(i_chosen, i_slots, ir_hi, ir_lo)], axis=1
+        ).astype(I32)
+        for o in range(owners):
+            outs[0][o] = req[o : o + 1]
+        return
+    lanes_ref, cols_ref = outs
     s_hi, s_lo = spread(u_chosen, rows(is_hi)), spread(u_chosen, rows(is_lo))
     s_flag = spread(u_chosen, rows(flag))
     lanes_ref[...] = (dot_nt(s_hi, u_slots) * 64.0 + dot_nt(s_lo, u_slots)).astype(I32)
@@ -327,24 +330,17 @@
     def exchange(x):
         return lax.all_to_all(x, "emb", split_axis=0, concat_axis=0, tiled=True)
 
-    req, lanes, cols = pl.pallas_call(
-        functools.partial(arrange_kernel, cap),
-        out_shape=(
-            jax.ShapeDtypeStruct((owners, 1, 512), I32),
-            jax.ShapeDtypeStruct((owners, 256), I32),
-            jax.ShapeDtypeStruct((2, 256, owners), I32),
-        ),
-        compiler_params=PARAMS,
-    )(*(a.reshape(blocks, 128) for a in (user_owner, user_row, item_owner, item_row, labels)))
-
+    lists = [a.reshape(blocks, 128) for a in (user_owner, user_row, item_owner, item_row, labels)]
+
+    def arrange(ask, out_shape, given):
+        return pl.pallas_call(
+            functools.partial(arrange_kernel, cap, ask), out_shape=out_shape, compiler_params=PARAMS
+        )(*given)
+
+    req = arrange(True, jax.ShapeDtypeStruct((owners, 1, 512), I32), lists)
     asked = exchange(req)
     wanted = asked.reshape(owners, 2, 256)[:, :, :cap]
     wlane = wanted.transpose(1, 0, 2).reshape(2, 1, slots)
-    ilane = lanes[:, :cap].reshape(1, slots)
-    side = cols[:, :cap, :].reshape(2, cap, groups, peers).transpose(0, 3, 1, 2)
-    side = side.reshape(2, m, groups)
-    icol, fcol = side[0], side[1]
-
     buffer = jax.ShapeDtypeStruct((owners, 2 * cap, D), BF)
     user_block = pl.BlockSpec((peers, cap, D), lambda i: (i, 0, 0))
     all_items = pl.BlockSpec((owners, cap, D), lambda i: (0, 1, 0))
@@ -363,8 +359,20 @@
             flops=4 * slots * rows * D, moved=4 * slots * D + 4 * rows * D,
         )(asked, user_table, item_table)
 
-    mlp_back = exchange(fetch(1))
-    gmf_back = exchange(fetch(0))
+    mlp_rows = fetch(1)
+    mlp_back = exchange(mlp_rows)
+    *later, _ = lax.optimization_barrier((*lists, mlp_rows))
+    lanes, cols = arrange(
+        False,
+        (jax.ShapeDtypeStruct((owners, 256), I32), jax.ShapeDtypeStruct((2, 256, owners), I32)),
+        later,
+    )
+    ilane = lanes[:, :cap].reshape(1, slots)
+    side = cols[:, :cap, :].reshape(2, cap, groups, peers).transpose(0, 3, 1, 2)
+    side = side.reshape(2, m, groups)
+    icol, fcol = side[0], side[1]
+    gmf_rows, ilane, icol, fcol = lax.optimization_barrier((fetch(0), ilane, icol, fcol))
+    gmf_back = exchange(gmf_rows)
 
     im, a1, s1, a2, s2, a3, s3, deep = call(
         forward_kernel, (groups,),

time: 260 us -> 259 us (level)
  waiting for transfers between devices: 62 us -> 58.1 us
    all_to_all x4, waiting for transfers between devices: 47 us -> 42.5 us  [exchange(): return lax.all_to_all(x, 'emb', split_axis=0, concat_axis=0, tiled=True)]
    pallas_call x1 -> x2, Pallas kernels: 4.31 us -> 6.05 us  [arrange(): pl.pallas_call(functools.partial(arrange_kernel, cap, ask), out_shape=out...]
  transfers between devices with their start and end apart: 27 -> 27, of which waited for: 11 -> 11; matrix products, arithmetic and copies ran while one was open for 4% -> 4% of each run, Pallas kernels for 29% -> 31%
where the time goes in v6:
time: 259 us; the launch traced here: 258 us
  Pallas kernels  122 us (47%)
  waiting for transfers between devices  58.1 us (22%)
  starting transfers between devices  48.5 us (19%)
  blocking collectives  15.7 us (6%)
  local copies, waits for them, and re-layouts  8.56 us (3%)
  other arithmetic  4.32 us (2%)
    all_to_all x4, waiting for transfers between devices, exchange(): return lax.all_to_all(x, 'emb', split_axis=0, concat_axis=0, tiled=True)  42.5 us
    pallas_call x1, Pallas kernels, body(): call(forward_kernel, (groups,), [whole((m, groups)), user_block, all_item...  25.3 us
    pallas_call x2, Pallas kernels, fetch(): call(fetch_kernel, (groups,), [whole((owners, 1, 512)), table, table], pl...  22.1 us
    pallas_call x2, Pallas kernels, gather_add(): call(gather_add_kernel, (2 * steps,), [pl.BlockSpec((1, 1, slots), lambda...  20.6 us
    all_to_all x4, starting transfers between devices, exchange(): return lax.all_to_all(x, 'emb', split_axis=0, concat_axis=0, tiled=True)  20.2 us
    ppermute x12, starting transfers between devices, shift_emb(): lax.ppermute(x, 'emb', [(a * side + b, (a + kx) % side * side + (b + kz)...  19.9 us
    pallas_call x1, Pallas kernels, body(): call(middle_kernel, (2 * groups,), [whole((m, groups)), whole((m, groups)...  18.2 us
    all_to_all x1, blocking collectives, exchange(): return lax.all_to_all(x, 'emb', split_axis=0, concat_axis=0, tiled=True)  15.7 us
  transfers between devices with their start and end apart: 27, of which 11 were waited for; matrix products, arithmetic and copies ran while one was open for 4% of the time, Pallas kernels for 31%

profile of v6, /device:TPU:0, one launch (start us, length us, event | category | flops | bytes accessed | tf_op | source)
XLA Modules:
  0.0 257.9 jit_solution(1014010512362117795)
XLA Ops:
  0.6 2.8 %shard_map.171 = s32[16,1,512]{2,1,0:T(1,128)} custom-call(s32[16,128]{1,0:T(8,128)} %bitcast.28, s32[16,128]{1,0:T(8,128)} %bitcast.30, s32[16,128]{1,0:T(8,128)} %bitcast.32, s32[16,128]{1,0:T(8,128)} %bitcast.34, s32[16,128]{1,0:T(8,128)} %bitcast.36), custom_call_target="tpu_custom_call" | custom-call | tf_op jit(solution)/shard_map/pallas_call | solution.py:336
  3.4 15.7 %all_to_all.25.asked_ref = s32[16,1,512]{2,1,0:T(1,128)} all-to-all(s32[16,1,512]{2,1,0:T(1,128)} %shard_map.171), channel_id=1, replica_groups=mesh['emb'=16,'dp'=8] {'emb'}, dimensions={0} | all-to-all | bytes 65536 | tf_op jit(solution)/shard_map/all_to_all | solution.py:331
  19.1 11.1 %shard_map.173 = bf16[16,384,256]{2,1,0:T(8,128)(2,1)} custom-call(s32[16,1,512]{2,1,0:T(1,128)} %all_to_all.25.asked_ref, bf16[2048,512]{1,0:T(8,128)(2,1)} %ut_ref.3, bf16[2048,512]{1,0:T(8,128)(2,1)} %it_ref.3), custom_call_target="tpu_custom_call" | custom-call | flops 100663296 | bytes 81920 | tf_op jit(solution)/shard_map/pallas_call | solution.py:356
  30.2 4.5 %all-to-all-start.2 = ((bf16[16,384,256]{2,1,0:T(8,128)(2,1)}), bf16[16,384,256]{2,1,0:T(8,128)(2,1)}, u32[]{:S(2)}, u32[]{:S(2)}) async-start(bf16[16,384,256]{2,1,0:T(8,128)(2,1)} %shard_map.173), calls=%async_computation.2 | async-start | bytes 6291456 | tf_op jit(solution)/shard_map/all_to_all | solution.py:331
  34.7 3.2 %shard_map.174 = (s32[16,256]{1,0:T(8,128)}, s32[2,256,16]{2,1,0:T(8,128)}) custom-call(s32[16,128]{1,0:T(8,128)} %bitcast.29, s32[16,128]{1,0:T(8,128)} %bitcast.31, s32[16,128]{1,0:T(8,128)} %bitcast.33, s32[16,128]{1,0:T(8,128)} %bitcast.35, s32[16,128]{1,0:T(8,128)} %bitcast.37), custom_call_target="tpu_custom_call" | custom-call | tf_op jit(solution)/shard_map/pallas_call | solution.py:336
  42.3 11.1 %shard_map.172 = bf16[16,384,256]{2,1,0:T(8,128)(2,1)} custom-call(s32[16,1,512]{2,1,0:T(1,128)} %all_to_all.25.asked_ref, bf16[2048,512]{1,0:T(8,128)(2,1)} %ut_ref.3, bf16[2048,512]{1,0:T(8,128)(2,1)} %it_ref.3), custom_call_target="tpu_custom_call" | custom-call | flops 100663296 | bytes 81920 | tf_op jit(solution)/shard_map/pallas_call | solution.py:356
  53.4 22.8 %all-to-all-done.2.um_ref.im_ref = bf16[16,384,256]{2,1,0:T(8,128)(2,1)} async-done(((bf16[16,384,256]{2,1,0:T(8,128)(2,1)}), bf16[16,384,256]{2,1,0:T(8,128)(2,1)}, u32[]{:S(2)}, u32[]{:S(2)}) %all-to-all-start.2) | async-done | bytes 3145760 | tf_op jit(solution)/shard_map/all_to_all | solution.py:331
  76.2 4.7 %all-to-all-start.1 = ((bf16[16,384,256]{2,1,0:T(8,128)(2,1)}), bf16[16,384,256]{2,1,0:T(8,128)(2,1)}, u32[]{:S(2)}, u32[]{:S(2)}) async-start(bf16[16,384,256]{2,1,0:T(8,128)(2,1)} %shard_map.172), calls=%async_computation.1 | async-start | bytes 6291456 | tf_op jit(solution)/shard_map/all_to_all | solution.py:331
  81.4 25.3 %shard_map.175 = (bf16[3072,256]{1,0:T(8,128)(2,1)}, bf16[3072,512]{1,0:T(8,128)(2,1)}, bf16[3072,512]{1,0:T(8,128)(2,1)}, bf16[3072,512]{1,0:T(8,128)(2,1)}, bf...) custom-call(s32[768,4]{1,0:T(8,128)} %bitcast.22, ...), custom_call_target="tpu_custom_call" | custom-call | flops 150994944 | bytes 393216 | tf_op jit(solution)/shard_map/pallas_call | solution.py:377
  106.7 11.2 %all-to-all-done.1.ug_ref.ig_ref = bf16[16,384,256]{2,1,0:T(8,128)(2,1)} async-done(((bf16[16,384,256]{2,1,0:T(8,128)(2,1)}), bf16[16,384,256]{2,1,0:T(8,128)(2,1)}, u32[]{:S(2)}, u32[]{:S(2)}) %all-to-all-start.1) | async-done | bytes 3145760 | tf_op jit(solution)/shard_map/all_to_all | solution.py:331
  117.9 18.2 %shard_map.176 = (bf16[16,384,256]{2,1,0:T(8,128)(2,1)}, f32[3072,128]{1,0:T(8,128)}, f32[1,256]{1,0:T(1,128)}) custom-call(s32[768,4]{1,0:T(8,128)} %bitcast.23, s32[768,4]{1,0:T(8,128)} %bitcast.24, s32[1,3072]{1,0:T(1,128)} %reshape.59.ilane_ref, bf16[16,384,256]{2,1,0:T(8,128)(2,1)} %all-to-all-done.1.ug_ref.ig_ref, ...), custom_call_target="tpu_custom_call" | custom-call | flops 150994944 | bytes 147456 | tf_op jit(solution)/shard_map/pallas_call | solution.py:386
  136.2 6.5 %all-to-all-start.4 = ((bf16[16,384,256]{2,1,0:T(8,128)(2,1)}), bf16[16,384,256]{2,1,0:T(8,128)(2,1)}, u32[]{:S(2)}, u32[]{:S(2)}) async-start(bf16[16,384,256]{2,1,0:T(8,128)(2,1)} %get-tuple-element.77), calls=%async_computation.4 | async-start | bytes 6291456 | tf_op jit(solution)/shard_map/all_to_all | solution.py:331
  142.7 15.2 %shard_map.177 = (bf16[3072,512]{1,0:T(8,128)(2,1)}, bf16[800,512]{1,0:T(8,128)(2,1)}, bf16[800,512]{1,0:T(8,128)(2,1)}) custom-call(s32[1]{0:T(128)} %bitcast.11.me_ref, f32[3072,128]{1,0:T(8,128)} %get-tuple-element.62.delta_ref, bf16[16,384,256]{2,1,0:T(8,128)(2,1)} %all-to-all-done.2.um_ref.im_ref, bf16[3072,256]{1,0:T(8,128)(2,1)} %get-tuple-element.63.im_ref, ...), custom_call_target="tpu_custom_call" | custom-call | flops 125829120 | bytes 393216 | tf_op jit(solution)/shard_map/pallas_call | solution.py:409
  158.0 2.5 collective-permute-done
  167.8 11.1 %shard_map.178 = bf16[16,384,256]{2,1,0:T(8,128)(2,1)} custom-call(s32[1,3072]{1,0:T(1,128)} %reshape.59.ilane_ref, bf16[3072,512]{1,0:T(8,128)(2,1)} %get-tuple-element.71.d1_ref, bf16[256,512]{1,0:T(8,128)(2,1)} %w1u_ref.3, bf16[256,512]{1,0:T(8,128)(2,1)} %w1i_ref.3), custom_call_target="tpu_custom_call" | custom-call | flops 100663296 | bytes 98304 | tf_op jit(solution)/shard_map/pallas_call | solution.py:420
  180.3 3.1 %collective-permute-start.12 = (bf16[96,512]{1,0:T(8,128)(2,1)S(1)}, bf16[96,512]{1,0:T(8,128)(2,1)S(1)}, u32[]{:S(2)}, u32[]{:S(2)}) collective-permute-start(bf16[96,512]{1,0:T(8,128)(2,1)S(1)} %slice.80), channel_id=1, source_target_pairs={{0,24},{8,0},{16,8},{24,16},{32,56},{40,32},{48,40},{56,48},{64,88... | collective-permute-start | bytes 294920 | tf_op jit(solution)/shard_map/ppermute | solution.py:449
  185.7 2.7 %collective-permute-start.6 = (bf16[104,512]{1,0:T(8,128)(2,1)S(1)}, bf16[104,512]{1,0:T(8,128)(2,1)S(1)}, u32[]{:S(2)}, u32[]{:S(2)}) collective-permute-start(bf16[104,512]{1,0:T(8,128)(2,1)S(1)} %slice.79), channel_id=1, source_target_pairs={{0,96},{8,104},{16,112},{24,120},{32,0},{40,8},{48,16},{56,24},{64... | collective-permute-start | bytes 319496 | tf_op jit(solution)/shard_map/ppermute | solution.py:449
  205.9 4.5 %all-to-all-start.3 = ((bf16[16,384,256]{2,1,0:T(8,128)(2,1)}), bf16[16,384,256]{2,1,0:T(8,128)(2,1)}, u32[]{:S(2)}, u32[]{:S(2)}) async-start(bf16[16,384,256]{2,1,0:T(8,128)(2,1)} %shard_map.178), calls=%async_computation.3 | async-start | bytes 6291456 | tf_op jit(solution)/shard_map/all_to_all | solution.py:331
  213.5 2.8 %collective-permute-done.18.refs_3_ = bf16[200,512]{1,0:T(8,128)(2,1)S(1)} collective-permute-done((bf16[200,512]{1,0:T(8,128)(2,1)S(1)}, bf16[200,512]{1,0:T(8,128)(2,1)S(1)}, u32[]{:S(2)}, u32[]{:S(2)}) %collective-permute-start.18) | collective-permute-done | bytes 204832 | tf_op jit(solution)/shard_map/ppermute | solution.py:445
  216.3 2.6 %collective-permute-done.17.refs_2_ = bf16[200,512]{1,0:T(8,128)(2,1)S(1)} collective-permute-done((bf16[200,512]{1,0:T(8,128)(2,1)S(1)}, bf16[200,512]{1,0:T(8,128)(2,1)S(1)}, u32[]{:S(2)}, u32[]{:S(2)}) %collective-permute-start.17) | collective-permute-done | bytes 204832 | tf_op jit(solution)/shard_map/ppermute | solution.py:445
  223.4 3.4 %shard_map.180 = (f32[256,512]{1,0:T(8,128)}, f32[256,512]{1,0:T(8,128)}, f32[512,512]{1,0:T(8,128)}, f32[512,512]{1,0:T(8,128)}, f32[64,512]{1,0:T(8,128)}) custom-call(s32[1]{0:T(128)} %bitcast.11.me_ref, bf16[200,512]{1,0:T(8,128)(2,1)} %copy-done, bf16[200,512]{1,0:T(8,128)(2,1)} %copy-done.4, bf16[200,512]{1,0:T(8,128)(2,1)} %copy-done.3, ...), custom_call_target="tpu_custom_call" | custom-call | tf_op jit(solution)/shard_map/pallas_call | solution.py:490
  228.8 10.3 %shard_map.179 = (f32[2048,512]{1,0:T(8,128)}, f32[2048,512]{1,0:T(8,128)}) custom-call(s32[2,1,3072]{2,1,0:T(1,128)} %reshape.58.lane_ref, bf16[16,384,256]{2,1,0:T(8,128)(2,1)} %all-to-all-done.4.terms_ref), custom_call_target="tpu_custom_call" | custom-call | flops 100663296 | bytes 114688 | tf_op jit(solution)/shard_map/pallas_call | solution.py:433
  239.1 8.5 %all-to-all-done.3.terms_ref = bf16[16,384,256]{2,1,0:T(8,128)(2,1)} async-done(((bf16[16,384,256]{2,1,0:T(8,128)(2,1)}), bf16[16,384,256]{2,1,0:T(8,128)(2,1)}, u32[]{:S(2)}, u32[]{:S(2)}) %all-to-all-start.3) | async-done | bytes 3145760 | tf_op jit(solution)/shard_map/all_to_all | solution.py:331
  247.6 10.3 %shard_map.181 = (f32[2048,512]{1,0:T(8,128)}, f32[2048,512]{1,0:T(8,128)}) custom-call(s32[2,1,3072]{2,1,0:T(1,128)} %reshape.58.lane_ref, bf16[16,384,256]{2,1,0:T(8,128)(2,1)} %all-to-all-done.3.terms_ref, f32[2048,512]{1,0:T(8,128)} %get-tuple-element.84.rest_0_, f32[2048,512]{1,0:T(8,128)} %get-tuple-element.85.rest_1_), custom_call_target="tpu_custom_call", output_to_operand_aliasing={{0}: (2, {}), {1}: (3, {})} | custom-call | flops 100663296 | bytes 114688 | tf_op jit(solution)/shard_map/pallas_call | solution.py:433
  (83 shorter events, 42.8 us)
Async XLA Ops:
  30.2 46.0 %all-to-all-start.2 = ((bf16[16,384,256]{2,1,0:T(8,128)(2,1)}), bf16[16,384,256]{2,1,0:T(8,128)(2,1)}, u32[]{:S(2)}, u32[]{:S(2)}) async-start(bf16[16,384,256]{2,1,0:T(8,128)(2,1)} %shard_map.173), calls=%async_computation.2 | async-start | bytes 6291456 | tf_op jit(solution)/shard_map/all_to_all | solution.py:331
  76.2 41.8 %all-to-all-start.1 = ((bf16[16,384,256]{2,1,0:T(8,128)(2,1)}), bf16[16,384,256]{2,1,0:T(8,128)(2,1)}, u32[]{:S(2)}, u32[]{:S(2)}) async-start(bf16[16,384,256]{2,1,0:T(8,128)(2,1)} %shard_map.172), calls=%async_computation.1 | async-start | bytes 6291456 | tf_op jit(solution)/shard_map/all_to_all | solution.py:331
  136.2 69.7 %all-to-all-start.4 = ((bf16[16,384,256]{2,1,0:T(8,128)(2,1)}), bf16[16,384,256]{2,1,0:T(8,128)(2,1)}, u32[]{:S(2)}, u32[]{:S(2)}) async-start(bf16[16,384,256]{2,1,0:T(8,128)(2,1)} %get-tuple-element.77), calls=%async_computation.4 | async-start | bytes 6291456 | tf_op jit(solution)/shard_map/all_to_all | solution.py:331
  162.6 16.3 %collective-permute-start.1 = (bf16[200,512]{1,0:T(8,128)(2,1)}, bf16[200,512]{1,0:T(8,128)(2,1)}, u32[]{:S(2)}, u32[]{:S(2)}) collective-permute-start(bf16[200,512]{1,0:T(8,128)(2,1)} %get-tuple-element.93), channel_id=1, source_target_pairs={{0,2},{1,3},{2,4},{3,5},{4,6},{5,7},{6,0},{7,1},{8,10},{9,11},{10,... | collective-permute-start | bytes 614408 | tf_op jit(solution)/shard_map/ppermute | solution.py:445
  164.1 14.7 %collective-permute-start.3 = (bf16[200,512]{1,0:T(8,128)(2,1)}, bf16[200,512]{1,0:T(8,128)(2,1)}, u32[]{:S(2)}, u32[]{:S(2)}) collective-permute-start(bf16[200,512]{1,0:T(8,128)(2,1)} %get-tuple-element.94), channel_id=1, source_target_pairs={{0,6},{1,7},{2,0},{3,1},{4,2},{5,3},{6,4},{7,5},{8,14},{9,15},{10,... | collective-permute-start | bytes 614408 | tf_op jit(solution)/shard_map/ppermute | solution.py:445
  165.8 13.1 %collective-permute-start.2 = (bf16[200,512]{1,0:T(8,128)(2,1)}, bf16[200,512]{1,0:T(8,128)(2,1)}, u32[]{:S(2)}, u32[]{:S(2)}) collective-permute-start(bf16[200,512]{1,0:T(8,128)(2,1)} %get-tuple-element.95), channel_id=1, source_target_pairs={{0,4},{1,5},{2,6},{3,7},{4,0},{5,1},{6,2},{7,3},{8,12},{9,13},{10,... | collective-permute-start | bytes 614408 | tf_op jit(solution)/shard_map/ppermute | solution.py:445
  180.3 8.2 %collective-permute-start.12 = (bf16[96,512]{1,0:T(8,128)(2,1)S(1)}, bf16[96,512]{1,0:T(8,128)(2,1)S(1)}, u32[]{:S(2)}, u32[]{:S(2)}) collective-permute-start(bf16[96,512]{1,0:T(8,128)(2,1)S(1)} %slice.80), channel_id=1, source_target_pairs={{0,24},{8,0},{16,8},{24,16},{32,56},{40,32},{48,40},{56,48},{64,88... | collective-permute-start | bytes 294920 | tf_op jit(solution)/shard_map/ppermute | solution.py:449
  183.4 7.4 %collective-permute-start.11 = (bf16[96,512]{1,0:T(8,128)(2,1)S(1)}, bf16[96,512]{1,0:T(8,128)(2,1)S(1)}, u32[]{:S(2)}, u32[]{:S(2)}) collective-permute-start(bf16[96,512]{1,0:T(8,128)(2,1)S(1)} %slice.80), channel_id=1, source_target_pairs={{0,8},{8,16},{16,24},{24,0},{32,40},{40,48},{48,56},{56,32},{64,72... | collective-permute-start | bytes 294920 | tf_op jit(solution)/shard_map/ppermute | solution.py:449
  183.4 7.4 %collective-permute-start.10 = (bf16[96,512]{1,0:T(8,128)(2,1)S(1)}, bf16[96,512]{1,0:T(8,128)(2,1)S(1)}, u32[]{:S(2)}, u32[]{:S(2)}) collective-permute-start(bf16[96,512]{1,0:T(8,128)(2,1)S(1)} %slice.80), channel_id=1, source_target_pairs={{0,16},{8,24},{16,0},{24,8},{32,48},{40,56},{48,32},{56,40},{64,80... | collective-permute-start | bytes 294920 | tf_op jit(solution)/shard_map/ppermute | solution.py:449
  185.7 7.5 %collective-permute-start.6 = (bf16[104,512]{1,0:T(8,128)(2,1)S(1)}, bf16[104,512]{1,0:T(8,128)(2,1)S(1)}, u32[]{:S(2)}, u32[]{:S(2)}) collective-permute-start(bf16[104,512]{1,0:T(8,128)(2,1)S(1)} %slice.79), channel_id=1, source_target_pairs={{0,96},{8,104},{16,112},{24,120},{32,0},{40,8},{48,16},{56,24},{64... | collective-permute-start | bytes 319496 | tf_op jit(solution)/shard_map/ppermute | solution.py:449
  188.5 8.4 %collective-permute-start.5 = (bf16[104,512]{1,0:T(8,128)(2,1)S(1)}, bf16[104,512]{1,0:T(8,128)(2,1)S(1)}, u32[]{:S(2)}, u32[]{:S(2)}) collective-permute-start(bf16[104,512]{1,0:T(8,128)(2,1)S(1)} %slice.79), channel_id=1, source_target_pairs={{0,32},{8,40},{16,48},{24,56},{32,64},{40,72},{48,80},{56,88},{64,... | collective-permute-start | bytes 319496 | tf_op jit(solution)/shard_map/ppermute | solution.py:449
  188.5 8.4 %collective-permute-start.4 = (bf16[104,512]{1,0:T(8,128)(2,1)S(1)}, bf16[104,512]{1,0:T(8,128)(2,1)S(1)}, u32[]{:S(2)}, u32[]{:S(2)}) collective-permute-start(bf16[104,512]{1,0:T(8,128)(2,1)S(1)} %slice.79), channel_id=1, source_target_pairs={{0,64},{8,72},{16,80},{24,88},{32,96},{40,104},{48,112},{56,120},{... | collective-permute-start | bytes 319496 | tf_op jit(solution)/shard_map/ppermute | solution.py:449
  190.9 8.8 %collective-permute-start.15 = (bf16[96,512]{1,0:T(8,128)(2,1)S(1)}, bf16[96,512]{1,0:T(8,128)(2,1)S(1)}, u32[]{:S(2)}, u32[]{:S(2)}) collective-permute-start(bf16[96,512]{1,0:T(8,128)(2,1)S(1)} %add_convert_fusion.4), channel_id=1, source_target_pairs={{0,96},{8,104},{16,112},{24,120},{32,0},{40,8},{48,16},{56,24},{64... | collective-permute-start | bytes 294920 | tf_op jit(solution)/shard_map/ppermute | solution.py:449
  193.2 8.4 %collective-permute-start.14 = (bf16[96,512]{1,0:T(8,128)(2,1)S(1)}, bf16[96,512]{1,0:T(8,128)(2,1)S(1)}, u32[]{:S(2)}, u32[]{:S(2)}) collective-permute-start(bf16[96,512]{1,0:T(8,128)(2,1)S(1)} %add_convert_fusion.4), channel_id=1, source_target_pairs={{0,32},{8,40},{16,48},{24,56},{32,64},{40,72},{48,80},{56,88},{64,... | collective-permute-start | bytes 294920 | tf_op jit(solution)/shard_map/ppermute | solution.py:449
  193.2 8.4 %collective-permute-start.13 = (bf16[96,512]{1,0:T(8,128)(2,1)S(1)}, bf16[96,512]{1,0:T(8,128)(2,1)S(1)}, u32[]{:S(2)}, u32[]{:S(2)}) collective-permute-start(bf16[96,512]{1,0:T(8,128)(2,1)S(1)} %add_convert_fusion.4), channel_id=1, source_target_pairs={{0,64},{8,72},{16,80},{24,88},{32,96},{40,104},{48,112},{56,120},{... | collective-permute-start | bytes 294920 | tf_op jit(solution)/shard_map/ppermute | solution.py:449
  196.9 5.3 %collective-permute-start.9 = (bf16[104,512]{1,0:T(8,128)(2,1)S(1)}, bf16[104,512]{1,0:T(8,128)(2,1)S(1)}, u32[]{:S(2)}, u32[]{:S(2)}) collective-permute-start(bf16[104,512]{1,0:T(8,128)(2,1)S(1)} %add_convert_fusion.3), channel_id=1, source_target_pairs={{0,24},{8,0},{16,8},{24,16},{32,56},{40,32},{48,40},{56,48},{64,88... | collective-permute-start | bytes 319496 | tf_op jit(solution)/shard_map/ppermute | solution.py:449
  198.0 5.9 %collective-permute-start.8 = (bf16[104,512]{1,0:T(8,128)(2,1)S(1)}, bf16[104,512]{1,0:T(8,128)(2,1)S(1)}, u32[]{:S(2)}, u32[]{:S(2)}) collective-permute-start(bf16[104,512]{1,0:T(8,128)(2,1)S(1)} %add_convert_fusion.3), channel_id=1, source_target_pairs={{0,8},{8,16},{16,24},{24,0},{32,40},{40,48},{48,56},{56,32},{64,72... | collective-permute-start | bytes 319496 | tf_op jit(solution)/shard_map/ppermute | solution.py:449
  199.6 6.2 %collective-permute-start.7 = (bf16[104,512]{1,0:T(8,128)(2,1)S(1)}, bf16[104,512]{1,0:T(8,128)(2,1)S(1)}, u32[]{:S(2)}, u32[]{:S(2)}) collective-permute-start(bf16[104,512]{1,0:T(8,128)(2,1)S(1)} %add_convert_fusion.3), channel_id=1, source_target_pairs={{0,16},{8,24},{16,0},{24,8},{32,48},{40,56},{48,32},{56,40},{64,80... | collective-permute-start | bytes 319496 | tf_op jit(solution)/shard_map/ppermute | solution.py:449
  205.9 41.7 %all-to-all-start.3 = ((bf16[16,384,256]{2,1,0:T(8,128)(2,1)}), bf16[16,384,256]{2,1,0:T(8,128)(2,1)}, u32[]{:S(2)}, u32[]{:S(2)}) async-start(bf16[16,384,256]{2,1,0:T(8,128)(2,1)} %shard_map.178), calls=%async_computation.3 | async-start | bytes 6291456 | tf_op jit(solution)/shard_map/all_to_all | solution.py:331
  210.5 5.8 %collective-permute-start.18 = (bf16[200,512]{1,0:T(8,128)(2,1)S(1)}, bf16[200,512]{1,0:T(8,128)(2,1)S(1)}, u32[]{:S(2)}, u32[]{:S(2)}) collective-permute-start(bf16[200,512]{1,0:T(8,128)(2,1)S(1)} %pad_maximum_fusion.refs_0_), channel_id=1, source_target_pairs={{0,6},{1,7},{2,0},{3,1},{4,2},{5,3},{6,4},{7,5},{8,14},{9,15},{10,... | collective-permute-start | bytes 614408 | tf_op jit(solution)/shard_map/ppermute | solution.py:445
  211.6 7.3 %collective-permute-start.17 = (bf16[200,512]{1,0:T(8,128)(2,1)S(1)}, bf16[200,512]{1,0:T(8,128)(2,1)S(1)}, u32[]{:S(2)}, u32[]{:S(2)}) collective-permute-start(bf16[200,512]{1,0:T(8,128)(2,1)S(1)} %pad_maximum_fusion.refs_0_), channel_id=1, source_target_pairs={{0,4},{1,5},{2,6},{3,7},{4,0},{5,1},{6,2},{7,3},{8,12},{9,13},{10,... | collective-permute-start | bytes 614408 | tf_op jit(solution)/shard_map/ppermute | solution.py:445
  213.3 7.8 %collective-permute-start.16 = (bf16[200,512]{1,0:T(8,128)(2,1)S(1)}, bf16[200,512]{1,0:T(8,128)(2,1)S(1)}, u32[]{:S(2)}, u32[]{:S(2)}) collective-permute-start(bf16[200,512]{1,0:T(8,128)(2,1)S(1)} %pad_maximum_fusion.refs_0_), channel_id=1, source_target_pairs={{0,2},{1,3},{2,4},{3,5},{4,6},{5,7},{6,0},{7,1},{8,10},{9,11},{10,... | collective-permute-start | bytes 614408 | tf_op jit(solution)/shard_map/ppermute | solution.py:445
  213.5 8.4 %collective-permute-start.19 = (bf16[200,512]{1,0:T(8,128)(2,1)S(1)}, bf16[200,512]{1,0:T(8,128)(2,1)S(1)}, u32[]{:S(2)}, u32[]{:S(2)}) collective-permute-start(bf16[200,512]{1,0:T(8,128)(2,1)S(1)} %pad_maximum_fusion.refs_0_), channel_id=1, source_target_pairs={{0,1},{1,0},{2,3},{3,2},{4,5},{5,4},{6,7},{7,6},{8,9},{9,8},{10,11... | collective-permute-start | bytes 614408 | tf_op jit(solution)/shard_map/ppermute | solution.py:463
  216.3 5.6 %collective-permute-start.22 = (bf16[200,512]{1,0:T(8,128)(2,1)S(1)}, bf16[200,512]{1,0:T(8,128)(2,1)S(1)}, u32[]{:S(2)}, u32[]{:S(2)}) collective-permute-start(bf16[200,512]{1,0:T(8,128)(2,1)S(1)} %collective-permute-done.18.refs_3_), channel_id=1, source_target_pairs={{0,1},{1,0},{2,3},{3,2},{4,5},{5,4},{6,7},{7,6},{8,9},{9,8},{10,11... | collective-permute-start | bytes 614408 | tf_op jit(solution)/shard_map/ppermute | solution.py:463
  (12 other events, 79.3 us)
